TPU v7x, 512 devices: a whole 4x8x8 slice. The times are simulated.
512 devices in a mesh: region: 64 (over z, x, core), slab: 8 (over y).
Axes of the slice: x: 4, y: 8, z: 8, core: 2. Of those that a mesh axis runs over, the one named last changes fastest.
Arguments:
- features: bfloat16 [131072, 96], P(('region', 'slab')), may hold values from -6 to 6
- neighbours: int32 [131072, 27], P(('region', 'slab')), may hold values from 0 to 2304, as said below
- down_map: int32 [32768, 8], P(('region', 'slab')), may hold values from 0 to 256, as said below
- w_conv: bfloat16 [2592, 96], replicated, may hold values from -0.125 to 0.125
- w_down: bfloat16 [768, 128], replicated, may hold values from -0.21875 to 0.21875
- coarse_grad: bfloat16 [32768, 128], P(('region', 'slab')), may hold values from -6 to 6
Outputs:
- coarse: bfloat16 [32768, 128], P(('region', 'slab'))
- grad_input: float32 [131072, 96], P(('region', 'slab'))
- conv_weight_grad: float32 [2592, 96], replicated
- down_weight_grad: float32 [768, 128], replicated
Inputs may be any that keep to these rules, and one draw needn't show every extreme that they name: `neighbours`: device d is the device at region index d // (slab axis size) and slab index d mod (slab axis size). Each device's live voxels are its first slots; dead slots list 9 * 256 everywhere and are named by no one. An entry k * 256 + j names slot j of the device whose region index differs by k // 3 - 1 and slab index by k mod 3 - 1; that device exists. A live voxel names itself at offset 13 (k = 4), and otherwise a live voxel or 2304. When k is not 4, j is below 64, the naming voxel lies in its device's first 64 slots, and some voxel names slot 63 of another device in every draw. 9 * 256 means no source. `down_map`: every live voxel of a device is named exactly once, by a coarse voxel slot of that device, by its slot on the device; all other entries are 256.
All inputs are finite; a program needn't handle non-finite values.
Results may differ from a plain program's by a relative error of at most 0.005.
Values may be sent and summed in bfloat16 or wider, within the bound.
A program may use at most 64 MiB of HBM per device.

v0:
```python
import jax
import jax.numpy as jnp
from jax import lax
from jax.sharding import PartitionSpec as P


def extended_2(block, sides, width):
    for axis, dim in sides:
        count = lax.axis_size(axis)
        forward = [(i, i + 1) for i in range(count - 1)]
        backward = [(target, source) for source, target in forward]
        low = lax.ppermute(
            lax.slice_in_dim(block, block.shape[dim] - width, None, axis=dim), axis, forward
        )
        high = lax.ppermute(lax.slice_in_dim(block, 0, width, axis=dim), axis, backward)
        block = jnp.concatenate([low, block, high], axis=dim)
    return block


def on_device(features, neighbours, down_map, w_conv, w_down, coarse_grad):
    voxels, channels = features.shape
    offsets = neighbours.shape[1]
    absent = neighbours >= 9 * voxels
    slot_idx = neighbours // voxels
    local_idx = neighbours - slot_idx * voxels
    zero_row = jnp.zeros((1, channels), features.dtype)
    sendable = features.reshape(1, 1, voxels * channels // 128, 128)
    extended = extended_2(sendable, (("region", 0), ("slab", 1)), 1)
    table = jnp.concatenate([extended.reshape(9 * voxels, channels), zero_row], axis=0)
    positions = jnp.where(absent, 9 * voxels, slot_idx * voxels + local_idx)
    row_block = min(voxels, 512)
    block_count = voxels // row_block
    pos_blocks = positions.reshape(block_count, row_block, offsets)

    def conv_block(block_pos):
        rows = table[block_pos].reshape(row_block, offsets * channels)
        return jnp.dot(rows, w_conv, preferred_element_type=jnp.float32)

    conv_out = lax.map(conv_block, pos_blocks).reshape(voxels, channels)
    hidden = (features.astype(jnp.float32) + jax.nn.silu(conv_out)).astype(jnp.bfloat16)
    coarse_count, taps = down_map.shape
    down_local = jnp.minimum(down_map, voxels)
    hidden_pad = jnp.concatenate([hidden, zero_row], axis=0)
    coarse_rows = hidden_pad[down_local].reshape(coarse_count, taps * channels)
    coarse = jnp.dot(coarse_rows, w_down, preferred_element_type=jnp.float32).astype(jnp.bfloat16)
    coarse_back = jnp.dot(coarse_grad, w_down.T, preferred_element_type=jnp.float32)
    hidden_grad = jnp.zeros((voxels + 1, channels), jnp.float32)
    hidden_grad = hidden_grad.at[down_local.reshape(-1)].add(coarse_back.reshape(-1, channels))[
        :voxels
    ]
    down_wgrad = lax.dot_general(
        coarse_rows, coarse_grad, (((0,), (0,)), ((), ())), preferred_element_type=jnp.float32
    )
    sigmoid_y = jax.nn.sigmoid(conv_out)
    conv_grad = (hidden_grad * sigmoid_y * (1.0 + conv_out * (1.0 - sigmoid_y))).astype(
        jnp.bfloat16
    )
    grad_blocks = conv_grad.reshape(block_count, row_block, channels)

    def back_block(carry, inputs):
        table_grad, weight_grad = carry
        block_pos, block_grad = inputs
        rows = table[block_pos].reshape(row_block, offsets * channels)
        weight_grad = weight_grad + lax.dot_general(
            rows, block_grad, (((0,), (0,)), ((), ())), preferred_element_type=jnp.float32
        )
        spread = jnp.dot(block_grad, w_conv.T, preferred_element_type=jnp.float32).reshape(
            -1, channels
        )
        table_grad = table_grad.at[block_pos.reshape(-1)].add(spread)
        return ((table_grad, weight_grad), None)

    start = (
        jnp.zeros((table.shape[0], channels), jnp.float32),
        jnp.zeros(w_conv.shape, jnp.float32),
    )
    (table_grad, conv_wgrad), unused = lax.scan(back_block, start, (pos_blocks, grad_blocks))
    conv_wgrad, down_wgrad = lax.psum((conv_wgrad, down_wgrad), ("region", "slab"))
    sections = table_grad[: 9 * voxels].reshape(3, 3, voxels, channels)
    own_part = sections[1, 1]
    outgoing = sections.at[1, 1].set(0.0).reshape(3, 3, voxels * channels // 128, 128)
    returned = extended_2(outgoing.astype(jnp.bfloat16), (("region", 0), ("slab", 1)), 1).astype(
        outgoing.dtype
    )
    returned = returned.reshape(5, 5, voxels, channels)
    incoming = jnp.sum(returned[0::2, 0::2], axis=(0, 1))
    grad_input = hidden_grad + own_part + incoming
    return (coarse, grad_input, conv_wgrad, down_wgrad)


def solution(mesh):
    in_specs = (
        P(("region", "slab"), None),
        P(("region", "slab"), None),
        P(("region", "slab"), None),
        P(),
        P(),
        P(("region", "slab"), None),
    )
    out_specs = (P(("region", "slab"), None), P(("region", "slab"), None), P(), P())
    return jax.shard_map(
        on_device, mesh=mesh, in_specs=in_specs, out_specs=out_specs, check_vma=False
    )
```

profile of v0, /device:TPU:1, one launch (start us, length us, event | category | flops | bytes accessed | tf_op | source)
XLA Modules:
  0.0 423.2 jit_solution(2961291640039998738)
XLA Ops:
  7.2 1.0 copy.42
  8.3 4.5 %collective-permute-start = (bf16[1,1,192,128]{3,2,1,0:T(8,128)(2,1)S(1)}, bf16[1,1,192,128]{3,2,1,0:T(8,128)(2,1)S(1)}, u32[]{:S(2)}, u32[]{:S(2)}) collective-permute-start(bf16[1,1,192,128]{3,2,1,0:T(8,128)(2,1)S(1)} %reshape.147), channel_id=1, source_target_pairs={{0,8},{8,16},{16,24},{24,32},{32,40},{40,48},{48,56},{56,64},{64,7... | collective-permute-start | bytes 147464 | tf_op jit(solution)/shard_map/ppermute | solution.py:12
  12.9 5.6 %collective-permute-start.1 = (bf16[1,1,192,128]{3,2,1,0:T(8,128)(2,1)S(1)}, bf16[1,1,192,128]{3,2,1,0:T(8,128)(2,1)S(1)}, u32[]{:S(2)}, u32[]{:S(2)}) collective-permute-start(bf16[1,1,192,128]{3,2,1,0:T(8,128)(2,1)S(1)} %reshape.147), channel_id=1, source_target_pairs={{8,0},{16,8},{24,16},{32,24},{40,32},{48,40},{56,48},{64,56},{72,6... | collective-permute-start | bytes 147464 | tf_op jit(solution)/shard_map/ppermute | solution.py:15
  20.4 1.1 fusion.8
  21.8 1.3 collective-permute-start.2
  23.1 1.3 collective-permute-start.3
  24.6 3.3 scatter_custom_fusion
  28.4 2.1 collective-permute-done.3
  31.2 13.0 %gather_fusion = bf16[6912,96]{1,0:T(8,128)(2,1)S(1)} fusion(bf16[2305,96]{1,0:T(8,128)(2,1)S(1)} %concatenate.29, s32[7168]{0:T(1024)S(1)} %pad_clamp_fusion), kind=kCustom, calls=%fused_computation | custom fusion | bytes 2681856 | tf_op jit(solution)/shard_map/while/body/eval_jaxpr/gather | solution.py:36
  44.2 2.1 reshape.149
  46.3 1.9 multiply_convert_fusion
  48.9 3.3 reshape.184
  52.2 45.0 %scatter_custom_fusion.1 = f32[2305,96]{1,0:T(8,128)S(1)} fusion(s32[6912]{0:T(1024)S(1)} %fusion.5, f32[6912,96]{1,0:T(8,128)} %reshape.184, f32[]{:T(128)} %constant.87.clone.1), kind=kCustom, calls=%fused_computation.7 | custom fusion | flops 663552 | bytes 885632 | tf_op jit(solution)/shard_map/while/body/eval_jaxpr/scatter-add | solution.py:70
  98.2 1.3 scatter.4
  99.7 1.3 copy.53
  101.2 1.0 slice.64
  102.2 2.2 collective-permute-start.4
  104.4 2.6 convert_element_type.25
  107.2 1.0 slice.66
  108.2 2.9 collective-permute-start.5
  111.2 1.9 gather_fusion.1
  113.1 1.8 reshape.150
  114.9 2.1 fusion.11
  117.0 1.0 constant_dynamic-update-slice_fusion.5
  118.1 0.9 constant_dynamic-update-slice_fusion.3
  119.8 4.9 %collective-permute-start.6 = (bf16[5,1,192,128]{3,2,1,0:T(8,128)(2,1)}, bf16[5,1,192,128]{3,2,1,0:T(8,128)(2,1)S(1)}, u32[]{:S(2)}, u32[]{:S(2)}) collective-permute-start(bf16[5,1,192,128]{3,2,1,0:T(8,128)(2,1)} %get-tuple-element.54), channel_id=1, source_target_pairs={{0,1},{1,2},{2,3},{3,4},{4,5},{5,6},{6,7},{8,9},{9,10},{10,11},{11... | collective-permute-start | bytes 737288 | tf_op jit(solution)/shard_map/ppermute | solution.py:12
  124.7 1.3 collective-permute-start.7
  126.0 1.0 fusion.10
  128.6 1.9 collective-permute-done.6
  130.7 3.8 collective-permute-done.7
  136.3 277.0 %all-reduce.5.cloned.1.call-done = (f32[2592,96]{0,1:T(8,128)}, f32[768,128]{1,0:T(8,128)}) async-done(((f32[2592,96]{0,1:T(8,128)}, f32[768,128]{1,0:T(8,128)}), (f32[2592,96]{0,1:T(8,128)}, f32[768,128]{1,0:T(8,128)})) %all-reduce.5.cloned.1.call-update) | async-done | bytes 1388560 | tf_op jit(solution)/shard_map/psum | solution.py:78
  413.3 2.3 copy.71
  (75 shorter events, 11.1 us)
Async XLA Ops:
  7.2 39.1 %copy-start = (bf16[2592,96]{0,1:T(8,128)(2,1)S(1)}, bf16[2592,96]{0,1:T(8,128)(2,1)}, u32[]{:S(2)}) copy-start(bf16[2592,96]{0,1:T(8,128)(2,1)} %param.11) | copy-start | bytes 1492996
  7.2 406.1 %all-reduce.5.cloned.1.call-start = ((), (), s32[]{:S(2)}) async-start(), calls=%async_computation | async-start | bytes 2850816 | tf_op jit(solution)/shard_map/psum | solution.py:78
  8.3 13.4 %collective-permute-start = (bf16[1,1,192,128]{3,2,1,0:T(8,128)(2,1)S(1)}, bf16[1,1,192,128]{3,2,1,0:T(8,128)(2,1)S(1)}, u32[]{:S(2)}, u32[]{:S(2)}) collective-permute-start(bf16[1,1,192,128]{3,2,1,0:T(8,128)(2,1)S(1)} %reshape.147), channel_id=1, source_target_pairs={{0,8},{8,16},{16,24},{24,32},{32,40},{40,48},{48,56},{56,64},{64,7... | collective-permute-start | bytes 147464 | tf_op jit(solution)/shard_map/ppermute | solution.py:12
  12.9 8.9 %collective-permute-start.1 = (bf16[1,1,192,128]{3,2,1,0:T(8,128)(2,1)S(1)}, bf16[1,1,192,128]{3,2,1,0:T(8,128)(2,1)S(1)}, u32[]{:S(2)}, u32[]{:S(2)}) collective-permute-start(bf16[1,1,192,128]{3,2,1,0:T(8,128)(2,1)S(1)} %reshape.147), channel_id=1, source_target_pairs={{8,0},{16,8},{24,16},{32,24},{40,32},{48,40},{56,48},{64,56},{72,6... | collective-permute-start | bytes 147464 | tf_op jit(solution)/shard_map/ppermute | solution.py:15
  21.8 6.6 %collective-permute-start.2 = (bf16[3,1,192,128]{3,2,1,0:T(8,128)(2,1)S(1)}, bf16[3,1,192,128]{3,2,1,0:T(8,128)(2,1)S(1)}, u32[]{:S(2)}, u32[]{:S(2)}) collective-permute-start(bf16[3,1,192,128]{3,2,1,0:T(8,128)(2,1)S(1)} %constant_dynamic-update-slice_fusion), channel_id=1, source_target_pairs={{0,1},{1,2},{2,3},{3,4},{4,5},{5,6},{6,7},{8,9},{9,10},{10,11},{11... | collective-permute-start | bytes 442376 | tf_op jit(solution)/shard_map/ppermute | solution.py:12
  23.1 7.4 %collective-permute-start.3 = (bf16[3,1,192,128]{3,2,1,0:T(8,128)(2,1)S(1)}, bf16[3,1,192,128]{3,2,1,0:T(8,128)(2,1)S(1)}, u32[]{:S(2)}, u32[]{:S(2)}) collective-permute-start(bf16[3,1,192,128]{3,2,1,0:T(8,128)(2,1)S(1)} %constant_dynamic-update-slice_fusion), channel_id=1, source_target_pairs={{1,0},{2,1},{3,2},{4,3},{5,4},{6,5},{7,6},{9,8},{10,9},{11,10},{12... | collective-permute-start | bytes 442376 | tf_op jit(solution)/shard_map/ppermute | solution.py:15
  28.0 18.3 %copy-start.6 = (f32[256,96]{0,1:T(8,128)}, f32[256,96]{0,1:T(8,128)S(1)}, u32[]{:S(2)}) copy-start(f32[256,96]{0,1:T(8,128)S(1)} %copy.61) | copy-start | bytes 294916
  44.2 2.1 copy-start.10
  48.3 0.6 copy-start.8
  102.2 12.7 %copy-start.1 = (bf16[256,2592]{1,0:T(8,128)(2,1)S(1)}, bf16[256,2592]{1,0:T(8,128)(2,1)}, u32[]{:S(2)}) copy-start(bf16[256,2592]{1,0:T(8,128)(2,1)} %reshape.149) | copy-start | bytes 3981316
  102.2 14.8 %collective-permute-start.4 = (bf16[1,3,192,128]{3,2,1,0:T(8,128)(2,1)}, bf16[1,3,192,128]{3,2,1,0:T(8,128)(2,1)}, u32[]{:S(2)}, u32[]{:S(2)}) collective-permute-start(bf16[1,3,192,128]{3,2,1,0:T(8,128)(2,1)} %slice.64), channel_id=1, source_target_pairs={{0,8},{8,16},{16,24},{24,32},{32,40},{40,48},{48,56},{56,64},{64,7... | collective-permute-start | bytes 442376 | tf_op jit(solution)/shard_map/ppermute | solution.py:12
  108.2 9.9 %collective-permute-start.5 = (bf16[1,3,192,128]{3,2,1,0:T(8,128)(2,1)}, bf16[1,3,192,128]{3,2,1,0:T(8,128)(2,1)}, u32[]{:S(2)}, u32[]{:S(2)}) collective-permute-start(bf16[1,3,192,128]{3,2,1,0:T(8,128)(2,1)} %slice.66), channel_id=1, source_target_pairs={{8,0},{16,8},{24,16},{32,24},{40,32},{48,40},{56,48},{64,56},{72,6... | collective-permute-start | bytes 442376 | tf_op jit(solution)/shard_map/ppermute | solution.py:15
  113.1 4.9 %copy-start.2 = (bf16[3,3,192,128]{3,2,1,0:T(8,128)(2,1)S(1)}, bf16[3,3,192,128]{3,2,1,0:T(8,128)(2,1)}, u32[]{:S(2)}) copy-start(bf16[3,3,192,128]{3,2,1,0:T(8,128)(2,1)} %convert_element_type.25) | copy-start | bytes 1327108
  117.0 9.0 %copy-start.3 = (bf16[64,768]{1,0:T(8,128)(2,1)S(1)}, bf16[64,768]{1,0:T(8,128)(2,1)}, u32[]{:S(2)}) copy-start(bf16[64,768]{1,0:T(8,128)(2,1)} %reshape.150) | copy-start | bytes 294916
  117.0 9.0 %copy-start.9 = (bf16[64,128]{1,0:T(8,128)(2,1)S(1)}, bf16[64,128]{1,0:T(8,128)(2,1)}, u32[]{:S(2)}) copy-start(bf16[64,128]{1,0:T(8,128)(2,1)} %param.13) | copy-start | bytes 49156
  119.0 8.1 %copy-start.4 = (bf16[768,128]{1,0:T(8,128)(2,1)S(1)}, bf16[768,128]{1,0:T(8,128)(2,1)}, u32[]{:S(2)}) copy-start(bf16[768,128]{1,0:T(8,128)(2,1)} %param.12) | copy-start | bytes 589828
  119.8 10.6 %collective-permute-start.6 = (bf16[5,1,192,128]{3,2,1,0:T(8,128)(2,1)}, bf16[5,1,192,128]{3,2,1,0:T(8,128)(2,1)S(1)}, u32[]{:S(2)}, u32[]{:S(2)}) collective-permute-start(bf16[5,1,192,128]{3,2,1,0:T(8,128)(2,1)} %get-tuple-element.54), channel_id=1, source_target_pairs={{0,1},{1,2},{2,3},{3,4},{4,5},{5,6},{6,7},{8,9},{9,10},{10,11},{11... | collective-permute-start | bytes 737288 | tf_op jit(solution)/shard_map/ppermute | solution.py:12
  124.7 9.8 %collective-permute-start.7 = (bf16[5,1,192,128]{3,2,1,0:T(8,128)(2,1)}, bf16[5,1,192,128]{3,2,1,0:T(8,128)(2,1)S(1)}, u32[]{:S(2)}, u32[]{:S(2)}) collective-permute-start(bf16[5,1,192,128]{3,2,1,0:T(8,128)(2,1)} %get-tuple-element.55), channel_id=1, source_target_pairs={{1,0},{2,1},{3,2},{4,3},{5,4},{6,5},{7,6},{9,8},{10,9},{11,10},{12... | collective-permute-start | bytes 737288 | tf_op jit(solution)/shard_map/ppermute | solution.py:15
  134.7 0.9 copy-start.7
  413.3 2.3 copy-start.5
Sparse Core Ops, SparseCore 0:
  127.3 285.9 all-reduce.4
where the time goes:
time: 424 us; the launch traced here: 423 us
  waiting for transfers between devices  285 us (67%)
  other arithmetic  51 us (12%)
  local copies, waits for them, and re-layouts  41.4 us (10%)
  starting transfers between devices  24 us (6%)
  between operations  14.5 us (3%)
  matrix products  7.5 us (2%)
    psum x1, waiting for transfers between devices, on_device(): lax.psum((conv_wgrad, down_wgrad), ('region', 'slab'))  277 us
    scatter-add x1, other arithmetic, back_block(): table_grad = table_grad.at[block_pos.reshape(-1)].add(spread)  45 us
    gather x1, local copies, waits for them, and re-layouts, conv_block(): rows = table[block_pos].reshape(row_block, offsets * channels)  13 us
    ppermute x4, starting transfers between devices, extended_2(): lax.ppermute(lax.slice_in_dim(block, block.shape[dim] - width, None, axis...  12.9 us
    ppermute x4, starting transfers between devices, extended_2(): lax.ppermute(lax.slice_in_dim(block, 0, width, axis=dim), axis, backward)  11 us
  transfers between devices with their start and end apart: 9, of which 4 were waited for; matrix products, arithmetic and copies ran while one was open for 5% of the time, Pallas kernels for 0%

commit v1 on v0

--- a/solution.py
+++ b/solution.py
@@ -1,7 +1,121 @@
 import jax
 import jax.numpy as jnp
 from jax import lax
+from jax.experimental import pallas as pl
+from jax.experimental.pallas import tpu as pltpu
 from jax.sharding import PartitionSpec as P
+from jax.experimental import pallas as pl
+from jax.experimental.pallas import tpu as pltpu
+
+MESH = pl.DeviceIdType.MESH
+HALVINGS = 7
+ORDER_A = [0, 4, 7, 1, 5, 8]
+ORDER_B = [4, 7, 0, 5, 8, 1]
+FULL_A = [2, 6]
+FULL_B = [6, 2]
+
+
+def _bit_partner(region, slab, b):
+    if b < 3:
+        v = (slab // (1 << b)) % 2
+        return v, region, slab + (1 - 2 * v) * (1 << b)
+    j = b - 3
+    v = (region // (1 << j)) % 2
+    return v, region + (1 - 2 * v) * (1 << j), slab
+
+
+def _step(region, slab, core, ba, bb):
+    va, ra, sa = _bit_partner(region, slab, ba)
+    vb, rb, sb = _bit_partner(region, slab, bb)
+    return va + core * (vb - va), ra + core * (rb - ra), sa + core * (sb - sa)
+
+
+def allreduce_kernel(x_ref, o_ref, *scratch):
+    HALVES = [x_ref.shape[0] >> (k + 1) for k in range(HALVINGS)]
+    recvs = scratch[:9]
+    send_sem, recv_sem, free_sem = scratch[9], scratch[10], scratch[11]
+    region = lax.axis_index("region")
+    slab = lax.axis_index("slab")
+    core = region % 2
+    steps = [(core, region + 1 - 2 * core, slab)]
+    for ba, bb in zip(ORDER_A, ORDER_B):
+        steps.append(_step(region, slab, core, ba, bb))
+    fulls = [_step(region, slab, core, ba, bb) for ba, bb in zip(FULL_A, FULL_B)]
+
+    barrier = pltpu.get_barrier_semaphore()
+    for _, r, s in steps + fulls:
+        pl.semaphore_signal(barrier, inc=1, device_id=(r, s), device_id_type=MESH)
+    pl.semaphore_wait(barrier, len(steps) + len(fulls))
+
+    off = 0
+    offs = []
+    for k, (v, r, s) in enumerate(steps):
+        size = HALVES[k]
+        keep = pl.multiple_of(off + v * size, 8)
+        send = pl.multiple_of(off + (1 - v) * size, 8)
+        src = x_ref if k == 0 else o_ref
+        copy = pltpu.make_async_remote_copy(
+            src_ref=src.at[pl.ds(send, size)], dst_ref=recvs[k],
+            send_sem=send_sem.at[k], recv_sem=recv_sem.at[k],
+            device_id=(r, s), device_id_type=MESH)
+        copy.start()
+        copy.wait()
+        pl.semaphore_signal(free_sem.at[k], inc=1, device_id=(r, s), device_id_type=MESH)
+        o_ref[pl.ds(keep, size)] = src[pl.ds(keep, size)] + recvs[k][...]
+        off = keep
+        offs.append(keep)
+    last = HALVES[-1]
+    for i, (v, r, s) in enumerate(fulls):
+        k = len(steps) + i
+        copy = pltpu.make_async_remote_copy(
+            src_ref=o_ref.at[pl.ds(off, last)], dst_ref=recvs[k],
+            send_sem=send_sem.at[k], recv_sem=recv_sem.at[k],
+            device_id=(r, s), device_id_type=MESH)
+        copy.start()
+        copy.wait()
+        o_ref[pl.ds(off, last)] = o_ref[pl.ds(off, last)] + recvs[k][...]
+    base = len(steps) + len(fulls)
+    for k in reversed(range(len(steps))):
+        v, r, s = steps[k]
+        size = HALVES[k]
+        j = base + (len(steps) - 1 - k)
+        copy = pltpu.make_async_remote_copy(
+            src_ref=o_ref.at[pl.ds(offs[k], size)], dst_ref=o_ref.at[pl.ds(offs[k], size)],
+            send_sem=send_sem.at[j], recv_sem=recv_sem.at[j],
+            device_id=(r, s), device_id_type=MESH)
+        pl.semaphore_wait(free_sem.at[k], 1)
+        copy.start()
+        copy.wait()
+
+
+def allreduce(x):
+    rows = x.shape[0]
+    HALVES = [rows >> (k + 1) for k in range(HALVINGS)]
+    n_copies = 9 + 7
+    return pl.pallas_call(
+        allreduce_kernel,
+        out_shape=jax.ShapeDtypeStruct((rows, 128), jnp.float32),
+        in_specs=[pl.BlockSpec(memory_space=pltpu.VMEM)],
+        out_specs=pl.BlockSpec(memory_space=pltpu.VMEM),
+        scratch_shapes=[pltpu.VMEM((h, 128), jnp.float32) for h in HALVES]
+        + [pltpu.VMEM((HALVES[-1], 128), jnp.float32)] * 2
+        + [pltpu.SemaphoreType.DMA((n_copies,)), pltpu.SemaphoreType.DMA((n_copies,))]
+        + [pltpu.SemaphoreType.REGULAR((HALVINGS,))],
+        compiler_params=pltpu.CompilerParams(collective_id=0, has_side_effects=True),
+    )(x)
+
+
+def summed_everywhere(arrays):
+    flat = jnp.concatenate([a.reshape(-1) for a in arrays])
+    unit = 128 * 8 << HALVINGS
+    rows = -(-flat.size // unit) * unit // 128
+    padded = jnp.pad(flat, (0, rows * 128 - flat.size)).reshape(rows, 128)
+    total = allreduce(padded).reshape(-1)
+    out, at = [], 0
+    for a in arrays:
+        out.append(total[at:at + a.size].reshape(a.shape))
+        at += a.size
+    return out
 
 
 def extended_2(block, sides, width):
@@ -75,7 +189,7 @@
         jnp.zeros(w_conv.shape, jnp.float32),
     )
     (table_grad, conv_wgrad), unused = lax.scan(back_block, start, (pos_blocks, grad_blocks))
-    conv_wgrad, down_wgrad = lax.psum((conv_wgrad, down_wgrad), ("region", "slab"))
+    conv_wgrad, down_wgrad = summed_everywhere([conv_wgrad, down_wgrad])
     sections = table_grad[: 9 * voxels].reshape(3, 3, voxels, channels)
     own_part = sections[1, 1]
     outgoing = sections.at[1, 1].set(0.0).reshape(3, 3, voxels * channels // 128, 128)

time: 424 us -> 227 us (0.54)
  waiting for transfers between devices: 285 us -> 2.17 us
  Pallas kernels: 0 us -> 89.8 us
  between operations: 14.5 us -> 1.15 us
  local copies, waits for them, and re-layouts: 41.4 us -> 49.7 us
    psum x1 -> x0, waiting for transfers between devices: 277 us -> none  [on_device(): lax.psum((conv_wgrad, down_wgrad), ('region', 'slab'))]
    pallas_call x0 -> x1, Pallas kernels: none -> 89.8 us  [allreduce(): pl.pallas_call(allreduce_kernel, out_shape=jax.ShapeDtypeStruct((rows, 12...]
  transfers between devices with their start and end apart: 9 -> 8, of which waited for: 4 -> 1; matrix products, arithmetic and copies ran while one was open for 5% -> 11% of each run, Pallas kernels for 0% -> 40%
where the time goes in v1:
time: 227 us; the launch traced here: 226 us
  Pallas kernels  89.8 us (40%)
  other arithmetic  52.1 us (23%)
  local copies, waits for them, and re-layouts  49.7 us (22%)
  starting transfers between devices  24.5 us (11%)
  matrix products  6.59 us (3%)
    pallas_call x1, Pallas kernels, allreduce(): pl.pallas_call(allreduce_kernel, out_shape=jax.ShapeDtypeStruct((rows, 12...  89.8 us
    scatter-add x1, other arithmetic, back_block(): table_grad = table_grad.at[block_pos.reshape(-1)].add(spread)  44.8 us
    ppermute x4, starting transfers between devices, extended_2(): lax.ppermute(lax.slice_in_dim(block, block.shape[dim] - width, None, axis...  13.4 us
    gather x1, local copies, waits for them, and re-layouts, conv_block(): rows = table[block_pos].reshape(row_block, offsets * channels)  13.1 us
    ppermute x4, starting transfers between devices, extended_2(): lax.ppermute(lax.slice_in_dim(block, 0, width, axis=dim), axis, backward)  11.1 us
    unnamed x31, local copies, waits for them, and re-layouts  6.85 us
  transfers between devices with their start and end apart: 8, of which 1 were waited for; matrix products, arithmetic and copies ran while one was open for 11% of the time, Pallas kernels for 40%

profile of v1, /device:TPU:1, one launch (start us, length us, event | category | flops | bytes accessed | tf_op | source)
XLA Modules:
  0.0 226.1 jit_solution(1811847419656428357)
XLA Ops:
  0.6 1.0 copy.47
  1.8 4.5 %collective-permute-start = (bf16[1,1,192,128]{3,2,1,0:T(8,128)(2,1)S(1)}, bf16[1,1,192,128]{3,2,1,0:T(8,128)(2,1)S(1)}, u32[]{:S(2)}, u32[]{:S(2)}) collective-permute-start(bf16[1,1,192,128]{3,2,1,0:T(8,128)(2,1)S(1)} %reshape.165), channel_id=1, source_target_pairs={{0,8},{8,16},{16,24},{24,32},{32,40},{40,48},{48,56},{56,64},{64,7... | collective-permute-start | bytes 147464 | tf_op jit(solution)/shard_map/ppermute | solution.py:126
  6.3 5.6 %collective-permute-start.1 = (bf16[1,1,192,128]{3,2,1,0:T(8,128)(2,1)S(1)}, bf16[1,1,192,128]{3,2,1,0:T(8,128)(2,1)S(1)}, u32[]{:S(2)}, u32[]{:S(2)}) collective-permute-start(bf16[1,1,192,128]{3,2,1,0:T(8,128)(2,1)S(1)} %reshape.165), channel_id=1, source_target_pairs={{8,0},{16,8},{24,16},{32,24},{40,32},{48,40},{56,48},{64,56},{72,6... | collective-permute-start | bytes 147464 | tf_op jit(solution)/shard_map/ppermute | solution.py:129
  13.8 1.1 fusion.9
  15.2 1.3 collective-permute-start.2
  16.5 1.3 collective-permute-start.3
  18.0 3.3 %scatter_custom_fusion = f32[257,96]{1,0:T(8,128)S(1)} fusion(s32[512]{0:T(512)S(1)} %bitcast.42, f32[512,96]{1,0:T(8,128)S(1)} %reshape.198, f32[]{:T(128)} %constant.88.clone.1), kind=kCustom, calls=%fused_computation.22 | custom fusion | flops 49152 | bytes 98692 | tf_op jit(solution)/shard_map/scatter-add | solution.py:162
  21.8 2.2 collective-permute-done.3
  24.6 13.1 %gather_fusion = bf16[6912,96]{1,0:T(8,128)(2,1)S(1)} fusion(bf16[2305,96]{1,0:T(8,128)(2,1)S(1)} %concatenate.32, s32[7168]{0:T(1024)S(1)} %pad_clamp_fusion), kind=kCustom, calls=%fused_computation | custom fusion | bytes 2681856 | tf_op jit(solution)/shard_map/while/body/eval_jaxpr/gather | solution.py:150
  37.7 2.1 reshape.167
  39.8 2.6 %multiply_convert_fusion = (bf16[256,96]{0,1:T(8,128)(2,1)S(1)}, bf16[256,96]{0,1:T(8,128)(2,1)}) fusion(f32[256,96]{0,1:T(8,128)S(1)} %copy.69, bf16[256,96]{0,1:T(8,128)(2,1)S(1)} %copy-done.10, bf16[256,2592]{1,0:T(8,128)(2,1)} %reshape.167, bf16[2592,96]{0,1:T(8,128)(2,1)S(1)} %copy-done), kind=kOutput, calls=%fused_computation.17 | convolution fusion | flops 127721472 | bytes 2070528 | tf_op jit(solution)/shard_map/while/body/eval_jaxpr/dot_general | solution.py:151
  42.9 3.3 %reshape.206 = f32[6912,96]{1,0:T(8,128)} reshape(f32[256,2592]{1,0:T(8,128)S(1)} %fusion.10) | data formatting | bytes 5308416 | tf_op jit(solution)/shard_map/while/body/eval_jaxpr/reshape | solution.py:181
  46.3 44.8 %scatter_custom_fusion.1 = f32[2305,96]{1,0:T(8,128)S(1)} fusion(s32[6912]{0:T(1024)S(1)} %fusion.6, f32[6912,96]{1,0:T(8,128)} %reshape.206, f32[]{:T(128)} %constant.88.clone.1), kind=kCustom, calls=%fused_computation.11 | custom fusion | flops 663552 | bytes 885632 | tf_op jit(solution)/shard_map/while/body/eval_jaxpr/scatter-add | solution.py:184
  91.2 1.4 copy.67
  92.6 3.1 %scatter.4 = bf16[3,3,256,96]{2,1,0,3:T(4,128)(2,1)} dynamic-update-slice(bf16[3,3,256,96]{2,1,0,3:T(4,128)(2,1)} %copy.67, bf16[1,1,256,96]{2,1,0,3:T(2,128)(2,1)S(1)} %broadcast.96, s32[]{:T(128)} %constant.89.clone.1, s32[]{:T(128)} %constant.89.clone.1, s32[]{:T(128)} %constant.83.clone.1, s32[]{:T(128)} %constant.83.clone.1) | dynamic-update-slice | bytes 98308 | tf_op jit(solution)/shard_map/scatter | solution.py:195
  95.7 1.8 fusion.8
  97.6 1.8 copy.57
  99.3 1.9 slice.72
  101.2 2.1 collective-permute-start.4
  103.3 1.3 fusion.11
  104.7 1.5 copy.58
  106.1 1.6 convert_element_type.27
  108.9 3.0 %collective-permute-start.5 = (bf16[1,3,192,128]{3,2,1,0:T(8,128)(2,1)}, bf16[1,3,192,128]{3,2,1,0:T(8,128)(2,1)S(1)}, u32[]{:S(2)}, u32[]{:S(2)}) collective-permute-start(bf16[1,3,192,128]{3,2,1,0:T(8,128)(2,1)} %slice.74), channel_id=1, source_target_pairs={{8,0},{16,8},{24,16},{32,24},{40,32},{48,40},{56,48},{64,56},{72,6... | collective-permute-start | bytes 442376 | tf_op jit(solution)/shard_map/ppermute | solution.py:129
  113.7 1.3 gather_fusion.1
  118.2 5.5 %collective-permute-start.6 = (bf16[5,1,192,128]{3,2,1,0:T(8,128)(2,1)}, bf16[5,1,192,128]{3,2,1,0:T(8,128)(2,1)}, u32[]{:S(2)}, u32[]{:S(2)}) collective-permute-start(bf16[5,1,192,128]{3,2,1,0:T(8,128)(2,1)} %get-tuple-element.68), channel_id=1, source_target_pairs={{0,1},{1,2},{2,3},{3,4},{4,5},{5,6},{6,7},{8,9},{9,10},{10,11},{11... | collective-permute-start | bytes 737288 | tf_op jit(solution)/shard_map/ppermute | solution.py:126
  123.6 1.3 collective-permute-start.7
  124.9 1.3 fusion.x_ref
  127.1 89.8 %shard_map.93 = f32[3072,128]{1,0:T(8,128)} custom-call(f32[3072,128]{1,0:T(8,128)} %fusion.x_ref), custom_call_target="tpu_custom_call" | custom-call | tf_op jit(solution)/shard_map/pallas_call | solution.py:95
  217.0 1.4 copy-done.1
  219.6 1.4 copy.64
  222.4 1.2 concatenate.35
  223.6 1.2 concatenate.37
  (78 shorter events, 15.1 us)
Async XLA Ops:
  0.6 39.1 %copy-start = (bf16[2592,96]{0,1:T(8,128)(2,1)S(1)}, bf16[2592,96]{0,1:T(8,128)(2,1)}, u32[]{:S(2)}) copy-start(bf16[2592,96]{0,1:T(8,128)(2,1)} %param.11) | copy-start | bytes 1492996
  1.8 13.4 %collective-permute-start = (bf16[1,1,192,128]{3,2,1,0:T(8,128)(2,1)S(1)}, bf16[1,1,192,128]{3,2,1,0:T(8,128)(2,1)S(1)}, u32[]{:S(2)}, u32[]{:S(2)}) collective-permute-start(bf16[1,1,192,128]{3,2,1,0:T(8,128)(2,1)S(1)} %reshape.165), channel_id=1, source_target_pairs={{0,8},{8,16},{16,24},{24,32},{32,40},{40,48},{48,56},{56,64},{64,7... | collective-permute-start | bytes 147464 | tf_op jit(solution)/shard_map/ppermute | solution.py:126
  6.3 8.9 %collective-permute-start.1 = (bf16[1,1,192,128]{3,2,1,0:T(8,128)(2,1)S(1)}, bf16[1,1,192,128]{3,2,1,0:T(8,128)(2,1)S(1)}, u32[]{:S(2)}, u32[]{:S(2)}) collective-permute-start(bf16[1,1,192,128]{3,2,1,0:T(8,128)(2,1)S(1)} %reshape.165), channel_id=1, source_target_pairs={{8,0},{16,8},{24,16},{32,24},{40,32},{48,40},{56,48},{64,56},{72,6... | collective-permute-start | bytes 147464 | tf_op jit(solution)/shard_map/ppermute | solution.py:129
  15.2 6.6 %collective-permute-start.2 = (bf16[3,1,192,128]{3,2,1,0:T(8,128)(2,1)S(1)}, bf16[3,1,192,128]{3,2,1,0:T(8,128)(2,1)S(1)}, u32[]{:S(2)}, u32[]{:S(2)}) collective-permute-start(bf16[3,1,192,128]{3,2,1,0:T(8,128)(2,1)S(1)} %constant_dynamic-update-slice_fusion), channel_id=1, source_target_pairs={{0,1},{1,2},{2,3},{3,4},{4,5},{5,6},{6,7},{8,9},{9,10},{10,11},{11... | collective-permute-start | bytes 442376 | tf_op jit(solution)/shard_map/ppermute | solution.py:126
  16.5 7.4 %collective-permute-start.3 = (bf16[3,1,192,128]{3,2,1,0:T(8,128)(2,1)S(1)}, bf16[3,1,192,128]{3,2,1,0:T(8,128)(2,1)S(1)}, u32[]{:S(2)}, u32[]{:S(2)}) collective-permute-start(bf16[3,1,192,128]{3,2,1,0:T(8,128)(2,1)S(1)} %constant_dynamic-update-slice_fusion), channel_id=1, source_target_pairs={{1,0},{2,1},{3,2},{4,3},{5,4},{6,5},{7,6},{9,8},{10,9},{11,10},{12... | collective-permute-start | bytes 442376 | tf_op jit(solution)/shard_map/ppermute | solution.py:129
  37.6 2.1 copy-start.10
  42.3 0.6 copy-start.8
  91.1 8.2 %copy-start.3 = (f32[2304,96]{1,0:T(8,128)}, f32[2304,96]{1,0:T(8,128)S(1)}, u32[]{:S(2)}) copy-start(f32[2304,96]{1,0:T(8,128)S(1)} %slice.86) | copy-start | bytes 2654212
  91.2 12.2 %copy-start.2 = (bf16[256,2592]{1,0:T(8,128)(2,1)S(1)}, bf16[256,2592]{1,0:T(8,128)(2,1)}, u32[]{:S(2)}) copy-start(bf16[256,2592]{1,0:T(8,128)(2,1)} %reshape.167) | copy-start | bytes 3981316
  101.2 14.2 %collective-permute-start.4 = (bf16[1,3,192,128]{3,2,1,0:T(8,128)(2,1)}, bf16[1,3,192,128]{3,2,1,0:T(8,128)(2,1)}, u32[]{:S(2)}, u32[]{:S(2)}) collective-permute-start(bf16[1,3,192,128]{3,2,1,0:T(8,128)(2,1)} %slice.72), channel_id=1, source_target_pairs={{0,8},{8,16},{16,24},{24,32},{32,40},{40,48},{48,56},{56,64},{64,7... | collective-permute-start | bytes 442376 | tf_op jit(solution)/shard_map/ppermute | solution.py:126
  108.9 6.3 %copy-start.9 = (bf16[64,128]{1,0:T(8,128)(2,1)S(1)}, bf16[64,128]{1,0:T(8,128)(2,1)}, u32[]{:S(2)}) copy-start(bf16[64,128]{1,0:T(8,128)(2,1)} %param.13) | copy-start | bytes 49156
  108.9 7.6 %collective-permute-start.5 = (bf16[1,3,192,128]{3,2,1,0:T(8,128)(2,1)}, bf16[1,3,192,128]{3,2,1,0:T(8,128)(2,1)S(1)}, u32[]{:S(2)}, u32[]{:S(2)}) collective-permute-start(bf16[1,3,192,128]{3,2,1,0:T(8,128)(2,1)} %slice.74), channel_id=1, source_target_pairs={{8,0},{16,8},{24,16},{32,24},{40,32},{48,40},{56,48},{64,56},{72,6... | collective-permute-start | bytes 442376 | tf_op jit(solution)/shard_map/ppermute | solution.py:129
  112.7 3.7 %copy-start.6 = (bf16[3,3,192,128]{3,2,1,0:T(8,128)(2,1)S(1)}, bf16[3,3,192,128]{3,2,1,0:T(8,128)(2,1)}, u32[]{:S(2)}) copy-start(bf16[3,3,192,128]{3,2,1,0:T(8,128)(2,1)} %convert_element_type.27) | copy-start | bytes 1327108
  116.5 0.9 copy-start.4
  118.2 104.2 %collective-permute-start.6 = (bf16[5,1,192,128]{3,2,1,0:T(8,128)(2,1)}, bf16[5,1,192,128]{3,2,1,0:T(8,128)(2,1)}, u32[]{:S(2)}, u32[]{:S(2)}) collective-permute-start(bf16[5,1,192,128]{3,2,1,0:T(8,128)(2,1)} %get-tuple-element.68), channel_id=1, source_target_pairs={{0,1},{1,2},{2,3},{3,4},{4,5},{5,6},{6,7},{8,9},{9,10},{10,11},{11... | collective-permute-start | bytes 737288 | tf_op jit(solution)/shard_map/ppermute | solution.py:126
  123.6 100.0 %collective-permute-start.7 = (bf16[5,1,192,128]{3,2,1,0:T(8,128)(2,1)}, bf16[5,1,192,128]{3,2,1,0:T(8,128)(2,1)}, u32[]{:S(2)}, u32[]{:S(2)}) collective-permute-start(bf16[5,1,192,128]{3,2,1,0:T(8,128)(2,1)} %get-tuple-element.69), channel_id=1, source_target_pairs={{1,0},{2,1},{3,2},{4,3},{5,4},{6,5},{7,6},{9,8},{10,9},{11,10},{12... | collective-permute-start | bytes 737288 | tf_op jit(solution)/shard_map/ppermute | solution.py:129
  216.9 1.4 copy-start.1
  216.9 2.3 %slice-start = ((f32[3072,128]{1,0:T(8,128)}), f32[1944,128]{1,0:T(8,128)S(1)}, s32[]{:S(2)}) async-start(f32[3072,128]{1,0:T(8,128)} %shard_map.93), calls=%async_computation | async-start | bytes 1990656 | tf_op jit(solution)/shard_map/slice | solution.py:116
  219.6 1.4 copy-start.7
  219.6 2.2 copy-start.5

commit v2 on v1

--- a/solution.py
+++ b/solution.py
@@ -131,27 +131,72 @@
     return block
 
 
+def _one_hot(pos_ref, o, rows):
+    column = pos_ref[:, o:o + 1]
+    lanes = lax.broadcasted_iota(jnp.int32, (column.shape[0], rows), 1)
+    return (column == lanes).astype(jnp.bfloat16)
+
+
+def conv_fwd_kernel(pos_ref, table_ref, w_ref, out_ref):
+    channels = table_ref.shape[1]
+    table = table_ref[...]
+    total = jnp.zeros(out_ref.shape, jnp.float32)
+    for o in range(pos_ref.shape[1]):
+        picked = jnp.dot(_one_hot(pos_ref, o, table.shape[0]), table, preferred_element_type=jnp.float32)
+        weight = w_ref[o * channels:(o + 1) * channels, :]
+        total = total + jnp.dot(picked.astype(jnp.bfloat16), weight, preferred_element_type=jnp.float32)
+    out_ref[...] = total
+
+
+def conv_bwd_kernel(pos_ref, table_ref, grad_ref, w_ref, tgrad_ref, wgrad_ref):
+    channels = table_ref.shape[1]
+    table = table_ref[...]
+    grad = grad_ref[...]
+    back = (((0,), (0,)), ((), ()))
+    total = jnp.zeros(tgrad_ref.shape, jnp.float32)
+    for o in range(pos_ref.shape[1]):
+        hot = _one_hot(pos_ref, o, table.shape[0])
+        picked = jnp.dot(hot, table, preferred_element_type=jnp.float32).astype(jnp.bfloat16)
+        wgrad_ref[o * channels:(o + 1) * channels, :] = lax.dot_general(
+            picked, grad, back, preferred_element_type=jnp.float32)
+        weight = w_ref[o * channels:(o + 1) * channels, :]
+        spread = lax.dot_general(grad, weight, (((1,), (1,)), ((), ())), preferred_element_type=jnp.float32)
+        high = spread.astype(jnp.bfloat16)
+        low = (spread - high.astype(jnp.float32)).astype(jnp.bfloat16)
+        total = total + lax.dot_general(hot, high, back, preferred_element_type=jnp.float32)
+        total = total + lax.dot_general(hot, low, back, preferred_element_type=jnp.float32)
+    tgrad_ref[...] = total
+
+
+def _vmem_call(kernel, outs, *args):
+    return pl.pallas_call(
+        kernel,
+        out_shape=outs,
+        in_specs=[pl.BlockSpec(memory_space=pltpu.VMEM)] * len(args),
+        out_specs=jax.tree.map(lambda _: pl.BlockSpec(memory_space=pltpu.VMEM), outs),
+    )(*args)
+
+
 def on_device(features, neighbours, down_map, w_conv, w_down, coarse_grad):
     voxels, channels = features.shape
     offsets = neighbours.shape[1]
+    rim = 64
     absent = neighbours >= 9 * voxels
     slot_idx = neighbours // voxels
     local_idx = neighbours - slot_idx * voxels
+    halo_slot = jnp.where(slot_idx < 4, slot_idx, slot_idx - 1)
+    compact = jnp.where(slot_idx == 4, 8 * rim + local_idx, halo_slot * rim + local_idx)
+    positions = jnp.where(absent, -1, compact).astype(jnp.int32)
+    sendable = features[:rim].reshape(1, 1, rim * channels // 128, 128)
+    extended = extended_2(sendable, (("region", 0), ("slab", 1)), 1).reshape(9, rim, channels)
+    halo = jnp.concatenate([extended[:4], extended[5:]], axis=0).reshape(8 * rim, channels)
+    table = jnp.concatenate([halo, features], axis=0)
+    table_rows = table.shape[0]
+
+    conv_out = _vmem_call(
+        conv_fwd_kernel, jax.ShapeDtypeStruct((voxels, channels), jnp.float32), positions, table, w_conv)
+    hidden = (features.astype(jnp.float32) + jax.nn.silu(conv_out)).astype(jnp.bfloat16)
     zero_row = jnp.zeros((1, channels), features.dtype)
-    sendable = features.reshape(1, 1, voxels * channels // 128, 128)
-    extended = extended_2(sendable, (("region", 0), ("slab", 1)), 1)
-    table = jnp.concatenate([extended.reshape(9 * voxels, channels), zero_row], axis=0)
-    positions = jnp.where(absent, 9 * voxels, slot_idx * voxels + local_idx)
-    row_block = min(voxels, 512)
-    block_count = voxels // row_block
-    pos_blocks = positions.reshape(block_count, row_block, offsets)
-
-    def conv_block(block_pos):
-        rows = table[block_pos].reshape(row_block, offsets * channels)
-        return jnp.dot(rows, w_conv, preferred_element_type=jnp.float32)
-
-    conv_out = lax.map(conv_block, pos_blocks).reshape(voxels, channels)
-    hidden = (features.astype(jnp.float32) + jax.nn.silu(conv_out)).astype(jnp.bfloat16)
     coarse_count, taps = down_map.shape
     down_local = jnp.minimum(down_map, voxels)
     hidden_pad = jnp.concatenate([hidden, zero_row], axis=0)
@@ -169,36 +214,24 @@
     conv_grad = (hidden_grad * sigmoid_y * (1.0 + conv_out * (1.0 - sigmoid_y))).astype(
         jnp.bfloat16
     )
-    grad_blocks = conv_grad.reshape(block_count, row_block, channels)
-
-    def back_block(carry, inputs):
-        table_grad, weight_grad = carry
-        block_pos, block_grad = inputs
-        rows = table[block_pos].reshape(row_block, offsets * channels)
-        weight_grad = weight_grad + lax.dot_general(
-            rows, block_grad, (((0,), (0,)), ((), ())), preferred_element_type=jnp.float32
-        )
-        spread = jnp.dot(block_grad, w_conv.T, preferred_element_type=jnp.float32).reshape(
-            -1, channels
-        )
-        table_grad = table_grad.at[block_pos.reshape(-1)].add(spread)
-        return ((table_grad, weight_grad), None)
-
-    start = (
-        jnp.zeros((table.shape[0], channels), jnp.float32),
-        jnp.zeros(w_conv.shape, jnp.float32),
-    )
-    (table_grad, conv_wgrad), unused = lax.scan(back_block, start, (pos_blocks, grad_blocks))
+    table_grad, conv_wgrad = _vmem_call(
+        conv_bwd_kernel,
+        (jax.ShapeDtypeStruct((table_rows, channels), jnp.float32),
+         jax.ShapeDtypeStruct(w_conv.shape, jnp.float32)),
+        positions, table, conv_grad, w_conv)
     conv_wgrad, down_wgrad = summed_everywhere([conv_wgrad, down_wgrad])
-    sections = table_grad[: 9 * voxels].reshape(3, 3, voxels, channels)
-    own_part = sections[1, 1]
-    outgoing = sections.at[1, 1].set(0.0).reshape(3, 3, voxels * channels // 128, 128)
+    own_part = table_grad[8 * rim:]
+    halo_grad = table_grad[: 8 * rim].reshape(8, rim, channels)
+    sections = jnp.concatenate(
+        [halo_grad[:4], jnp.zeros((1, rim, channels), jnp.float32), halo_grad[4:]], axis=0)
+    outgoing = sections.reshape(3, 3, rim * channels // 128, 128)
     returned = extended_2(outgoing.astype(jnp.bfloat16), (("region", 0), ("slab", 1)), 1).astype(
         outgoing.dtype
     )
-    returned = returned.reshape(5, 5, voxels, channels)
+    returned = returned.reshape(5, 5, rim, channels)
     incoming = jnp.sum(returned[0::2, 0::2], axis=(0, 1))
-    grad_input = hidden_grad + own_part + incoming
+    grad_input = hidden_grad + own_part
+    grad_input = grad_input.at[:rim].add(incoming)
     return (coarse, grad_input, conv_wgrad, down_wgrad)
 
 

time: 227 us -> 166 us (0.73)
  other arithmetic: 52.1 us -> 11.3 us
  local copies, waits for them, and re-layouts: 49.7 us -> 12.2 us
  Pallas kernels: 89.8 us -> 112 us
  matrix products: 6.59 us -> 1.92 us
    scatter-add x1, other arithmetic: 44.8 us -> 0.01 us  [on_device(): grad_input = grad_input.at[:rim].add(incoming)]
    pallas_call x0 -> x2, Pallas kernels: none -> 25.7 us  [_vmem_call(): pl.pallas_call(kernel, out_shape=outs, in_specs=[pl.BlockSpec(memory_spac...]
    gather x1 -> x0, local copies, waits for them, and re-layouts: 13.1 us -> none  [conv_block(): rows = table[block_pos].reshape(row_block, offsets * channels)]
    reshape x6 -> x2, local copies, waits for them, and re-layouts: 7.6 us -> 0.25 us  [the longest x1 0.14 us: on_device(): extended_2(sendable, (('region', 0), ('slab', 1)), 1)]
    dot_general x3 -> x0, matrix products: 4.44 us -> none  [the longest x1 2.56 us: conv_block(): return jnp.dot(rows, w_conv, preferred_element_type=jnp.float32)]
    slice x3 -> x2, local copies, waits for them, and re-layouts: 4.43 us -> 0.13 us  [extended_2(): lax.slice_in_dim(block, block.shape[dim] - width, None, axis=dim)]
    ppermute x4, starting transfers between devices: 13.4 us -> 9.7 us  [extended_2(): lax.ppermute(lax.slice_in_dim(block, block.shape[dim] - width, None, axis...]
    pallas_call x1, Pallas kernels: 89.8 us -> 86.4 us  [allreduce(): pl.pallas_call(allreduce_kernel, out_shape=jax.ShapeDtypeStruct((rows, 12...]
  transfers between devices with their start and end apart: 8 -> 8, of which waited for: 1 -> 1; matrix products, arithmetic and copies ran while one was open for 11% -> 10% of each run, Pallas kernels for 40% -> 52%
where the time goes in v2:
time: 166 us; the launch traced here: 165 us
  Pallas kernels  112 us (67%)
  starting transfers between devices  23.5 us (14%)
  local copies, waits for them, and re-layouts  12.2 us (7%)
  other arithmetic  11.3 us (7%)
  waiting for transfers between devices  2.84 us (2%)
  matrix products  1.92 us (1%)
    pallas_call x1, Pallas kernels, allreduce(): pl.pallas_call(allreduce_kernel, out_shape=jax.ShapeDtypeStruct((rows, 12...  86.4 us
    pallas_call x2, Pallas kernels, _vmem_call(): pl.pallas_call(kernel, out_shape=outs, in_specs=[pl.BlockSpec(memory_spac...  25.7 us
    ppermute x4, starting transfers between devices, extended_2(): lax.ppermute(lax.slice_in_dim(block, 0, width, axis=dim), axis, backward)  13.8 us
    ppermute x4, starting transfers between devices, extended_2(): lax.ppermute(lax.slice_in_dim(block, block.shape[dim] - width, None, axis...  9.7 us
    unnamed x17, local copies, waits for them, and re-layouts  5.05 us
    scatter-add x1, other arithmetic, on_device(): hidden_grad.at[down_local.reshape(-1)]  3.86 us
  transfers between devices with their start and end apart: 8, of which 1 were waited for; matrix products, arithmetic and copies ran while one was open for 10% of the time, Pallas kernels for 52%

profile of v2, /device:TPU:1, one launch (start us, length us, event | category | flops | bytes accessed | tf_op | source)
XLA Modules:
  0.0 164.8 jit_solution(14374647112692585174)
XLA Ops:
  0.7 0.8 slice.89
  1.7 8.8 %collective-permute-start.1 = (bf16[1,1,48,128]{3,2,1,0:T(8,128)(2,1)S(1)}, bf16[1,1,48,128]{3,2,1,0:T(8,128)(2,1)S(1)}, u32[]{:S(2)}, u32[]{:S(2)}) collective-permute-start(bf16[1,1,48,128]{3,2,1,0:T(8,128)(2,1)S(1)} %reshape.115), channel_id=1, source_target_pairs={{8,0},{16,8},{24,16},{32,24},{40,32},{48,40},{56,48},{64,56},{72,6... | collective-permute-start | bytes 36872 | tf_op jit(solution)/shard_map/ppermute | solution.py:129
  10.5 1.9 %collective-permute-start = (bf16[1,1,48,128]{3,2,1,0:T(8,128)(2,1)S(1)}, bf16[1,1,48,128]{3,2,1,0:T(8,128)(2,1)S(1)}, u32[]{:S(2)}, u32[]{:S(2)}) collective-permute-start(bf16[1,1,48,128]{3,2,1,0:T(8,128)(2,1)S(1)} %reshape.115), channel_id=1, source_target_pairs={{0,8},{8,16},{16,24},{24,32},{32,40},{40,48},{48,56},{56,64},{64,7... | collective-permute-start | bytes 36872 | tf_op jit(solution)/shard_map/ppermute | solution.py:126
  12.4 0.7 broadcast_minimum_fusion
  13.3 0.9 copy.25
  14.1 0.8 fusion.5.pos_ref
  14.9 0.9 fusion.14
  16.1 1.3 collective-permute-start.3
  17.4 4.0 %collective-permute-start.2 = (bf16[3,1,48,128]{3,2,1,0:T(8,128)(2,1)S(1)}, bf16[3,1,48,128]{3,2,1,0:T(8,128)(2,1)S(1)}, u32[]{:S(2)}, u32[]{:S(2)}) collective-permute-start(bf16[3,1,48,128]{3,2,1,0:T(8,128)(2,1)S(1)} %constant_dynamic-update-slice_fusion), channel_id=1, source_target_pairs={{0,1},{1,2},{2,3},{3,4},{4,5},{5,6},{6,7},{8,9},{9,10},{10,11},{11... | collective-permute-start | bytes 110600 | tf_op jit(solution)/shard_map/ppermute | solution.py:126
  21.4 0.9 copy.24
  22.4 1.1 copy.33.w_ref
  23.6 3.9 %scatter_custom_fusion = f32[257,96]{1,0:T(8,128)S(1)} fusion(s32[512]{0:T(512)S(1)} %bitcast.30, f32[512,96]{1,0:T(8,128)S(1)} %reshape.137, f32[]{:T(128)} %constant.74.clone.1), kind=kCustom, calls=%fused_computation.29 | custom fusion | flops 49152 | bytes 98692 | tf_op jit(solution)/shard_map/scatter-add | solution.py:207
  27.7 0.7 pad_maximum_fusion.1.table_ref
  28.5 7.7 %shard_map.93 = f32[256,96]{1,0:T(8,128)} custom-call(s32[256,27]{1,0:T(8,128)} %fusion.5.pos_ref, bf16[768,96]{1,0:T(8,128)(2,1)} %pad_maximum_fusion.1.table_ref, bf16[2592,96]{1,0:T(8,128)(2,1)} %copy.33.w_ref), custom_call_target="tpu_custom_call" | custom-call | tf_op jit(solution)/shard_map/pallas_call | solution.py:172
  36.1 1.6 multiply_convert_fusion
  37.8 18.0 %shard_map.94 = (f32[768,96]{1,0:T(8,128)}, f32[2592,96]{1,0:T(8,128)}) custom-call(s32[256,27]{1,0:T(8,128)} %fusion.5.pos_ref, bf16[768,96]{1,0:T(8,128)(2,1)} %pad_maximum_fusion.1.table_ref, bf16[256,96]{1,0:T(8,128)(2,1)} %get-tuple-element.36.grad_ref, bf16[2592,96]{1,0:T(8,128)(2,1)} %copy.33.w_ref), custom_call_target="tpu_custom_call" | custom-call | tf_op jit(solution)/shard_map/pallas_call | solution.py:172
  55.7 0.9 slice_add_fusion
  56.7 1.1 convert.11
  57.9 1.3 gather_fusion
  59.6 0.8 reshape.121
  60.6 1.9 %collective-permute-start.4 = (bf16[1,3,48,128]{3,2,1,0:T(8,128)(2,1)S(1)}, bf16[1,3,48,128]{3,2,1,0:T(8,128)(2,1)S(1)}, u32[]{:S(2)}, u32[]{:S(2)}) collective-permute-start(bf16[1,3,48,128]{3,2,1,0:T(8,128)(2,1)S(1)} %slice.96), channel_id=1, source_target_pairs={{0,8},{8,16},{16,24},{24,32},{32,40},{40,48},{48,56},{56,64},{64,7... | collective-permute-start | bytes 110600 | tf_op jit(solution)/shard_map/ppermute | solution.py:126
  62.5 1.3 fusion.x_ref
  64.2 2.4 %collective-permute-start.5 = (bf16[1,3,48,128]{3,2,1,0:T(8,128)(2,1)S(1)}, bf16[1,3,48,128]{3,2,1,0:T(8,128)(2,1)S(1)}, u32[]{:S(2)}, u32[]{:S(2)}) collective-permute-start(bf16[1,3,48,128]{3,2,1,0:T(8,128)(2,1)S(1)} %slice.102), channel_id=1, source_target_pairs={{8,0},{16,8},{24,16},{32,24},{40,32},{48,40},{56,48},{64,56},{72,6... | collective-permute-start | bytes 110600 | tf_op jit(solution)/shard_map/ppermute | solution.py:129
  66.7 2.8 %collective-permute-done.5 = bf16[1,3,48,128]{3,2,1,0:T(8,128)(2,1)S(1)} collective-permute-done((bf16[1,3,48,128]{3,2,1,0:T(8,128)(2,1)S(1)}, bf16[1,3,48,128]{3,2,1,0:T(8,128)(2,1)S(1)}, u32[]{:S(2)}, u32[]{:S(2)}) %collective-permute-start.5) | collective-permute-done | bytes 36896 | tf_op jit(solution)/shard_map/ppermute | solution.py:129
  69.5 1.9 %collective-permute-start.6 = (bf16[5,1,48,128]{3,2,1,0:T(8,128)(2,1)S(1)}, bf16[5,1,48,128]{3,2,1,0:T(8,128)(2,1)S(1)}, u32[]{:S(2)}, u32[]{:S(2)}) collective-permute-start(bf16[5,1,48,128]{3,2,1,0:T(8,128)(2,1)S(1)} %get-tuple-element.32), channel_id=1, source_target_pairs={{0,1},{1,2},{2,3},{3,4},{4,5},{5,6},{6,7},{8,9},{9,10},{10,11},{11... | collective-permute-start | bytes 184328 | tf_op jit(solution)/shard_map/ppermute | solution.py:126
  71.4 1.3 collective-permute-start.7
  72.7 0.8 convolution_convert_fusion
  73.5 86.4 %shard_map.95 = f32[3072,128]{1,0:T(8,128)} custom-call(f32[3072,128]{1,0:T(8,128)} %fusion.x_ref), custom_call_target="tpu_custom_call" | custom-call | tf_op jit(solution)/shard_map/pallas_call | solution.py:95
  159.9 1.9 %slice.108 = f32[768,128]{1,0:T(8,128)} slice(f32[3072,128]{1,0:T(8,128)} %shard_map.95), slice={[1944:2712], [0:128]} | slice | bytes 786432 | tf_op jit(solution)/shard_map/slice | solution.py:116
  161.8 0.3 reshape.124
  162.1 1.4 copy.40
  164.1 0.7 copy.39
  (53 shorter events, 2.6 us)
Async XLA Ops:
  0.6 14.3 %copy-start = (bf16[768,128]{1,0:T(8,128)(2,1)S(1)}, bf16[768,128]{1,0:T(8,128)(2,1)}, u32[]{:S(2)}) copy-start(bf16[768,128]{1,0:T(8,128)(2,1)} %param.12) | copy-start | bytes 589828
  0.6 21.8 %copy-start.2 = (bf16[2592,96]{0,1:T(8,128)(2,1)S(1)}, bf16[2592,96]{0,1:T(8,128)(2,1)}, u32[]{:S(2)}) copy-start(bf16[2592,96]{0,1:T(8,128)(2,1)} %param.11) | copy-start | bytes 1492996
  1.7 14.4 %collective-permute-start.1 = (bf16[1,1,48,128]{3,2,1,0:T(8,128)(2,1)S(1)}, bf16[1,1,48,128]{3,2,1,0:T(8,128)(2,1)S(1)}, u32[]{:S(2)}, u32[]{:S(2)}) collective-permute-start(bf16[1,1,48,128]{3,2,1,0:T(8,128)(2,1)S(1)} %reshape.115), channel_id=1, source_target_pairs={{8,0},{16,8},{24,16},{32,24},{40,32},{48,40},{56,48},{64,56},{72,6... | collective-permute-start | bytes 36872 | tf_op jit(solution)/shard_map/ppermute | solution.py:129
  10.5 5.5 %collective-permute-start = (bf16[1,1,48,128]{3,2,1,0:T(8,128)(2,1)S(1)}, bf16[1,1,48,128]{3,2,1,0:T(8,128)(2,1)S(1)}, u32[]{:S(2)}, u32[]{:S(2)}) collective-permute-start(bf16[1,1,48,128]{3,2,1,0:T(8,128)(2,1)S(1)} %reshape.115), channel_id=1, source_target_pairs={{0,8},{8,16},{16,24},{24,32},{32,40},{40,48},{48,56},{56,64},{64,7... | collective-permute-start | bytes 36872 | tf_op jit(solution)/shard_map/ppermute | solution.py:126
  16.1 11.4 %collective-permute-start.3 = (bf16[3,1,48,128]{3,2,1,0:T(8,128)(2,1)S(1)}, bf16[3,1,48,128]{3,2,1,0:T(8,128)(2,1)S(1)}, u32[]{:S(2)}, u32[]{:S(2)}) collective-permute-start(bf16[3,1,48,128]{3,2,1,0:T(8,128)(2,1)S(1)} %constant_dynamic-update-slice_fusion), channel_id=1, source_target_pairs={{1,0},{2,1},{3,2},{4,3},{5,4},{6,5},{7,6},{9,8},{10,9},{11,10},{12... | collective-permute-start | bytes 110600 | tf_op jit(solution)/shard_map/ppermute | solution.py:129
  17.4 10.1 %collective-permute-start.2 = (bf16[3,1,48,128]{3,2,1,0:T(8,128)(2,1)S(1)}, bf16[3,1,48,128]{3,2,1,0:T(8,128)(2,1)S(1)}, u32[]{:S(2)}, u32[]{:S(2)}) collective-permute-start(bf16[3,1,48,128]{3,2,1,0:T(8,128)(2,1)S(1)} %constant_dynamic-update-slice_fusion), channel_id=1, source_target_pairs={{0,1},{1,2},{2,3},{3,4},{4,5},{5,6},{6,7},{8,9},{9,10},{10,11},{11... | collective-permute-start | bytes 110600 | tf_op jit(solution)/shard_map/ppermute | solution.py:126
  55.7 3.6 %copy-start.3 = (bf16[64,128]{1,0:T(8,128)(2,1)S(1)}, bf16[64,128]{1,0:T(8,128)(2,1)}, u32[]{:S(2)}) copy-start(bf16[64,128]{1,0:T(8,128)(2,1)} %param.13) | copy-start | bytes 49156
  56.7 2.9 %copy-start.1 = (f32[2592,96]{1,0:T(8,128)S(1)}, f32[2592,96]{1,0:T(8,128)}, u32[]{:S(2)}) copy-start(f32[2592,96]{1,0:T(8,128)} %get-tuple-element.19) | copy-start | bytes 2985988
  60.6 6.1 %collective-permute-start.4 = (bf16[1,3,48,128]{3,2,1,0:T(8,128)(2,1)S(1)}, bf16[1,3,48,128]{3,2,1,0:T(8,128)(2,1)S(1)}, u32[]{:S(2)}, u32[]{:S(2)}) collective-permute-start(bf16[1,3,48,128]{3,2,1,0:T(8,128)(2,1)S(1)} %slice.96), channel_id=1, source_target_pairs={{0,8},{8,16},{16,24},{24,32},{32,40},{40,48},{48,56},{56,64},{64,7... | collective-permute-start | bytes 110600 | tf_op jit(solution)/shard_map/ppermute | solution.py:126
  64.2 5.3 %collective-permute-start.5 = (bf16[1,3,48,128]{3,2,1,0:T(8,128)(2,1)S(1)}, bf16[1,3,48,128]{3,2,1,0:T(8,128)(2,1)S(1)}, u32[]{:S(2)}, u32[]{:S(2)}) collective-permute-start(bf16[1,3,48,128]{3,2,1,0:T(8,128)(2,1)S(1)} %slice.102), channel_id=1, source_target_pairs={{8,0},{16,8},{24,16},{32,24},{40,32},{48,40},{56,48},{64,56},{72,6... | collective-permute-start | bytes 110600 | tf_op jit(solution)/shard_map/ppermute | solution.py:129
  69.5 94.2 %collective-permute-start.6 = (bf16[5,1,48,128]{3,2,1,0:T(8,128)(2,1)S(1)}, bf16[5,1,48,128]{3,2,1,0:T(8,128)(2,1)S(1)}, u32[]{:S(2)}, u32[]{:S(2)}) collective-permute-start(bf16[5,1,48,128]{3,2,1,0:T(8,128)(2,1)S(1)} %get-tuple-element.32), channel_id=1, source_target_pairs={{0,1},{1,2},{2,3},{3,4},{4,5},{5,6},{6,7},{8,9},{9,10},{10,11},{11... | collective-permute-start | bytes 184328 | tf_op jit(solution)/shard_map/ppermute | solution.py:126
  71.4 92.4 %collective-permute-start.7 = (bf16[5,1,48,128]{3,2,1,0:T(8,128)(2,1)S(1)}, bf16[5,1,48,128]{3,2,1,0:T(8,128)(2,1)S(1)}, u32[]{:S(2)}, u32[]{:S(2)}) collective-permute-start(bf16[5,1,48,128]{3,2,1,0:T(8,128)(2,1)S(1)} %get-tuple-element.33), channel_id=1, source_target_pairs={{1,0},{2,1},{3,2},{4,3},{5,4},{6,5},{7,6},{9,8},{10,9},{11,10},{12... | collective-permute-start | bytes 184328 | tf_op jit(solution)/shard_map/ppermute | solution.py:129
  159.9 1.9 %slice-start = ((f32[3072,128]{1,0:T(8,128)}), f32[1944,128]{1,0:T(8,128)S(1)}, s32[]{:S(2)}) async-start(f32[3072,128]{1,0:T(8,128)} %shard_map.95), calls=%async_computation | async-start | bytes 1990656 | tf_op jit(solution)/shard_map/slice | solution.py:116

commit v3 on v2

--- a/solution.py
+++ b/solution.py
@@ -49,6 +49,12 @@
 
     off = 0
     offs = []
+    pending = []
+
+    def settle(copy, k, r, s):
+        copy.wait_send()
+        pl.semaphore_signal(free_sem.at[k], inc=1, device_id=(r, s), device_id_type=MESH)
+
     for k, (v, r, s) in enumerate(steps):
         size = HALVES[k]
         keep = pl.multiple_of(off + v * size, 8)
@@ -59,11 +65,14 @@
             send_sem=send_sem.at[k], recv_sem=recv_sem.at[k],
             device_id=(r, s), device_id_type=MESH)
         copy.start()
-        copy.wait()
-        pl.semaphore_signal(free_sem.at[k], inc=1, device_id=(r, s), device_id_type=MESH)
+        if pending:
+            settle(*pending.pop())
+        copy.wait_recv()
         o_ref[pl.ds(keep, size)] = src[pl.ds(keep, size)] + recvs[k][...]
+        pending.append((copy, k, r, s))
         off = keep
         offs.append(keep)
+    settle(*pending.pop())
     last = HALVES[-1]
     for i, (v, r, s) in enumerate(fulls):
         k = len(steps) + i
@@ -75,6 +84,7 @@
         copy.wait()
         o_ref[pl.ds(off, last)] = o_ref[pl.ds(off, last)] + recvs[k][...]
     base = len(steps) + len(fulls)
+    sent = []
     for k in reversed(range(len(steps))):
         v, r, s = steps[k]
         size = HALVES[k]
@@ -85,7 +95,10 @@
             device_id=(r, s), device_id_type=MESH)
         pl.semaphore_wait(free_sem.at[k], 1)
         copy.start()
-        copy.wait()
+        copy.wait_recv()
+        sent.append(copy)
+    for copy in sent:
+        copy.wait_send()
 
 
 def allreduce(x):

time: 166 us -> 168 us (1.012)
  Pallas kernels: 112 us -> 115 us
    pallas_call x1, Pallas kernels: 86.4 us -> 88.9 us  [allreduce(): pl.pallas_call(allreduce_kernel, out_shape=jax.ShapeDtypeStruct((rows, 12...]
  transfers between devices with their start and end apart: 8 -> 8, of which waited for: 1 -> 1; matrix products, arithmetic and copies ran while one was open for 10% -> 10% of each run, Pallas kernels for 52% -> 53%
where the time goes in v3:
time: 168 us; the launch traced here: 167 us
  Pallas kernels  115 us (68%)
  starting transfers between devices  23.5 us (14%)
  local copies, waits for them, and re-layouts  12.2 us (7%)
  other arithmetic  11.3 us (7%)
  waiting for transfers between devices  2.84 us (2%)
  matrix products  1.92 us (1%)
    pallas_call x1, Pallas kernels, allreduce(): pl.pallas_call(allreduce_kernel, out_shape=jax.ShapeDtypeStruct((rows, 12...  88.9 us
    pallas_call x2, Pallas kernels, _vmem_call(): pl.pallas_call(kernel, out_shape=outs, in_specs=[pl.BlockSpec(memory_spac...  25.7 us
    ppermute x4, starting transfers between devices, extended_2(): lax.ppermute(lax.slice_in_dim(block, 0, width, axis=dim), axis, backward)  13.8 us
    ppermute x4, starting transfers between devices, extended_2(): lax.ppermute(lax.slice_in_dim(block, block.shape[dim] - width, None, axis...  9.71 us
    unnamed x17, local copies, waits for them, and re-layouts  5.05 us
    scatter-add x1, other arithmetic, on_device(): hidden_grad.at[down_local.reshape(-1)]  3.85 us
  transfers between devices with their start and end apart: 8, of which 1 were waited for; matrix products, arithmetic and copies ran while one was open for 10% of the time, Pallas kernels for 53%

profile of v3, /device:TPU:1, one launch (start us, length us, event | category | flops | bytes accessed | tf_op | source)
XLA Modules:
  0.0 167.4 jit_solution(6837132619225298466)
XLA Ops:
  0.7 0.8 slice.89
  1.7 8.8 %collective-permute-start.1 = (bf16[1,1,48,128]{3,2,1,0:T(8,128)(2,1)S(1)}, bf16[1,1,48,128]{3,2,1,0:T(8,128)(2,1)S(1)}, u32[]{:S(2)}, u32[]{:S(2)}) collective-permute-start(bf16[1,1,48,128]{3,2,1,0:T(8,128)(2,1)S(1)} %reshape.115), channel_id=1, source_target_pairs={{8,0},{16,8},{24,16},{32,24},{40,32},{48,40},{56,48},{64,56},{72,6... | collective-permute-start | bytes 36872 | tf_op jit(solution)/shard_map/ppermute | solution.py:142
  10.5 1.9 %collective-permute-start = (bf16[1,1,48,128]{3,2,1,0:T(8,128)(2,1)S(1)}, bf16[1,1,48,128]{3,2,1,0:T(8,128)(2,1)S(1)}, u32[]{:S(2)}, u32[]{:S(2)}) collective-permute-start(bf16[1,1,48,128]{3,2,1,0:T(8,128)(2,1)S(1)} %reshape.115), channel_id=1, source_target_pairs={{0,8},{8,16},{16,24},{24,32},{32,40},{40,48},{48,56},{56,64},{64,7... | collective-permute-start | bytes 36872 | tf_op jit(solution)/shard_map/ppermute | solution.py:139
  12.4 0.7 broadcast_minimum_fusion
  13.3 0.9 copy.25
  14.1 0.8 fusion.5.pos_ref
  14.9 0.9 fusion.14
  16.1 1.3 collective-permute-start.3
  17.4 4.0 %collective-permute-start.2 = (bf16[3,1,48,128]{3,2,1,0:T(8,128)(2,1)S(1)}, bf16[3,1,48,128]{3,2,1,0:T(8,128)(2,1)S(1)}, u32[]{:S(2)}, u32[]{:S(2)}) collective-permute-start(bf16[3,1,48,128]{3,2,1,0:T(8,128)(2,1)S(1)} %constant_dynamic-update-slice_fusion), channel_id=1, source_target_pairs={{0,1},{1,2},{2,3},{3,4},{4,5},{5,6},{6,7},{8,9},{9,10},{10,11},{11... | collective-permute-start | bytes 110600 | tf_op jit(solution)/shard_map/ppermute | solution.py:139
  21.4 0.9 copy.24
  22.4 1.1 copy.33.w_ref
  23.6 3.9 %scatter_custom_fusion = f32[257,96]{1,0:T(8,128)S(1)} fusion(s32[512]{0:T(512)S(1)} %bitcast.30, f32[512,96]{1,0:T(8,128)S(1)} %reshape.137, f32[]{:T(128)} %constant.74.clone.1), kind=kCustom, calls=%fused_computation.29 | custom fusion | flops 49152 | bytes 98692 | tf_op jit(solution)/shard_map/scatter-add | solution.py:220
  27.7 0.7 pad_maximum_fusion.1.table_ref
  28.5 7.7 %shard_map.93 = f32[256,96]{1,0:T(8,128)} custom-call(s32[256,27]{1,0:T(8,128)} %fusion.5.pos_ref, bf16[768,96]{1,0:T(8,128)(2,1)} %pad_maximum_fusion.1.table_ref, bf16[2592,96]{1,0:T(8,128)(2,1)} %copy.33.w_ref), custom_call_target="tpu_custom_call" | custom-call | tf_op jit(solution)/shard_map/pallas_call | solution.py:185
  36.1 1.6 multiply_convert_fusion
  37.8 18.0 %shard_map.94 = (f32[768,96]{1,0:T(8,128)}, f32[2592,96]{1,0:T(8,128)}) custom-call(s32[256,27]{1,0:T(8,128)} %fusion.5.pos_ref, bf16[768,96]{1,0:T(8,128)(2,1)} %pad_maximum_fusion.1.table_ref, bf16[256,96]{1,0:T(8,128)(2,1)} %get-tuple-element.36.grad_ref, bf16[2592,96]{1,0:T(8,128)(2,1)} %copy.33.w_ref), custom_call_target="tpu_custom_call" | custom-call | tf_op jit(solution)/shard_map/pallas_call | solution.py:185
  55.7 0.9 slice_add_fusion
  56.7 1.1 convert.11
  57.9 1.3 gather_fusion
  59.6 0.8 reshape.121
  60.6 1.9 %collective-permute-start.4 = (bf16[1,3,48,128]{3,2,1,0:T(8,128)(2,1)S(1)}, bf16[1,3,48,128]{3,2,1,0:T(8,128)(2,1)S(1)}, u32[]{:S(2)}, u32[]{:S(2)}) collective-permute-start(bf16[1,3,48,128]{3,2,1,0:T(8,128)(2,1)S(1)} %slice.96), channel_id=1, source_target_pairs={{0,8},{8,16},{16,24},{24,32},{32,40},{40,48},{48,56},{56,64},{64,7... | collective-permute-start | bytes 110600 | tf_op jit(solution)/shard_map/ppermute | solution.py:139
  62.5 1.3 fusion.x_ref
  64.2 2.4 %collective-permute-start.5 = (bf16[1,3,48,128]{3,2,1,0:T(8,128)(2,1)S(1)}, bf16[1,3,48,128]{3,2,1,0:T(8,128)(2,1)S(1)}, u32[]{:S(2)}, u32[]{:S(2)}) collective-permute-start(bf16[1,3,48,128]{3,2,1,0:T(8,128)(2,1)S(1)} %slice.102), channel_id=1, source_target_pairs={{8,0},{16,8},{24,16},{32,24},{40,32},{48,40},{56,48},{64,56},{72,6... | collective-permute-start | bytes 110600 | tf_op jit(solution)/shard_map/ppermute | solution.py:142
  66.7 2.8 %collective-permute-done.5 = bf16[1,3,48,128]{3,2,1,0:T(8,128)(2,1)S(1)} collective-permute-done((bf16[1,3,48,128]{3,2,1,0:T(8,128)(2,1)S(1)}, bf16[1,3,48,128]{3,2,1,0:T(8,128)(2,1)S(1)}, u32[]{:S(2)}, u32[]{:S(2)}) %collective-permute-start.5) | collective-permute-done | bytes 36896 | tf_op jit(solution)/shard_map/ppermute | solution.py:142
  69.5 1.9 %collective-permute-start.6 = (bf16[5,1,48,128]{3,2,1,0:T(8,128)(2,1)S(1)}, bf16[5,1,48,128]{3,2,1,0:T(8,128)(2,1)S(1)}, u32[]{:S(2)}, u32[]{:S(2)}) collective-permute-start(bf16[5,1,48,128]{3,2,1,0:T(8,128)(2,1)S(1)} %get-tuple-element.32), channel_id=1, source_target_pairs={{0,1},{1,2},{2,3},{3,4},{4,5},{5,6},{6,7},{8,9},{9,10},{10,11},{11... | collective-permute-start | bytes 184328 | tf_op jit(solution)/shard_map/ppermute | solution.py:139
  71.4 1.3 collective-permute-start.7
  72.7 0.8 convolution_convert_fusion
  73.5 88.9 %shard_map.95 = f32[3072,128]{1,0:T(8,128)} custom-call(f32[3072,128]{1,0:T(8,128)} %fusion.x_ref), custom_call_target="tpu_custom_call" | custom-call | tf_op jit(solution)/shard_map/pallas_call | solution.py:108
  162.4 1.9 %slice.108 = f32[768,128]{1,0:T(8,128)} slice(f32[3072,128]{1,0:T(8,128)} %shard_map.95), slice={[1944:2712], [0:128]} | slice | bytes 786432 | tf_op jit(solution)/shard_map/slice | solution.py:129
  164.3 0.3 reshape.124
  164.6 1.4 copy.40
  166.6 0.7 copy.39
  (53 shorter events, 2.6 us)
Async XLA Ops:
  0.6 14.3 %copy-start = (bf16[768,128]{1,0:T(8,128)(2,1)S(1)}, bf16[768,128]{1,0:T(8,128)(2,1)}, u32[]{:S(2)}) copy-start(bf16[768,128]{1,0:T(8,128)(2,1)} %param.12) | copy-start | bytes 589828
  0.6 21.8 %copy-start.2 = (bf16[2592,96]{0,1:T(8,128)(2,1)S(1)}, bf16[2592,96]{0,1:T(8,128)(2,1)}, u32[]{:S(2)}) copy-start(bf16[2592,96]{0,1:T(8,128)(2,1)} %param.11) | copy-start | bytes 1492996
  1.7 14.4 %collective-permute-start.1 = (bf16[1,1,48,128]{3,2,1,0:T(8,128)(2,1)S(1)}, bf16[1,1,48,128]{3,2,1,0:T(8,128)(2,1)S(1)}, u32[]{:S(2)}, u32[]{:S(2)}) collective-permute-start(bf16[1,1,48,128]{3,2,1,0:T(8,128)(2,1)S(1)} %reshape.115), channel_id=1, source_target_pairs={{8,0},{16,8},{24,16},{32,24},{40,32},{48,40},{56,48},{64,56},{72,6... | collective-permute-start | bytes 36872 | tf_op jit(solution)/shard_map/ppermute | solution.py:142
  10.5 5.5 %collective-permute-start = (bf16[1,1,48,128]{3,2,1,0:T(8,128)(2,1)S(1)}, bf16[1,1,48,128]{3,2,1,0:T(8,128)(2,1)S(1)}, u32[]{:S(2)}, u32[]{:S(2)}) collective-permute-start(bf16[1,1,48,128]{3,2,1,0:T(8,128)(2,1)S(1)} %reshape.115), channel_id=1, source_target_pairs={{0,8},{8,16},{16,24},{24,32},{32,40},{40,48},{48,56},{56,64},{64,7... | collective-permute-start | bytes 36872 | tf_op jit(solution)/shard_map/ppermute | solution.py:139
  16.1 11.4 %collective-permute-start.3 = (bf16[3,1,48,128]{3,2,1,0:T(8,128)(2,1)S(1)}, bf16[3,1,48,128]{3,2,1,0:T(8,128)(2,1)S(1)}, u32[]{:S(2)}, u32[]{:S(2)}) collective-permute-start(bf16[3,1,48,128]{3,2,1,0:T(8,128)(2,1)S(1)} %constant_dynamic-update-slice_fusion), channel_id=1, source_target_pairs={{1,0},{2,1},{3,2},{4,3},{5,4},{6,5},{7,6},{9,8},{10,9},{11,10},{12... | collective-permute-start | bytes 110600 | tf_op jit(solution)/shard_map/ppermute | solution.py:142
  17.4 10.1 %collective-permute-start.2 = (bf16[3,1,48,128]{3,2,1,0:T(8,128)(2,1)S(1)}, bf16[3,1,48,128]{3,2,1,0:T(8,128)(2,1)S(1)}, u32[]{:S(2)}, u32[]{:S(2)}) collective-permute-start(bf16[3,1,48,128]{3,2,1,0:T(8,128)(2,1)S(1)} %constant_dynamic-update-slice_fusion), channel_id=1, source_target_pairs={{0,1},{1,2},{2,3},{3,4},{4,5},{5,6},{6,7},{8,9},{9,10},{10,11},{11... | collective-permute-start | bytes 110600 | tf_op jit(solution)/shard_map/ppermute | solution.py:139
  55.7 3.6 %copy-start.3 = (bf16[64,128]{1,0:T(8,128)(2,1)S(1)}, bf16[64,128]{1,0:T(8,128)(2,1)}, u32[]{:S(2)}) copy-start(bf16[64,128]{1,0:T(8,128)(2,1)} %param.13) | copy-start | bytes 49156
  56.7 2.9 %copy-start.1 = (f32[2592,96]{1,0:T(8,128)S(1)}, f32[2592,96]{1,0:T(8,128)}, u32[]{:S(2)}) copy-start(f32[2592,96]{1,0:T(8,128)} %get-tuple-element.19) | copy-start | bytes 2985988
  60.6 6.1 %collective-permute-start.4 = (bf16[1,3,48,128]{3,2,1,0:T(8,128)(2,1)S(1)}, bf16[1,3,48,128]{3,2,1,0:T(8,128)(2,1)S(1)}, u32[]{:S(2)}, u32[]{:S(2)}) collective-permute-start(bf16[1,3,48,128]{3,2,1,0:T(8,128)(2,1)S(1)} %slice.96), channel_id=1, source_target_pairs={{0,8},{8,16},{16,24},{24,32},{32,40},{40,48},{48,56},{56,64},{64,7... | collective-permute-start | bytes 110600 | tf_op jit(solution)/shard_map/ppermute | solution.py:139
  64.2 5.3 %collective-permute-start.5 = (bf16[1,3,48,128]{3,2,1,0:T(8,128)(2,1)S(1)}, bf16[1,3,48,128]{3,2,1,0:T(8,128)(2,1)S(1)}, u32[]{:S(2)}, u32[]{:S(2)}) collective-permute-start(bf16[1,3,48,128]{3,2,1,0:T(8,128)(2,1)S(1)} %slice.102), channel_id=1, source_target_pairs={{8,0},{16,8},{24,16},{32,24},{40,32},{48,40},{56,48},{64,56},{72,6... | collective-permute-start | bytes 110600 | tf_op jit(solution)/shard_map/ppermute | solution.py:142
  69.5 96.7 %collective-permute-start.6 = (bf16[5,1,48,128]{3,2,1,0:T(8,128)(2,1)S(1)}, bf16[5,1,48,128]{3,2,1,0:T(8,128)(2,1)S(1)}, u32[]{:S(2)}, u32[]{:S(2)}) collective-permute-start(bf16[5,1,48,128]{3,2,1,0:T(8,128)(2,1)S(1)} %get-tuple-element.32), channel_id=1, source_target_pairs={{0,1},{1,2},{2,3},{3,4},{4,5},{5,6},{6,7},{8,9},{9,10},{10,11},{11... | collective-permute-start | bytes 184328 | tf_op jit(solution)/shard_map/ppermute | solution.py:139
  71.4 94.9 %collective-permute-start.7 = (bf16[5,1,48,128]{3,2,1,0:T(8,128)(2,1)S(1)}, bf16[5,1,48,128]{3,2,1,0:T(8,128)(2,1)S(1)}, u32[]{:S(2)}, u32[]{:S(2)}) collective-permute-start(bf16[5,1,48,128]{3,2,1,0:T(8,128)(2,1)S(1)} %get-tuple-element.33), channel_id=1, source_target_pairs={{1,0},{2,1},{3,2},{4,3},{5,4},{6,5},{7,6},{9,8},{10,9},{11,10},{12... | collective-permute-start | bytes 184328 | tf_op jit(solution)/shard_map/ppermute | solution.py:142
  162.4 1.9 %slice-start = ((f32[3072,128]{1,0:T(8,128)}), f32[1944,128]{1,0:T(8,128)S(1)}, s32[]{:S(2)}) async-start(f32[3072,128]{1,0:T(8,128)} %shard_map.95), calls=%async_computation | async-start | bytes 1990656 | tf_op jit(solution)/shard_map/slice | solution.py:129

commit v4 on v2

--- a/solution.py
+++ b/solution.py
@@ -30,8 +30,8 @@
     return va + core * (vb - va), ra + core * (rb - ra), sa + core * (sb - sa)
 
 
-def allreduce_kernel(x_ref, o_ref, *scratch):
-    HALVES = [x_ref.shape[0] >> (k + 1) for k in range(HALVINGS)]
+def bwd_allreduce_kernel(pos_ref, table_ref, grad_ref, w_ref, down_ref, o_ref, tgrad_ref, *scratch):
+    HALVES = [o_ref.shape[0] >> (k + 1) for k in range(HALVINGS)]
     recvs = scratch[:9]
     send_sem, recv_sem, free_sem = scratch[9], scratch[10], scratch[11]
     region = lax.axis_index("region")
@@ -45,6 +45,11 @@
     barrier = pltpu.get_barrier_semaphore()
     for _, r, s in steps + fulls:
         pl.semaphore_signal(barrier, inc=1, device_id=(r, s), device_id_type=MESH)
+    conv_bwd_body(pos_ref, table_ref, grad_ref, w_ref, tgrad_ref, o_ref)
+    filled = w_ref.shape[0]
+    o_ref[filled:filled + down_ref.shape[0]] = down_ref[...]
+    o_ref[filled + down_ref.shape[0]:] = jnp.zeros(
+        (o_ref.shape[0] - filled - down_ref.shape[0], o_ref.shape[1]), jnp.float32)
     pl.semaphore_wait(barrier, len(steps) + len(fulls))
 
     off = 0
@@ -53,7 +58,7 @@
         size = HALVES[k]
         keep = pl.multiple_of(off + v * size, 8)
         send = pl.multiple_of(off + (1 - v) * size, 8)
-        src = x_ref if k == 0 else o_ref
+        src = o_ref
         copy = pltpu.make_async_remote_copy(
             src_ref=src.at[pl.ds(send, size)], dst_ref=recvs[k],
             send_sem=send_sem.at[k], recv_sem=recv_sem.at[k],
@@ -88,34 +93,25 @@
         copy.wait()
 
 
-def allreduce(x):
-    rows = x.shape[0]
+def bwd_allreduce(positions, table, conv_grad, w_conv, down):
+    width = w_conv.shape[1]
+    unit = 8 << HALVINGS
+    rows = -(-(w_conv.shape[0] + down.shape[0]) // unit) * unit
     HALVES = [rows >> (k + 1) for k in range(HALVINGS)]
     n_copies = 9 + 7
+    args = (positions, table, conv_grad, w_conv, down)
     return pl.pallas_call(
-        allreduce_kernel,
-        out_shape=jax.ShapeDtypeStruct((rows, 128), jnp.float32),
-        in_specs=[pl.BlockSpec(memory_space=pltpu.VMEM)],
-        out_specs=pl.BlockSpec(memory_space=pltpu.VMEM),
-        scratch_shapes=[pltpu.VMEM((h, 128), jnp.float32) for h in HALVES]
-        + [pltpu.VMEM((HALVES[-1], 128), jnp.float32)] * 2
+        bwd_allreduce_kernel,
+        out_shape=(jax.ShapeDtypeStruct((rows, width), jnp.float32),
+                   jax.ShapeDtypeStruct(table.shape, jnp.float32)),
+        in_specs=[pl.BlockSpec(memory_space=pltpu.VMEM)] * len(args),
+        out_specs=(pl.BlockSpec(memory_space=pltpu.VMEM), pl.BlockSpec(memory_space=pltpu.VMEM)),
+        scratch_shapes=[pltpu.VMEM((h, width), jnp.float32) for h in HALVES]
+        + [pltpu.VMEM((HALVES[-1], width), jnp.float32)] * 2
         + [pltpu.SemaphoreType.DMA((n_copies,)), pltpu.SemaphoreType.DMA((n_copies,))]
         + [pltpu.SemaphoreType.REGULAR((HALVINGS,))],
         compiler_params=pltpu.CompilerParams(collective_id=0, has_side_effects=True),
-    )(x)
-
-
-def summed_everywhere(arrays):
-    flat = jnp.concatenate([a.reshape(-1) for a in arrays])
-    unit = 128 * 8 << HALVINGS
-    rows = -(-flat.size // unit) * unit // 128
-    padded = jnp.pad(flat, (0, rows * 128 - flat.size)).reshape(rows, 128)
-    total = allreduce(padded).reshape(-1)
-    out, at = [], 0
-    for a in arrays:
-        out.append(total[at:at + a.size].reshape(a.shape))
-        at += a.size
-    return out
+    )(*args)
 
 
 def extended_2(block, sides, width):
@@ -148,7 +144,7 @@
     out_ref[...] = total
 
 
-def conv_bwd_kernel(pos_ref, table_ref, grad_ref, w_ref, tgrad_ref, wgrad_ref):
+def conv_bwd_body(pos_ref, table_ref, grad_ref, w_ref, tgrad_ref, wgrad_ref):
     channels = table_ref.shape[1]
     table = table_ref[...]
     grad = grad_ref[...]
@@ -214,12 +210,10 @@
     conv_grad = (hidden_grad * sigmoid_y * (1.0 + conv_out * (1.0 - sigmoid_y))).astype(
         jnp.bfloat16
     )
-    table_grad, conv_wgrad = _vmem_call(
-        conv_bwd_kernel,
-        (jax.ShapeDtypeStruct((table_rows, channels), jnp.float32),
-         jax.ShapeDtypeStruct(w_conv.shape, jnp.float32)),
-        positions, table, conv_grad, w_conv)
-    conv_wgrad, down_wgrad = summed_everywhere([conv_wgrad, down_wgrad])
+    down_flat = down_wgrad.reshape(-1, channels)
+    summed, table_grad = bwd_allreduce(positions, table, conv_grad, w_conv, down_flat)
+    conv_wgrad = summed[: w_conv.shape[0]]
+    down_wgrad = summed[w_conv.shape[0]: w_conv.shape[0] + down_flat.shape[0]].reshape(w_down.shape)
     own_part = table_grad[8 * rim:]
     halo_grad = table_grad[: 8 * rim].reshape(8, rim, channels)
     sections = jnp.concatenate(

time: 166 us -> 168 us (1.012)
  the two profiles are of different devices: /device:TPU:1 before, /device:TPU:207 now
where the time goes in v4:
time: 168 us
  Pallas kernels  107 us (64%)
  starting transfers between devices  28.4 us (17%)
  local copies, waits for them, and re-layouts  13.9 us (8%)
  other arithmetic  8.88 us (5%)
  waiting for transfers between devices  6.64 us (4%)
  matrix products  1.91 us (1%)
    pallas_call x1, Pallas kernels, bwd_allreduce(): pl.pallas_call(bwd_allreduce_kernel, out_shape=(jax.ShapeDtypeStruct((row...  99.1 us
    ppermute x4, starting transfers between devices, extended_2(): lax.ppermute(lax.slice_in_dim(block, block.shape[dim] - width, None, axis...  19.3 us
    ppermute x4, starting transfers between devices, extended_2(): lax.ppermute(lax.slice_in_dim(block, 0, width, axis=dim), axis, backward)  9.14 us
    pallas_call x1, Pallas kernels, _vmem_call(): pl.pallas_call(kernel, out_shape=outs, in_specs=[pl.BlockSpec(memory_spac...  7.68 us
    ppermute x4, waiting for transfers between devices, extended_2(): lax.ppermute(lax.slice_in_dim(block, 0, width, axis=dim), axis, backward)  6.63 us
    unnamed x15, local copies, waits for them, and re-layouts  5.05 us
  transfers between devices with their start and end apart: 8, of which 1 were waited for; matrix products, arithmetic and copies ran while one was open for 9% of the time, Pallas kernels for 0%

profile of v4, /device:TPU:207, one launch (start us, length us, event | category | flops | bytes accessed | tf_op | source)
XLA Modules:
  0.0 167.6 jit_solution(15261071837883626290)
XLA Ops:
  0.7 0.8 slice.87
  1.7 2.6 %collective-permute-start.1 = (bf16[1,1,48,128]{3,2,1,0:T(8,128)(2,1)S(1)}, bf16[1,1,48,128]{3,2,1,0:T(8,128)(2,1)S(1)}, u32[]{:S(2)}, u32[]{:S(2)}) collective-permute-start(bf16[1,1,48,128]{3,2,1,0:T(8,128)(2,1)S(1)} %reshape.103), channel_id=1, source_target_pairs={{8,0},{16,8},{24,16},{32,24},{40,32},{48,40},{56,48},{64,56},{72,6... | collective-permute-start | bytes 36872 | tf_op jit(solution)/shard_map/ppermute | solution.py:125
  4.3 6.3 %collective-permute-start = (bf16[1,1,48,128]{3,2,1,0:T(8,128)(2,1)S(1)}, bf16[1,1,48,128]{3,2,1,0:T(8,128)(2,1)S(1)}, u32[]{:S(2)}, u32[]{:S(2)}) collective-permute-start(bf16[1,1,48,128]{3,2,1,0:T(8,128)(2,1)S(1)} %reshape.103), channel_id=1, source_target_pairs={{0,8},{8,16},{16,24},{24,32},{32,40},{40,48},{48,56},{56,64},{64,7... | collective-permute-start | bytes 36872 | tf_op jit(solution)/shard_map/ppermute | solution.py:122
  10.6 0.7 broadcast_minimum_fusion
  11.4 0.9 copy.25
  12.3 0.8 fusion.4.pos_ref
  13.1 0.9 fusion.13
  14.2 2.1 %collective-permute-start.3 = (bf16[3,1,48,128]{3,2,1,0:T(8,128)(2,1)S(1)}, bf16[3,1,48,128]{3,2,1,0:T(8,128)(2,1)S(1)}, u32[]{:S(2)}, u32[]{:S(2)}) collective-permute-start(bf16[3,1,48,128]{3,2,1,0:T(8,128)(2,1)S(1)} %constant_dynamic-update-slice_fusion), channel_id=1, source_target_pairs={{1,0},{2,1},{3,2},{4,3},{5,4},{6,5},{7,6},{9,8},{10,9},{11,10},{12... | collective-permute-start | bytes 110600 | tf_op jit(solution)/shard_map/ppermute | solution.py:125
  16.3 3.2 %collective-permute-start.2 = (bf16[3,1,48,128]{3,2,1,0:T(8,128)(2,1)S(1)}, bf16[3,1,48,128]{3,2,1,0:T(8,128)(2,1)S(1)}, u32[]{:S(2)}, u32[]{:S(2)}) collective-permute-start(bf16[3,1,48,128]{3,2,1,0:T(8,128)(2,1)S(1)} %constant_dynamic-update-slice_fusion), channel_id=1, source_target_pairs={{0,1},{1,2},{2,3},{3,4},{4,5},{5,6},{6,7},{8,9},{9,10},{10,11},{11... | collective-permute-start | bytes 110600 | tf_op jit(solution)/shard_map/ppermute | solution.py:122
  19.6 0.9 copy.24
  20.6 1.1 copy.33.w_ref
  21.8 2.9 %scatter_custom_fusion = f32[257,96]{1,0:T(8,128)S(1)} fusion(s32[512]{0:T(512)S(1)} %bitcast.26, f32[512,96]{1,0:T(8,128)S(1)} %reshape.123, f32[]{:T(128)} %constant.72.clone.1), kind=kCustom, calls=%fused_computation.25 | custom fusion | flops 49152 | bytes 98692 | tf_op jit(solution)/shard_map/scatter-add | solution.py:203
  24.9 0.7 pad_maximum_fusion.1.table_ref
  25.7 7.7 %shard_map.93 = f32[256,96]{1,0:T(8,128)} custom-call(s32[256,27]{1,0:T(8,128)} %fusion.4.pos_ref, bf16[768,96]{1,0:T(8,128)(2,1)} %pad_maximum_fusion.1.table_ref, bf16[2592,96]{1,0:T(8,128)(2,1)} %copy.33.w_ref), custom_call_target="tpu_custom_call" | custom-call | tf_op jit(solution)/shard_map/pallas_call | solution.py:168
  33.3 1.6 multiply_convert_fusion
  35.0 1.5 gather_fusion
  36.9 1.0 reshape.109.down_ref
  37.9 99.1 %shard_map.94 = (f32[4096,96]{1,0:T(8,128)}, f32[768,96]{1,0:T(8,128)}) custom-call(s32[256,27]{1,0:T(8,128)} %fusion.4.pos_ref, bf16[768,96]{1,0:T(8,128)(2,1)} %pad_maximum_fusion.1.table_ref, bf16[256,96]{1,0:T(8,128)(2,1)} %get-tuple-element.36.grad_ref, bf16[2592,96]{1,0:T(8,128)(2,1)} %copy.33.w_ref, f32[1024,96]{1,0:T(8,128)} %reshape.109.down_ref), custom_call_target="tpu_custom_call" | custom-call | tf_op jit(solution)/shard_map/pallas_call | solution.py:103
  137.0 0.9 slice_add_fusion
  137.9 1.0 convert.11
  139.1 7.1 %collective-permute-start.4 = (bf16[1,3,48,128]{3,2,1,0:T(8,128)(2,1)S(1)}, bf16[1,3,48,128]{3,2,1,0:T(8,128)(2,1)S(1)}, u32[]{:S(2)}, u32[]{:S(2)}) collective-permute-start(bf16[1,3,48,128]{3,2,1,0:T(8,128)(2,1)S(1)} %slice.94), channel_id=1, source_target_pairs={{0,8},{8,16},{16,24},{24,32},{32,40},{40,48},{48,56},{56,64},{64,7... | collective-permute-start | bytes 110600 | tf_op jit(solution)/shard_map/ppermute | solution.py:122
  146.4 0.2 convert_element_type.22
  146.6 1.9 %collective-permute-start.5 = (bf16[1,3,48,128]{3,2,1,0:T(8,128)(2,1)S(1)}, bf16[1,3,48,128]{3,2,1,0:T(8,128)(2,1)S(1)}, u32[]{:S(2)}, u32[]{:S(2)}) collective-permute-start(bf16[1,3,48,128]{3,2,1,0:T(8,128)(2,1)S(1)} %slice.100), channel_id=1, source_target_pairs={{8,0},{16,8},{24,16},{32,24},{40,32},{48,40},{56,48},{64,56},{72,6... | collective-permute-start | bytes 110600 | tf_op jit(solution)/shard_map/ppermute | solution.py:125
  148.6 6.6 %collective-permute-done.5 = bf16[1,3,48,128]{3,2,1,0:T(8,128)(2,1)S(1)} collective-permute-done((bf16[1,3,48,128]{3,2,1,0:T(8,128)(2,1)S(1)}, bf16[1,3,48,128]{3,2,1,0:T(8,128)(2,1)S(1)}, u32[]{:S(2)}, u32[]{:S(2)}) %collective-permute-start.5) | collective-permute-done | bytes 36896 | tf_op jit(solution)/shard_map/ppermute | solution.py:125
  155.2 2.7 %collective-permute-start.6 = (bf16[5,1,48,128]{3,2,1,0:T(8,128)(2,1)S(1)}, bf16[5,1,48,128]{3,2,1,0:T(8,128)(2,1)S(1)}, u32[]{:S(2)}, u32[]{:S(2)}) collective-permute-start(bf16[5,1,48,128]{3,2,1,0:T(8,128)(2,1)S(1)} %get-tuple-element.32), channel_id=1, source_target_pairs={{0,1},{1,2},{2,3},{3,4},{4,5},{5,6},{6,7},{8,9},{9,10},{10,11},{11... | collective-permute-start | bytes 184328 | tf_op jit(solution)/shard_map/ppermute | solution.py:122
  157.9 2.6 %collective-permute-start.7 = (bf16[5,1,48,128]{3,2,1,0:T(8,128)(2,1)S(1)}, bf16[5,1,48,128]{3,2,1,0:T(8,128)(2,1)S(1)}, u32[]{:S(2)}, u32[]{:S(2)}) collective-permute-start(bf16[5,1,48,128]{3,2,1,0:T(8,128)(2,1)S(1)} %get-tuple-element.33), channel_id=1, source_target_pairs={{1,0},{2,1},{3,2},{4,3},{5,4},{6,5},{7,6},{9,8},{10,9},{11,10},{12... | collective-permute-start | bytes 184328 | tf_op jit(solution)/shard_map/ppermute | solution.py:125
  160.5 0.8 convolution_convert_fusion
  161.3 1.1 slice.106
  162.4 1.4 slice.105
  163.8 1.4 copy.40
  165.2 1.1 reshape.110
  166.9 0.7 copy.39
  (48 shorter events, 2.4 us)
Async XLA Ops:
  0.6 12.5 %copy-start = (bf16[768,128]{1,0:T(8,128)(2,1)S(1)}, bf16[768,128]{1,0:T(8,128)(2,1)}, u32[]{:S(2)}) copy-start(bf16[768,128]{1,0:T(8,128)(2,1)} %param.12) | copy-start | bytes 589828
  0.6 20.0 %copy-start.1 = (bf16[2592,96]{0,1:T(8,128)(2,1)S(1)}, bf16[2592,96]{0,1:T(8,128)(2,1)}, u32[]{:S(2)}) copy-start(bf16[2592,96]{0,1:T(8,128)(2,1)} %param.11) | copy-start | bytes 1492996
  1.7 12.6 %collective-permute-start.1 = (bf16[1,1,48,128]{3,2,1,0:T(8,128)(2,1)S(1)}, bf16[1,1,48,128]{3,2,1,0:T(8,128)(2,1)S(1)}, u32[]{:S(2)}, u32[]{:S(2)}) collective-permute-start(bf16[1,1,48,128]{3,2,1,0:T(8,128)(2,1)S(1)} %reshape.103), channel_id=1, source_target_pairs={{8,0},{16,8},{24,16},{32,24},{40,32},{48,40},{56,48},{64,56},{72,6... | collective-permute-start | bytes 36872 | tf_op jit(solution)/shard_map/ppermute | solution.py:125
  4.3 9.9 %collective-permute-start = (bf16[1,1,48,128]{3,2,1,0:T(8,128)(2,1)S(1)}, bf16[1,1,48,128]{3,2,1,0:T(8,128)(2,1)S(1)}, u32[]{:S(2)}, u32[]{:S(2)}) collective-permute-start(bf16[1,1,48,128]{3,2,1,0:T(8,128)(2,1)S(1)} %reshape.103), channel_id=1, source_target_pairs={{0,8},{8,16},{16,24},{24,32},{32,40},{40,48},{48,56},{56,64},{64,7... | collective-permute-start | bytes 36872 | tf_op jit(solution)/shard_map/ppermute | solution.py:122
  14.2 10.4 %collective-permute-start.3 = (bf16[3,1,48,128]{3,2,1,0:T(8,128)(2,1)S(1)}, bf16[3,1,48,128]{3,2,1,0:T(8,128)(2,1)S(1)}, u32[]{:S(2)}, u32[]{:S(2)}) collective-permute-start(bf16[3,1,48,128]{3,2,1,0:T(8,128)(2,1)S(1)} %constant_dynamic-update-slice_fusion), channel_id=1, source_target_pairs={{1,0},{2,1},{3,2},{4,3},{5,4},{6,5},{7,6},{9,8},{10,9},{11,10},{12... | collective-permute-start | bytes 110600 | tf_op jit(solution)/shard_map/ppermute | solution.py:125
  16.3 8.3 %collective-permute-start.2 = (bf16[3,1,48,128]{3,2,1,0:T(8,128)(2,1)S(1)}, bf16[3,1,48,128]{3,2,1,0:T(8,128)(2,1)S(1)}, u32[]{:S(2)}, u32[]{:S(2)}) collective-permute-start(bf16[3,1,48,128]{3,2,1,0:T(8,128)(2,1)S(1)} %constant_dynamic-update-slice_fusion), channel_id=1, source_target_pairs={{0,1},{1,2},{2,3},{3,4},{4,5},{5,6},{6,7},{8,9},{9,10},{10,11},{11... | collective-permute-start | bytes 110600 | tf_op jit(solution)/shard_map/ppermute | solution.py:122
  24.9 11.8 %copy-start.2 = (bf16[64,128]{1,0:T(8,128)(2,1)S(1)}, bf16[64,128]{1,0:T(8,128)(2,1)}, u32[]{:S(2)}) copy-start(bf16[64,128]{1,0:T(8,128)(2,1)} %param.13) | copy-start | bytes 49156
  139.1 9.5 %collective-permute-start.4 = (bf16[1,3,48,128]{3,2,1,0:T(8,128)(2,1)S(1)}, bf16[1,3,48,128]{3,2,1,0:T(8,128)(2,1)S(1)}, u32[]{:S(2)}, u32[]{:S(2)}) collective-permute-start(bf16[1,3,48,128]{3,2,1,0:T(8,128)(2,1)S(1)} %slice.94), channel_id=1, source_target_pairs={{0,8},{8,16},{16,24},{24,32},{32,40},{40,48},{48,56},{56,64},{64,7... | collective-permute-start | bytes 110600 | tf_op jit(solution)/shard_map/ppermute | solution.py:122
  146.6 8.6 %collective-permute-start.5 = (bf16[1,3,48,128]{3,2,1,0:T(8,128)(2,1)S(1)}, bf16[1,3,48,128]{3,2,1,0:T(8,128)(2,1)S(1)}, u32[]{:S(2)}, u32[]{:S(2)}) collective-permute-start(bf16[1,3,48,128]{3,2,1,0:T(8,128)(2,1)S(1)} %slice.100), channel_id=1, source_target_pairs={{8,0},{16,8},{24,16},{32,24},{40,32},{48,40},{56,48},{64,56},{72,6... | collective-permute-start | bytes 110600 | tf_op jit(solution)/shard_map/ppermute | solution.py:125
  155.2 11.2 %collective-permute-start.6 = (bf16[5,1,48,128]{3,2,1,0:T(8,128)(2,1)S(1)}, bf16[5,1,48,128]{3,2,1,0:T(8,128)(2,1)S(1)}, u32[]{:S(2)}, u32[]{:S(2)}) collective-permute-start(bf16[5,1,48,128]{3,2,1,0:T(8,128)(2,1)S(1)} %get-tuple-element.32), channel_id=1, source_target_pairs={{0,1},{1,2},{2,3},{3,4},{4,5},{5,6},{6,7},{8,9},{9,10},{10,11},{11... | collective-permute-start | bytes 184328 | tf_op jit(solution)/shard_map/ppermute | solution.py:122
  157.9 8.6 %collective-permute-start.7 = (bf16[5,1,48,128]{3,2,1,0:T(8,128)(2,1)S(1)}, bf16[5,1,48,128]{3,2,1,0:T(8,128)(2,1)S(1)}, u32[]{:S(2)}, u32[]{:S(2)}) collective-permute-start(bf16[5,1,48,128]{3,2,1,0:T(8,128)(2,1)S(1)} %get-tuple-element.33), channel_id=1, source_target_pairs={{1,0},{2,1},{3,2},{4,3},{5,4},{6,5},{7,6},{9,8},{10,9},{11,10},{12... | collective-permute-start | bytes 184328 | tf_op jit(solution)/shard_map/ppermute | solution.py:125

commit v5 on v2

--- a/solution.py
+++ b/solution.py
@@ -118,6 +118,60 @@
     return out
 
 
+def _exists(index, size):
+    low = (index + size - 1) // size
+    high = (2 * size - 3 - index) // (size - 1)
+    return (low, 1, high)
+
+
+def halo_kernel(src_ref, out_ref, send_sem, recv_sem):
+    region = lax.axis_index("region")
+    slab = lax.axis_index("slab")
+    along_region = _exists(region, lax.axis_size("region"))
+    along_slab = _exists(slab, lax.axis_size("slab"))
+    codes = [c for c in range(9) if c != 4]
+    slot = {c: i for i, c in enumerate(codes)}
+    out_ref[...] = jnp.zeros(out_ref.shape, out_ref.dtype)
+    barrier = pltpu.get_barrier_semaphore()
+    present = {}
+    for c in codes:
+        present[c] = along_region[c // 3] * along_slab[c % 3]
+        target = (region + c // 3 - 1, slab + c % 3 - 1)
+
+        @pl.when(present[c] == 1)
+        def _():
+            pl.semaphore_signal(barrier, inc=1, device_id=target, device_id_type=MESH)
+    count = (along_region[0] + 1 + along_region[2]) * (along_slab[0] + 1 + along_slab[2]) - 1
+    pl.semaphore_wait(barrier, count)
+    copies = {}
+    for c in codes:
+        target = (region + c // 3 - 1, slab + c % 3 - 1)
+        copies[c] = pltpu.make_async_remote_copy(
+            src_ref=src_ref.at[slot[c]], dst_ref=out_ref.at[slot[8 - c]],
+            send_sem=send_sem.at[slot[c]], recv_sem=recv_sem.at[slot[8 - c]],
+            device_id=target, device_id_type=MESH)
+
+        @pl.when(present[c] == 1)
+        def _():
+            copies[c].start()
+    for c in codes:
+        @pl.when(present[c] == 1)
+        def _():
+            copies[8 - c].wait_recv()
+            copies[c].wait_send()
+
+
+def halo_exchange(src, cid):
+    return pl.pallas_call(
+        halo_kernel,
+        out_shape=jax.ShapeDtypeStruct(src.shape, src.dtype),
+        in_specs=[pl.BlockSpec(memory_space=pltpu.VMEM)],
+        out_specs=pl.BlockSpec(memory_space=pltpu.VMEM),
+        scratch_shapes=[pltpu.SemaphoreType.DMA((8,)), pltpu.SemaphoreType.DMA((8,))],
+        compiler_params=pltpu.CompilerParams(collective_id=cid, has_side_effects=True),
+    )(src)
+
+
 def extended_2(block, sides, width):
     for axis, dim in sides:
         count = lax.axis_size(axis)
@@ -187,9 +241,8 @@
     halo_slot = jnp.where(slot_idx < 4, slot_idx, slot_idx - 1)
     compact = jnp.where(slot_idx == 4, 8 * rim + local_idx, halo_slot * rim + local_idx)
     positions = jnp.where(absent, -1, compact).astype(jnp.int32)
-    sendable = features[:rim].reshape(1, 1, rim * channels // 128, 128)
-    extended = extended_2(sendable, (("region", 0), ("slab", 1)), 1).reshape(9, rim, channels)
-    halo = jnp.concatenate([extended[:4], extended[5:]], axis=0).reshape(8 * rim, channels)
+    sendable = jnp.broadcast_to(features[None, :rim], (8, rim, channels))
+    halo = halo_exchange(sendable, 1).reshape(8 * rim, channels)
     table = jnp.concatenate([halo, features], axis=0)
     table_rows = table.shape[0]
 
@@ -222,14 +275,7 @@
     conv_wgrad, down_wgrad = summed_everywhere([conv_wgrad, down_wgrad])
     own_part = table_grad[8 * rim:]
     halo_grad = table_grad[: 8 * rim].reshape(8, rim, channels)
-    sections = jnp.concatenate(
-        [halo_grad[:4], jnp.zeros((1, rim, channels), jnp.float32), halo_grad[4:]], axis=0)
-    outgoing = sections.reshape(3, 3, rim * channels // 128, 128)
-    returned = extended_2(outgoing.astype(jnp.bfloat16), (("region", 0), ("slab", 1)), 1).astype(
-        outgoing.dtype
-    )
-    returned = returned.reshape(5, 5, rim, channels)
-    incoming = jnp.sum(returned[0::2, 0::2], axis=(0, 1))
+    incoming = jnp.sum(halo_exchange(halo_grad, 2), axis=0)
     grad_input = hidden_grad + own_part
     grad_input = grad_input.at[:rim].add(incoming)
     return (coarse, grad_input, conv_wgrad, down_wgrad)

time: 166 us -> 155 us (0.934)
  starting transfers between devices: 23.5 us -> 0 us
  Pallas kernels: 112 us -> 128 us
  waiting for transfers between devices: 2.84 us -> 0 us
    ppermute x8 -> x0, starting transfers between devices: 23.5 us -> none  [the longest x4 13.8 us: extended_2(): lax.ppermute(lax.slice_in_dim(block, 0, width, axis=dim), axis, backward)]
    pallas_call x0 -> x2, Pallas kernels: none -> 19.5 us  [halo_exchange(): pl.pallas_call(halo_kernel, out_shape=jax.ShapeDtypeStruct(src.shape, src...]
    pallas_call x1, Pallas kernels: 86.4 us -> 83.2 us  [allreduce(): pl.pallas_call(allreduce_kernel, out_shape=jax.ShapeDtypeStruct((rows, 12...]
    ppermute x8 -> x0, waiting for transfers between devices: 2.84 us -> none  [the longest x4 2.83 us: extended_2(): lax.ppermute(lax.slice_in_dim(block, 0, width, axis=dim), axis, backward)]
    unnamed x17 -> x15, local copies, waits for them, and re-layouts: 5.05 us -> 5.02 us
  transfers between devices with their start and end apart: 8 -> 0, of which waited for: 1 -> 0; matrix products, arithmetic and copies ran while one was open for 10% -> 0% of each run, Pallas kernels for 52% -> 0%
where the time goes in v5:
time: 155 us
  Pallas kernels  128 us (83%)
  local copies, waits for them, and re-layouts  12.7 us (8%)
  other arithmetic  11.4 us (7%)
    pallas_call x1, Pallas kernels, allreduce(): pl.pallas_call(allreduce_kernel, out_shape=jax.ShapeDtypeStruct((rows, 12...  83.2 us
    pallas_call x2, Pallas kernels, _vmem_call(): pl.pallas_call(kernel, out_shape=outs, in_specs=[pl.BlockSpec(memory_spac...  25.7 us
    pallas_call x2, Pallas kernels, halo_exchange(): pl.pallas_call(halo_kernel, out_shape=jax.ShapeDtypeStruct(src.shape, src...  19.5 us
    unnamed x15, local copies, waits for them, and re-layouts  5.02 us
    scatter-add x1, other arithmetic, on_device(): hidden_grad.at[down_local.reshape(-1)]  3.48 us

profile of v5, /device:TPU:1, one launch (start us, length us, event | category | flops | bytes accessed | tf_op | source)
XLA Modules:
  0.0 154.6 jit_solution(11599157064308560642)
XLA Ops:
  0.7 0.8 broadcast_minimum_fusion
  1.4 0.7 slice.39
  2.3 0.1 reshape.98
  2.5 0.1 reshape.107
  2.6 0.9 copy.23
  3.6 0.7 broadcast_in_dim.19.src_ref
  4.2 12.7 %shard_map.93 = bf16[8,64,96]{2,1,0:T(8,128)(2,1)} custom-call(bf16[8,64,96]{2,1,0:T(8,128)(2,1)} %broadcast_in_dim.19.src_ref), custom_call_target="tpu_custom_call" | custom-call | tf_op jit(solution)/shard_map/pallas_call | solution.py:165
  16.9 1.6 %pad_maximum_fusion.table_ref = bf16[768,96]{1,0:T(8,128)(2,1)} fusion(bf16[256,96]{1,0:T(8,128)(2,1)S(1)} %copy.23, bf16[512,96]{1,0:T(8,128)(2,1)} %bitcast.14), kind=kLoop, calls=%fused_computation.8 | loop fusion | flops 294912 | bytes 294912 | tf_op jit(solution)/shard_map/concatenate | solution.py:246
  18.5 0.9 copy.24
  19.4 0.8 fusion.5.pos_ref
  20.2 0.2 fusion.10
  20.4 0.1 reshape.117
  20.5 3.5 %scatter_custom_fusion = f32[257,96]{1,0:T(8,128)S(1)} fusion(s32[512]{0:T(512)S(1)} %bitcast.15, f32[512,96]{1,0:T(8,128)S(1)} %reshape.117, f32[]{:T(128)} %constant.72.clone.1), kind=kCustom, calls=%fused_computation.24 | custom fusion | flops 49152 | bytes 98692 | tf_op jit(solution)/shard_map/scatter-add | solution.py:260
  24.0 1.1 copy.32.w_ref
  25.1 7.7 %shard_map.94 = f32[256,96]{1,0:T(8,128)} custom-call(s32[256,27]{1,0:T(8,128)} %fusion.5.pos_ref, bf16[768,96]{1,0:T(8,128)(2,1)} %pad_maximum_fusion.table_ref, bf16[2592,96]{1,0:T(8,128)(2,1)} %copy.32.w_ref), custom_call_target="tpu_custom_call" | custom-call | tf_op jit(solution)/shard_map/pallas_call | solution.py:226
  32.8 1.6 %multiply_convert_fusion = (bf16[256,96]{1,0:T(8,128)(2,1)}, bf16[256,96]{1,0:T(8,128)(2,1)S(1)}) fusion(f32[256,96]{1,0:T(8,128)} %shard_map.94, f32[257,96]{1,0:T(8,128)S(1)} %scatter_custom_fusion, bf16[256,96]{1,0:T(8,128)(2,1)S(1)} %copy.23), kind=kLoop, calls=%fused_computation.19 | loop fusion | flops 319488 | bytes 344064 | tf_op jit(solution)/shard_map/convert_element_type | solution.py:267
  34.4 1.5 gather_fusion
  36.0 0.1 reshape.97
  36.1 0.8 convolution_convert_fusion
  36.9 0.2 convolution_bitcast_fusion
  37.1 18.0 %shard_map.95 = (f32[768,96]{1,0:T(8,128)}, f32[2592,96]{1,0:T(8,128)}) custom-call(s32[256,27]{1,0:T(8,128)} %fusion.5.pos_ref, bf16[768,96]{1,0:T(8,128)(2,1)} %pad_maximum_fusion.table_ref, bf16[256,96]{1,0:T(8,128)(2,1)} %get-tuple-element.28.grad_ref, bf16[2592,96]{1,0:T(8,128)(2,1)} %copy.32.w_ref), custom_call_target="tpu_custom_call" | custom-call | tf_op jit(solution)/shard_map/pallas_call | solution.py:226
  55.1 0.9 slice_add_fusion
  56.0 2.2 %reshape.101 = f32[248832]{0:T(1024)S(1)} reshape(f32[2592,96]{1,0:T(8,128)} %get-tuple-element.19) | data formatting | bytes 1990656 | tf_op jit(solution)/shard_map/reshape | solution.py:109
  58.3 1.3 fusion.x_ref
  59.5 83.2 %shard_map.97 = f32[3072,128]{1,0:T(8,128)} custom-call(f32[3072,128]{1,0:T(8,128)} %fusion.x_ref), custom_call_target="tpu_custom_call" | custom-call | tf_op jit(solution)/shard_map/pallas_call | solution.py:95
  142.8 0.7 slice.43
  143.5 6.9 %shard_map.96 = f32[8,64,96]{2,1,0:T(8,128)} custom-call(f32[8,64,96]{2,1,0:T(8,128)} %bitcast.13), custom_call_target="tpu_custom_call" | custom-call | tf_op jit(solution)/shard_map/pallas_call | solution.py:165
  150.4 1.0 reduce_sum.9
  151.4 0.7 copy.36
  152.1 0.8 slice.45
  152.9 0.3 reshape.104
  153.2 1.4 copy.37
  (19 shorter events, 0.3 us)
Async XLA Ops:
  0.6 19.6 %copy-start = (bf16[768,128]{1,0:T(8,128)(2,1)S(1)}, bf16[768,128]{1,0:T(8,128)(2,1)}, u32[]{:S(2)}) copy-start(bf16[768,128]{1,0:T(8,128)(2,1)} %param.12) | copy-start | bytes 589828
  0.6 19.5 %copy-start.4 = (bf16[64,128]{1,0:T(8,128)(2,1)S(1)}, bf16[64,128]{1,0:T(8,128)(2,1)}, u32[]{:S(2)}) copy-start(bf16[64,128]{1,0:T(8,128)(2,1)} %param.13) | copy-start | bytes 49156
  0.7 23.4 %copy-start.2 = (bf16[2592,96]{0,1:T(8,128)(2,1)S(1)}, bf16[2592,96]{0,1:T(8,128)(2,1)}, u32[]{:S(2)}) copy-start(bf16[2592,96]{0,1:T(8,128)(2,1)} %param.11) | copy-start | bytes 1492996
  59.5 83.2 %copy-start.3 = (f32[768,96]{1,0:T(8,128)S(1)}, f32[768,96]{1,0:T(8,128)}, u32[]{:S(2)}) copy-start(f32[768,96]{1,0:T(8,128)} %get-tuple-element.18) | copy-start | bytes 884740
  142.8 9.3 %copy-start.1 = (f32[3072,128]{1,0:T(8,128)S(1)}, f32[3072,128]{1,0:T(8,128)}, u32[]{:S(2)}) copy-start(f32[3072,128]{1,0:T(8,128)} %shard_map.97) | copy-start | bytes 4718596
  151.3 1.5 slice-start

commit v6 on v5

--- a/solution.py
+++ b/solution.py
@@ -30,10 +30,12 @@
     return va + core * (vb - va), ra + core * (rb - ra), sa + core * (sb - sa)
 
 
-def allreduce_kernel(x_ref, o_ref, *scratch):
+def allreduce_kernel(x_ref, hsrc_ref, o_ref, hout_ref, *scratch):
     HALVES = [x_ref.shape[0] >> (k + 1) for k in range(HALVINGS)]
     recvs = scratch[:9]
     send_sem, recv_sem, free_sem = scratch[9], scratch[10], scratch[11]
+    codes, present, targets, hcopies, hcount = _halo_plan(hsrc_ref, hout_ref, scratch[12], scratch[13])
+    hout_ref[...] = jnp.zeros(hout_ref.shape, hout_ref.dtype)
     region = lax.axis_index("region")
     slab = lax.axis_index("slab")
     core = region % 2
@@ -45,7 +47,9 @@
     barrier = pltpu.get_barrier_semaphore()
     for _, r, s in steps + fulls:
         pl.semaphore_signal(barrier, inc=1, device_id=(r, s), device_id_type=MESH)
-    pl.semaphore_wait(barrier, len(steps) + len(fulls))
+    _halo_signal(barrier, codes, present, targets)
+    pl.semaphore_wait(barrier, len(steps) + len(fulls) + hcount)
+    _halo_start(codes, present, hcopies)
 
     off = 0
     offs = []
@@ -86,36 +90,40 @@
         pl.semaphore_wait(free_sem.at[k], 1)
         copy.start()
         copy.wait()
-
-
-def allreduce(x):
+    _halo_finish(codes, present, hcopies)
+
+
+def allreduce(x, hsrc):
     rows = x.shape[0]
     HALVES = [rows >> (k + 1) for k in range(HALVINGS)]
     n_copies = 9 + 7
     return pl.pallas_call(
         allreduce_kernel,
-        out_shape=jax.ShapeDtypeStruct((rows, 128), jnp.float32),
-        in_specs=[pl.BlockSpec(memory_space=pltpu.VMEM)],
-        out_specs=pl.BlockSpec(memory_space=pltpu.VMEM),
+        out_shape=(jax.ShapeDtypeStruct((rows, 128), jnp.float32),
+                   jax.ShapeDtypeStruct(hsrc.shape, hsrc.dtype)),
+        in_specs=[pl.BlockSpec(memory_space=pltpu.VMEM)] * 2,
+        out_specs=(pl.BlockSpec(memory_space=pltpu.VMEM), pl.BlockSpec(memory_space=pltpu.VMEM)),
         scratch_shapes=[pltpu.VMEM((h, 128), jnp.float32) for h in HALVES]
         + [pltpu.VMEM((HALVES[-1], 128), jnp.float32)] * 2
         + [pltpu.SemaphoreType.DMA((n_copies,)), pltpu.SemaphoreType.DMA((n_copies,))]
-        + [pltpu.SemaphoreType.REGULAR((HALVINGS,))],
+        + [pltpu.SemaphoreType.REGULAR((HALVINGS,))]
+        + [pltpu.SemaphoreType.DMA((8,)), pltpu.SemaphoreType.DMA((8,))],
         compiler_params=pltpu.CompilerParams(collective_id=0, has_side_effects=True),
-    )(x)
-
-
-def summed_everywhere(arrays):
+    )(x, hsrc)
+
+
+def summed_everywhere(arrays, hsrc):
     flat = jnp.concatenate([a.reshape(-1) for a in arrays])
     unit = 128 * 8 << HALVINGS
     rows = -(-flat.size // unit) * unit // 128
     padded = jnp.pad(flat, (0, rows * 128 - flat.size)).reshape(rows, 128)
-    total = allreduce(padded).reshape(-1)
+    total, hout = allreduce(padded, hsrc)
+    total = total.reshape(-1)
     out, at = [], 0
     for a in arrays:
         out.append(total[at:at + a.size].reshape(a.shape))
         at += a.size
-    return out
+    return out, hout
 
 
 def _exists(index, size):
@@ -124,41 +132,55 @@
     return (low, 1, high)
 
 
-def halo_kernel(src_ref, out_ref, send_sem, recv_sem):
+def _halo_plan(src_ref, out_ref, send_sem, recv_sem):
     region = lax.axis_index("region")
     slab = lax.axis_index("slab")
     along_region = _exists(region, lax.axis_size("region"))
     along_slab = _exists(slab, lax.axis_size("slab"))
     codes = [c for c in range(9) if c != 4]
     slot = {c: i for i, c in enumerate(codes)}
-    out_ref[...] = jnp.zeros(out_ref.shape, out_ref.dtype)
-    barrier = pltpu.get_barrier_semaphore()
-    present = {}
+    present, targets, copies = {}, {}, {}
     for c in codes:
         present[c] = along_region[c // 3] * along_slab[c % 3]
-        target = (region + c // 3 - 1, slab + c % 3 - 1)
-
-        @pl.when(present[c] == 1)
-        def _():
-            pl.semaphore_signal(barrier, inc=1, device_id=target, device_id_type=MESH)
-    count = (along_region[0] + 1 + along_region[2]) * (along_slab[0] + 1 + along_slab[2]) - 1
-    pl.semaphore_wait(barrier, count)
-    copies = {}
-    for c in codes:
-        target = (region + c // 3 - 1, slab + c % 3 - 1)
+        targets[c] = (region + c // 3 - 1, slab + c % 3 - 1)
         copies[c] = pltpu.make_async_remote_copy(
             src_ref=src_ref.at[slot[c]], dst_ref=out_ref.at[slot[8 - c]],
             send_sem=send_sem.at[slot[c]], recv_sem=recv_sem.at[slot[8 - c]],
-            device_id=target, device_id_type=MESH)
-
+            device_id=targets[c], device_id_type=MESH)
+    count = (along_region[0] + 1 + along_region[2]) * (along_slab[0] + 1 + along_slab[2]) - 1
+    return codes, present, targets, copies, count
+
+
+def _halo_signal(barrier, codes, present, targets):
+    for c in codes:
+        @pl.when(present[c] == 1)
+        def _():
+            pl.semaphore_signal(barrier, inc=1, device_id=targets[c], device_id_type=MESH)
+
+
+def _halo_start(codes, present, copies):
+    for c in codes:
         @pl.when(present[c] == 1)
         def _():
             copies[c].start()
+
+
+def _halo_finish(codes, present, copies):
     for c in codes:
         @pl.when(present[c] == 1)
         def _():
             copies[8 - c].wait_recv()
             copies[c].wait_send()
+
+
+def halo_kernel(src_ref, out_ref, send_sem, recv_sem):
+    codes, present, targets, copies, count = _halo_plan(src_ref, out_ref, send_sem, recv_sem)
+    out_ref[...] = jnp.zeros(out_ref.shape, out_ref.dtype)
+    barrier = pltpu.get_barrier_semaphore()
+    _halo_signal(barrier, codes, present, targets)
+    pl.semaphore_wait(barrier, count)
+    _halo_start(codes, present, copies)
+    _halo_finish(codes, present, copies)
 
 
 def halo_exchange(src, cid):
@@ -272,10 +294,10 @@
         (jax.ShapeDtypeStruct((table_rows, channels), jnp.float32),
          jax.ShapeDtypeStruct(w_conv.shape, jnp.float32)),
         positions, table, conv_grad, w_conv)
-    conv_wgrad, down_wgrad = summed_everywhere([conv_wgrad, down_wgrad])
+    halo_grad = table_grad[: 8 * rim].reshape(8, rim, channels)
+    (conv_wgrad, down_wgrad), returned = summed_everywhere([conv_wgrad, down_wgrad], halo_grad)
     own_part = table_grad[8 * rim:]
-    halo_grad = table_grad[: 8 * rim].reshape(8, rim, channels)
-    incoming = jnp.sum(halo_exchange(halo_grad, 2), axis=0)
+    incoming = jnp.sum(returned, axis=0)
     grad_input = hidden_grad + own_part
     grad_input = grad_input.at[:rim].add(incoming)
     return (coarse, grad_input, conv_wgrad, down_wgrad)

time: 155 us -> 149 us (0.961)
  Pallas kernels: 128 us -> 120 us
  local copies, waits for them, and re-layouts: 12.7 us -> 15 us
    pallas_call x2 -> x1, Pallas kernels: 19.5 us -> 12.7 us  [halo_exchange(): pl.pallas_call(halo_kernel, out_shape=jax.ShapeDtypeStruct(src.shape, src...]
    slice x3 -> x2, local copies, waits for them, and re-layouts: 0.78 us -> 3.04 us  [summed_everywhere(): out.append(total[at:at + a.size].reshape(a.shape))]
    pallas_call x1, Pallas kernels: 83.2 us -> 81.7 us  [allreduce(): pl.pallas_call(allreduce_kernel, out_shape=(jax.ShapeDtypeStruct((rows, 1...]
    unnamed x15 -> x13, local copies, waits for them, and re-layouts: 5.02 us -> 5.02 us
where the time goes in v6:
time: 149 us
  Pallas kernels  120 us (81%)
  local copies, waits for them, and re-layouts  15 us (10%)
  other arithmetic  11.6 us (8%)
    pallas_call x1, Pallas kernels, allreduce(): pl.pallas_call(allreduce_kernel, out_shape=(jax.ShapeDtypeStruct((rows, 1...  81.7 us
    pallas_call x2, Pallas kernels, _vmem_call(): pl.pallas_call(kernel, out_shape=outs, in_specs=[pl.BlockSpec(memory_spac...  25.7 us
    pallas_call x1, Pallas kernels, halo_exchange(): pl.pallas_call(halo_kernel, out_shape=jax.ShapeDtypeStruct(src.shape, src...  12.7 us
    unnamed x13, local copies, waits for them, and re-layouts  5.02 us
    scatter-add x1, other arithmetic, on_device(): hidden_grad.at[down_local.reshape(-1)]  3.66 us
    slice x2, local copies, waits for them, and re-layouts, summed_everywhere(): out.append(total[at:at + a.size].reshape(a.shape))  3.04 us

profile of v6, /device:TPU:1, one launch (start us, length us, event | category | flops | bytes accessed | tf_op | source)
XLA Modules:
  0.0 148.6 jit_solution(15270171084038772173)
XLA Ops:
  0.7 0.8 broadcast_minimum_fusion
  1.4 0.7 slice.39
  2.3 0.1 reshape.98
  2.5 0.1 reshape.107
  2.6 0.9 copy.23
  3.6 0.7 broadcast_in_dim.19.src_ref
  4.2 12.7 %shard_map.93 = bf16[8,64,96]{2,1,0:T(8,128)(2,1)} custom-call(bf16[8,64,96]{2,1,0:T(8,128)(2,1)} %broadcast_in_dim.19.src_ref), custom_call_target="tpu_custom_call" | custom-call | tf_op jit(solution)/shard_map/pallas_call | solution.py:187
  16.9 1.6 %pad_maximum_fusion.table_ref = bf16[768,96]{1,0:T(8,128)(2,1)} fusion(bf16[256,96]{1,0:T(8,128)(2,1)S(1)} %copy.23, bf16[512,96]{1,0:T(8,128)(2,1)} %bitcast.14), kind=kLoop, calls=%fused_computation.8 | loop fusion | flops 294912 | bytes 294912 | tf_op jit(solution)/shard_map/concatenate | solution.py:268
  18.5 0.9 copy.24
  19.4 0.8 fusion.5.pos_ref
  20.2 0.2 fusion.10
  20.4 0.1 reshape.117
  20.5 3.7 %scatter_custom_fusion = f32[257,96]{1,0:T(8,128)S(1)} fusion(s32[512]{0:T(512)S(1)} %bitcast.15, f32[512,96]{1,0:T(8,128)S(1)} %reshape.117, f32[]{:T(128)} %constant.72.clone.1), kind=kCustom, calls=%fused_computation.24 | custom fusion | flops 49152 | bytes 98692 | tf_op jit(solution)/shard_map/scatter-add | solution.py:282
  24.2 1.1 copy.32.w_ref
  25.3 7.7 %shard_map.94 = f32[256,96]{1,0:T(8,128)} custom-call(s32[256,27]{1,0:T(8,128)} %fusion.5.pos_ref, bf16[768,96]{1,0:T(8,128)(2,1)} %pad_maximum_fusion.table_ref, bf16[2592,96]{1,0:T(8,128)(2,1)} %copy.32.w_ref), custom_call_target="tpu_custom_call" | custom-call | tf_op jit(solution)/shard_map/pallas_call | solution.py:248
  33.0 1.6 %multiply_convert_fusion = (bf16[256,96]{1,0:T(8,128)(2,1)}, bf16[256,96]{1,0:T(8,128)(2,1)S(1)}) fusion(f32[256,96]{1,0:T(8,128)} %shard_map.94, f32[257,96]{1,0:T(8,128)S(1)} %scatter_custom_fusion, bf16[256,96]{1,0:T(8,128)(2,1)S(1)} %copy.23), kind=kLoop, calls=%fused_computation.19 | loop fusion | flops 319488 | bytes 344064 | tf_op jit(solution)/shard_map/convert_element_type | solution.py:289
  34.6 1.5 %gather_fusion = bf16[512,96]{1,0:T(8,128)(2,1)S(1)} fusion(bf16[257,96]{1,0:T(8,128)(2,1)S(1)} %concatenate.12, s32[1024]{0:T(1024)S(1)} %pad_clamp_fusion), kind=kCustom, calls=%fused_computation | custom fusion | bytes 198656 | tf_op jit(solution)/shard_map/gather | solution.py:278
  36.2 0.1 reshape.97
  36.3 0.8 convolution_convert_fusion
  37.1 0.2 convolution_bitcast_fusion
  37.3 18.0 %shard_map.95 = (f32[768,96]{1,0:T(8,128)}, f32[2592,96]{1,0:T(8,128)}) custom-call(s32[256,27]{1,0:T(8,128)} %fusion.5.pos_ref, bf16[768,96]{1,0:T(8,128)(2,1)} %pad_maximum_fusion.table_ref, bf16[256,96]{1,0:T(8,128)(2,1)} %get-tuple-element.32.grad_ref, bf16[2592,96]{1,0:T(8,128)(2,1)} %copy.32.w_ref), custom_call_target="tpu_custom_call" | custom-call | tf_op jit(solution)/shard_map/pallas_call | solution.py:248
  55.3 0.9 slice_add_fusion
  56.2 2.2 %reshape.100 = f32[248832]{0:T(1024)S(1)} reshape(f32[2592,96]{1,0:T(8,128)} %get-tuple-element.21) | data formatting | bytes 1990656 | tf_op jit(solution)/shard_map/reshape | solution.py:116
  58.5 1.3 fusion.x_ref
  59.7 0.7 slice.43
  60.5 81.7 %shard_map.96 = (f32[3072,128]{1,0:T(8,128)}, f32[8,64,96]{2,1,0:T(8,128)}) custom-call(f32[3072,128]{1,0:T(8,128)} %fusion.x_ref, f32[8,64,96]{2,1,0:T(8,128)} %bitcast.13), custom_call_target="tpu_custom_call" | custom-call | tf_op jit(solution)/shard_map/pallas_call | solution.py:100
  142.1 1.0 reduce_sum.9
  143.1 0.7 copy.36
  143.9 1.8 %slice.45 = f32[768,128]{1,0:T(8,128)} slice(f32[3072,128]{1,0:T(8,128)} %get-tuple-element.23), slice={[1944:2712], [0:128]} | slice | bytes 786432 | tf_op jit(solution)/shard_map/slice | solution.py:124
  145.6 1.3 slice.44
  146.9 0.3 reshape.104
  147.3 1.4 copy.37
  (15 shorter events, 0.3 us)
Async XLA Ops:
  0.6 19.6 %copy-start = (bf16[768,128]{1,0:T(8,128)(2,1)S(1)}, bf16[768,128]{1,0:T(8,128)(2,1)}, u32[]{:S(2)}) copy-start(bf16[768,128]{1,0:T(8,128)(2,1)} %param.12) | copy-start | bytes 589828
  0.6 19.5 %copy-start.3 = (bf16[64,128]{1,0:T(8,128)(2,1)S(1)}, bf16[64,128]{1,0:T(8,128)(2,1)}, u32[]{:S(2)}) copy-start(bf16[64,128]{1,0:T(8,128)(2,1)} %param.13) | copy-start | bytes 49156
  0.7 23.5 %copy-start.1 = (bf16[2592,96]{0,1:T(8,128)(2,1)S(1)}, bf16[2592,96]{0,1:T(8,128)(2,1)}, u32[]{:S(2)}) copy-start(bf16[2592,96]{0,1:T(8,128)(2,1)} %param.11) | copy-start | bytes 1492996
  58.5 1.3 copy-start.2

commit v7 on v6

--- a/solution.py
+++ b/solution.py
@@ -224,14 +224,16 @@
     out_ref[...] = total
 
 
-def conv_bwd_kernel(pos_ref, table_ref, grad_ref, w_ref, tgrad_ref, wgrad_ref):
+def conv_bwd_kernel(pos_ref, post_ref, table_ref, grad_ref, w_ref, tgrad_ref, wgrad_ref):
     channels = table_ref.shape[1]
     table = table_ref[...]
     grad = grad_ref[...]
+    rows = table.shape[0]
     back = (((0,), (0,)), ((), ()))
-    total = jnp.zeros(tgrad_ref.shape, jnp.float32)
+    sublanes = lax.broadcasted_iota(jnp.int32, (rows, post_ref.shape[1]), 0)
+    total = jnp.zeros((rows, 2 * channels), jnp.float32)
     for o in range(pos_ref.shape[1]):
-        hot = _one_hot(pos_ref, o, table.shape[0])
+        hot = _one_hot(pos_ref, o, rows)
         picked = jnp.dot(hot, table, preferred_element_type=jnp.float32).astype(jnp.bfloat16)
         wgrad_ref[o * channels:(o + 1) * channels, :] = lax.dot_general(
             picked, grad, back, preferred_element_type=jnp.float32)
@@ -239,9 +241,10 @@
         spread = lax.dot_general(grad, weight, (((1,), (1,)), ((), ())), preferred_element_type=jnp.float32)
         high = spread.astype(jnp.bfloat16)
         low = (spread - high.astype(jnp.float32)).astype(jnp.bfloat16)
-        total = total + lax.dot_general(hot, high, back, preferred_element_type=jnp.float32)
-        total = total + lax.dot_general(hot, low, back, preferred_element_type=jnp.float32)
-    tgrad_ref[...] = total
+        hot_t = (sublanes == post_ref[o:o + 1, :]).astype(jnp.bfloat16)
+        total = total + jnp.dot(hot_t, jnp.concatenate([high, low], axis=1),
+                                preferred_element_type=jnp.float32)
+    tgrad_ref[...] = total[:, :channels] + total[:, channels:]
 
 
 def _vmem_call(kernel, outs, *args):
@@ -293,7 +296,7 @@
         conv_bwd_kernel,
         (jax.ShapeDtypeStruct((table_rows, channels), jnp.float32),
          jax.ShapeDtypeStruct(w_conv.shape, jnp.float32)),
-        positions, table, conv_grad, w_conv)
+        positions, positions.T, table, conv_grad, w_conv)
     halo_grad = table_grad[: 8 * rim].reshape(8, rim, channels)
     (conv_wgrad, down_wgrad), returned = summed_everywhere([conv_wgrad, down_wgrad], halo_grad)
     own_part = table_grad[8 * rim:]

time: 149 us -> 148 us (level)
  Pallas kernels: 120 us -> 116 us
    pallas_call x2, Pallas kernels: 25.7 us -> 20.7 us  [_vmem_call(): pl.pallas_call(kernel, out_shape=outs, in_specs=[pl.BlockSpec(memory_spac...]
    unnamed x13 -> x12, local copies, waits for them, and re-layouts: 5.02 us -> 4.15 us
where the time goes in v7:
time: 148 us; the launch traced here: 147 us
  Pallas kernels  116 us (78%)
  local copies, waits for them, and re-layouts  14.9 us (10%)
  other arithmetic  13 us (9%)
  matrix products  1.9 us (1%)
    pallas_call x1, Pallas kernels, allreduce(): pl.pallas_call(allreduce_kernel, out_shape=(jax.ShapeDtypeStruct((rows, 1...  83 us
    pallas_call x2, Pallas kernels, _vmem_call(): pl.pallas_call(kernel, out_shape=outs, in_specs=[pl.BlockSpec(memory_spac...  20.7 us
    pallas_call x1, Pallas kernels, halo_exchange(): pl.pallas_call(halo_kernel, out_shape=jax.ShapeDtypeStruct(src.shape, src...  12.7 us
    unnamed x12, local copies, waits for them, and re-layouts  4.15 us
    scatter-add x1, other arithmetic, on_device(): hidden_grad.at[down_local.reshape(-1)]  3.64 us
    slice x2, local copies, waits for them, and re-layouts, summed_everywhere(): out.append(total[at:at + a.size].reshape(a.shape))  3.04 us

profile of v7, /device:TPU:1, one launch (start us, length us, event | category | flops | bytes accessed | tf_op | source)
XLA Modules:
  0.0 147.0 jit_solution(10426704322804290770)
XLA Ops:
  0.7 0.8 broadcast_minimum_fusion
  1.4 0.7 slice.39
  2.3 0.1 reshape.98
  2.6 1.4 fusion.17.post_ref
  4.0 0.8 fusion.7
  4.8 0.9 copy.19
  5.7 0.8 copy.22.pos_ref
  6.5 0.7 broadcast_in_dim.19.src_ref
  7.2 12.7 %shard_map.93 = bf16[8,64,96]{2,1,0:T(8,128)(2,1)} custom-call(bf16[8,64,96]{2,1,0:T(8,128)(2,1)} %broadcast_in_dim.19.src_ref), custom_call_target="tpu_custom_call" | custom-call | tf_op jit(solution)/shard_map/pallas_call | solution.py:187
  19.8 1.6 %pad_maximum_fusion.table_ref = bf16[768,96]{1,0:T(8,128)(2,1)} fusion(bf16[256,96]{1,0:T(8,128)(2,1)S(1)} %copy.19, bf16[512,96]{1,0:T(8,128)(2,1)} %bitcast.16), kind=kLoop, calls=%fused_computation.7 | loop fusion | flops 294912 | bytes 294912 | tf_op jit(solution)/shard_map/concatenate | solution.py:271
  21.5 0.9 fusion.10
  22.4 0.1 reshape.117
  22.5 3.6 %scatter_custom_fusion = f32[257,96]{1,0:T(8,128)S(1)} fusion(s32[512]{0:T(512)S(1)} %bitcast.17, f32[512,96]{1,0:T(8,128)S(1)} %reshape.117, f32[]{:T(128)} %constant.72.clone.1), kind=kCustom, calls=%fused_computation.13 | custom fusion | flops 49152 | bytes 98692 | tf_op jit(solution)/shard_map/scatter-add | solution.py:285
  26.2 1.1 copy.23.w_ref
  27.3 7.7 %shard_map.94 = f32[256,96]{1,0:T(8,128)} custom-call(s32[256,27]{1,0:T(8,128)} %copy.22.pos_ref, bf16[768,96]{1,0:T(8,128)(2,1)} %pad_maximum_fusion.table_ref, bf16[2592,96]{1,0:T(8,128)(2,1)} %copy.23.w_ref), custom_call_target="tpu_custom_call" | custom-call | tf_op jit(solution)/shard_map/pallas_call | solution.py:251
  35.0 1.6 %multiply_convert_fusion = (bf16[256,96]{1,0:T(8,128)(2,1)}, bf16[256,96]{1,0:T(8,128)(2,1)S(1)}) fusion(f32[256,96]{1,0:T(8,128)} %shard_map.94, f32[257,96]{1,0:T(8,128)S(1)} %scatter_custom_fusion, bf16[256,96]{1,0:T(8,128)(2,1)S(1)} %copy.19), kind=kLoop, calls=%fused_computation.9 | loop fusion | flops 319488 | bytes 344064 | tf_op jit(solution)/shard_map/convert_element_type | solution.py:292
  36.6 1.5 %gather_fusion = bf16[512,96]{1,0:T(8,128)(2,1)S(1)} fusion(bf16[257,96]{1,0:T(8,128)(2,1)S(1)} %concatenate.12, s32[1024]{0:T(1024)S(1)} %pad_clamp_fusion), kind=kCustom, calls=%fused_computation | custom fusion | bytes 198656 | tf_op jit(solution)/shard_map/gather | solution.py:281
  38.1 0.1 reshape.97
  38.3 0.8 convolution_convert_fusion
  39.1 0.2 convolution_bitcast_fusion
  39.3 13.0 %shard_map.95 = (f32[768,96]{1,0:T(8,128)}, f32[2592,96]{1,0:T(8,128)}) custom-call(s32[256,27]{1,0:T(8,128)} %copy.22.pos_ref, s32[27,256]{1,0:T(8,128)} %fusion.17.post_ref, bf16[768,96]{1,0:T(8,128)(2,1)} %pad_maximum_fusion.table_ref, bf16[256,96]{1,0:T(8,128)(2,1)} %get-tuple-element.32.grad_ref, bf16[2592,96]{1,0:T(8,128)(2,1)} %copy.23.w_ref), custom_call_target="tpu_custom_call" | custom-call | tf_op jit(solution)/shard_map/pallas_call | solution.py:251
  52.3 0.9 slice_add_fusion
  53.2 2.2 %reshape.100 = f32[248832]{0:T(1024)S(1)} reshape(f32[2592,96]{1,0:T(8,128)} %get-tuple-element.21) | data formatting | bytes 1990656 | tf_op jit(solution)/shard_map/reshape | solution.py:116
  55.5 1.3 fusion.x_ref
  56.7 0.7 slice.43
  57.5 83.0 %shard_map.96 = (f32[3072,128]{1,0:T(8,128)}, f32[8,64,96]{2,1,0:T(8,128)}) custom-call(f32[3072,128]{1,0:T(8,128)} %fusion.x_ref, f32[8,64,96]{2,1,0:T(8,128)} %bitcast.15), custom_call_target="tpu_custom_call" | custom-call | tf_op jit(solution)/shard_map/pallas_call | solution.py:100
  140.5 1.0 reduce_sum.9
  141.5 0.7 copy.28
  142.2 1.8 %slice.45 = f32[768,128]{1,0:T(8,128)} slice(f32[3072,128]{1,0:T(8,128)} %get-tuple-element.23), slice={[1944:2712], [0:128]} | slice | bytes 786432 | tf_op jit(solution)/shard_map/slice | solution.py:124
  144.0 1.3 slice.44
  145.2 0.3 reshape.104
  145.6 1.4 copy.29
  (16 shorter events, 0.4 us)
Async XLA Ops:
  0.6 20.8 %copy-start = (bf16[768,128]{1,0:T(8,128)(2,1)S(1)}, bf16[768,128]{1,0:T(8,128)(2,1)}, u32[]{:S(2)}) copy-start(bf16[768,128]{1,0:T(8,128)(2,1)} %param.12) | copy-start | bytes 589828
  0.6 25.5 %copy-start.1 = (bf16[2592,96]{0,1:T(8,128)(2,1)S(1)}, bf16[2592,96]{0,1:T(8,128)(2,1)}, u32[]{:S(2)}) copy-start(bf16[2592,96]{0,1:T(8,128)(2,1)} %param.11) | copy-start | bytes 1492996
  27.3 11.8 %copy-start.3 = (bf16[64,128]{1,0:T(8,128)(2,1)S(1)}, bf16[64,128]{1,0:T(8,128)(2,1)}, u32[]{:S(2)}) copy-start(bf16[64,128]{1,0:T(8,128)(2,1)} %param.13) | copy-start | bytes 49156
  55.4 1.3 copy-start.2

commit v8 on v7

--- a/solution.py
+++ b/solution.py
@@ -224,24 +224,22 @@
     out_ref[...] = total
 
 
-def conv_bwd_kernel(pos_ref, post_ref, table_ref, grad_ref, w_ref, tgrad_ref, wgrad_ref):
-    channels = table_ref.shape[1]
-    table = table_ref[...]
+def conv_bwd_kernel(post_ref, tablet_ref, grad_ref, w_ref, tgrad_ref, wgrad_ref):
+    channels = tablet_ref.shape[0]
+    table_t = tablet_ref[...]
     grad = grad_ref[...]
-    rows = table.shape[0]
-    back = (((0,), (0,)), ((), ()))
+    rows = table_t.shape[1]
     sublanes = lax.broadcasted_iota(jnp.int32, (rows, post_ref.shape[1]), 0)
     total = jnp.zeros((rows, 2 * channels), jnp.float32)
-    for o in range(pos_ref.shape[1]):
-        hot = _one_hot(pos_ref, o, rows)
-        picked = jnp.dot(hot, table, preferred_element_type=jnp.float32).astype(jnp.bfloat16)
-        wgrad_ref[o * channels:(o + 1) * channels, :] = lax.dot_general(
-            picked, grad, back, preferred_element_type=jnp.float32)
+    for o in range(post_ref.shape[0]):
+        hot_t = (sublanes == post_ref[o:o + 1, :]).astype(jnp.bfloat16)
+        picked_t = jnp.dot(table_t, hot_t, preferred_element_type=jnp.float32).astype(jnp.bfloat16)
+        wgrad_ref[o * channels:(o + 1) * channels, :] = jnp.dot(
+            picked_t, grad, preferred_element_type=jnp.float32)
         weight = w_ref[o * channels:(o + 1) * channels, :]
         spread = lax.dot_general(grad, weight, (((1,), (1,)), ((), ())), preferred_element_type=jnp.float32)
         high = spread.astype(jnp.bfloat16)
         low = (spread - high.astype(jnp.float32)).astype(jnp.bfloat16)
-        hot_t = (sublanes == post_ref[o:o + 1, :]).astype(jnp.bfloat16)
         total = total + jnp.dot(hot_t, jnp.concatenate([high, low], axis=1),
                                 preferred_element_type=jnp.float32)
     tgrad_ref[...] = total[:, :channels] + total[:, channels:]
@@ -296,7 +294,7 @@
         conv_bwd_kernel,
         (jax.ShapeDtypeStruct((table_rows, channels), jnp.float32),
          jax.ShapeDtypeStruct(w_conv.shape, jnp.float32)),
-        positions, positions.T, table, conv_grad, w_conv)
+        positions.T, table.T, conv_grad, w_conv)
     halo_grad = table_grad[: 8 * rim].reshape(8, rim, channels)
     (conv_wgrad, down_wgrad), returned = summed_everywhere([conv_wgrad, down_wgrad], halo_grad)
     own_part = table_grad[8 * rim:]

time: 148 us -> 146 us (0.986)
  Pallas kernels: 116 us -> 113 us
  local copies, waits for them, and re-layouts: 14.9 us -> 16.7 us
    pallas_call x2, Pallas kernels: 20.7 us -> 18.9 us  [_vmem_call(): pl.pallas_call(kernel, out_shape=outs, in_specs=[pl.BlockSpec(memory_spac...]
    concatenate x1 -> x0, other arithmetic: 1.64 us -> none  [on_device(): table = jnp.concatenate([halo, features], axis=0)]
    unnamed x12 -> x14, local copies, waits for them, and re-layouts: 4.15 us -> 4.16 us
where the time goes in v8:
time: 146 us; the launch traced here: 145 us
  Pallas kernels  113 us (77%)
  local copies, waits for them, and re-layouts  16.7 us (11%)
  other arithmetic  12.1 us (8%)
  matrix products  1.91 us (1%)
    pallas_call x1, Pallas kernels, allreduce(): pl.pallas_call(allreduce_kernel, out_shape=(jax.ShapeDtypeStruct((rows, 1...  81.7 us
    pallas_call x2, Pallas kernels, _vmem_call(): pl.pallas_call(kernel, out_shape=outs, in_specs=[pl.BlockSpec(memory_spac...  18.9 us
    pallas_call x1, Pallas kernels, halo_exchange(): pl.pallas_call(halo_kernel, out_shape=jax.ShapeDtypeStruct(src.shape, src...  12.7 us
    unnamed x14, local copies, waits for them, and re-layouts  4.16 us
    scatter-add x1, other arithmetic, on_device(): hidden_grad.at[down_local.reshape(-1)]  3.67 us
    slice x2, local copies, waits for them, and re-layouts, summed_everywhere(): out.append(total[at:at + a.size].reshape(a.shape))  3.04 us

profile of v8, /device:TPU:1, one launch (start us, length us, event | category | flops | bytes accessed | tf_op | source)
XLA Modules:
  0.0 144.9 jit_solution(14160315244781500319)
XLA Ops:
  0.7 0.8 broadcast_minimum_fusion
  1.4 0.7 slice.39
  2.6 1.4 fusion.18.post_ref
  4.0 0.8 fusion.7
  4.8 0.9 copy.19
  5.8 0.8 copy.22.pos_ref
  6.5 0.7 broadcast_in_dim.19.src_ref
  7.2 12.7 %shard_map.93 = bf16[8,64,96]{2,1,0:T(8,128)(2,1)} custom-call(bf16[8,64,96]{2,1,0:T(8,128)(2,1)} %broadcast_in_dim.19.src_ref), custom_call_target="tpu_custom_call" | custom-call | tf_op jit(solution)/shard_map/pallas_call | solution.py:187
  19.9 1.0 copy.21
  20.9 0.9 fusion.11
  21.8 0.1 reshape.117
  21.9 3.7 %scatter_custom_fusion = f32[257,96]{1,0:T(8,128)S(1)} fusion(s32[512]{0:T(512)S(1)} %bitcast.19, f32[512,96]{1,0:T(8,128)S(1)} %reshape.117, f32[]{:T(128)} %constant.72.clone.1), kind=kCustom, calls=%fused_computation.13 | custom fusion | flops 49152 | bytes 98692 | tf_op jit(solution)/shard_map/scatter-add | solution.py:283
  25.6 0.7 fusion.10
  26.3 0.8 copy.23.table_ref
  27.1 1.1 copy.24.w_ref
  28.2 7.7 %shard_map.94 = f32[256,96]{1,0:T(8,128)} custom-call(s32[256,27]{1,0:T(8,128)} %copy.22.pos_ref, bf16[768,96]{1,0:T(8,128)(2,1)} %copy.23.table_ref, bf16[2592,96]{1,0:T(8,128)(2,1)} %copy.24.w_ref), custom_call_target="tpu_custom_call" | custom-call | tf_op jit(solution)/shard_map/pallas_call | solution.py:249
  35.9 1.6 %multiply_convert_fusion = (bf16[256,96]{1,0:T(8,128)(2,1)}, bf16[256,96]{1,0:T(8,128)(2,1)S(1)}) fusion(f32[256,96]{1,0:T(8,128)} %shard_map.94, f32[257,96]{1,0:T(8,128)S(1)} %scatter_custom_fusion, bf16[256,96]{1,0:T(8,128)(2,1)S(1)} %copy.19), kind=kLoop, calls=%fused_computation.9 | loop fusion | flops 319488 | bytes 344064 | tf_op jit(solution)/shard_map/convert_element_type | solution.py:290
  37.5 1.5 %gather_fusion = bf16[512,96]{1,0:T(8,128)(2,1)S(1)} fusion(bf16[257,96]{1,0:T(8,128)(2,1)S(1)} %concatenate.12, s32[1024]{0:T(1024)S(1)} %pad_clamp_fusion), kind=kCustom, calls=%fused_computation | custom fusion | bytes 198656 | tf_op jit(solution)/shard_map/gather | solution.py:279
  39.2 0.8 convolution_convert_fusion
  40.0 0.2 convolution_bitcast_fusion
  40.2 11.2 %shard_map.95 = (f32[768,96]{1,0:T(8,128)}, f32[2592,96]{1,0:T(8,128)}) custom-call(s32[27,256]{1,0:T(8,128)} %fusion.18.post_ref, bf16[96,768]{1,0:T(8,128)(2,1)} %get-tuple-element.32.tablet_ref, bf16[256,96]{1,0:T(8,128)(2,1)} %get-tuple-element.34.grad_ref, bf16[2592,96]{1,0:T(8,128)(2,1)} %copy.24.w_ref), custom_call_target="tpu_custom_call" | custom-call | tf_op jit(solution)/shard_map/pallas_call | solution.py:249
  51.5 0.9 slice_add_fusion
  52.4 2.2 %reshape.100 = f32[248832]{0:T(1024)S(1)} reshape(f32[2592,96]{1,0:T(8,128)} %get-tuple-element.21) | data formatting | bytes 1990656 | tf_op jit(solution)/shard_map/reshape | solution.py:116
  54.6 1.3 fusion.x_ref
  55.9 0.7 slice.43
  56.6 81.7 %shard_map.96 = (f32[3072,128]{1,0:T(8,128)}, f32[8,64,96]{2,1,0:T(8,128)}) custom-call(f32[3072,128]{1,0:T(8,128)} %fusion.x_ref, f32[8,64,96]{2,1,0:T(8,128)} %bitcast.17), custom_call_target="tpu_custom_call" | custom-call | tf_op jit(solution)/shard_map/pallas_call | solution.py:100
  138.4 1.0 reduce_sum.9
  139.3 0.7 copy.28
  140.1 1.8 %slice.45 = f32[768,128]{1,0:T(8,128)} slice(f32[3072,128]{1,0:T(8,128)} %get-tuple-element.23), slice={[1944:2712], [0:128]} | slice | bytes 786432 | tf_op jit(solution)/shard_map/slice | solution.py:124
  141.8 1.3 slice.44
  143.1 0.3 reshape.104
  143.5 1.4 copy.29
  (20 shorter events, 0.6 us)
Async XLA Ops:
  0.6 20.2 %copy-start = (bf16[768,128]{1,0:T(8,128)(2,1)S(1)}, bf16[768,128]{1,0:T(8,128)(2,1)}, u32[]{:S(2)}) copy-start(bf16[768,128]{1,0:T(8,128)(2,1)} %param.12) | copy-start | bytes 589828
  0.6 25.0 %copy-start.3 = (bf16[256,96]{0,1:T(8,128)(2,1)S(1)}, bf16[256,96]{0,1:T(8,128)(2,1)}, u32[]{:S(2)}) copy-start(bf16[256,96]{0,1:T(8,128)(2,1)} %param.8) | copy-start | bytes 147460
  0.7 26.5 %copy-start.1 = (bf16[2592,96]{0,1:T(8,128)(2,1)S(1)}, bf16[2592,96]{0,1:T(8,128)(2,1)}, u32[]{:S(2)}) copy-start(bf16[2592,96]{0,1:T(8,128)(2,1)} %param.11) | copy-start | bytes 1492996
  28.2 11.8 %copy-start.4 = (bf16[64,128]{1,0:T(8,128)(2,1)S(1)}, bf16[64,128]{1,0:T(8,128)(2,1)}, u32[]{:S(2)}) copy-start(bf16[64,128]{1,0:T(8,128)(2,1)} %param.13) | copy-start | bytes 49156
  54.6 1.3 copy-start.2

commit v9 on v8

--- a/solution.py
+++ b/solution.py
@@ -245,6 +245,36 @@
     tgrad_ref[...] = total[:, :channels] + total[:, channels:]
 
 
+def down_kernel(down_ref, downt_ref, hidden_ref, hiddent_ref, w_ref, cgrad_ref,
+                coarse_ref, hgrad_ref, wgrad_ref):
+    channels = hidden_ref.shape[1]
+    voxels = hidden_ref.shape[0]
+    coarse_count = down_ref.shape[0]
+    hidden = hidden_ref[...]
+    hidden_t = hiddent_ref[...]
+    cgrad = cgrad_ref[...]
+    lanes = lax.broadcasted_iota(jnp.int32, (coarse_count, voxels), 1)
+    sublanes = lax.broadcasted_iota(jnp.int32, (voxels, coarse_count), 0)
+    coarse = jnp.zeros(coarse_ref.shape, jnp.float32)
+    spread_total = jnp.zeros((voxels, 2 * channels), jnp.float32)
+    for t in range(down_ref.shape[1]):
+        hot = (lanes == down_ref[:, t:t + 1]).astype(jnp.bfloat16)
+        hot_t = (sublanes == downt_ref[t:t + 1, :]).astype(jnp.bfloat16)
+        weight = w_ref[t * channels:(t + 1) * channels, :]
+        picked = jnp.dot(hot, hidden, preferred_element_type=jnp.float32).astype(jnp.bfloat16)
+        coarse = coarse + jnp.dot(picked, weight, preferred_element_type=jnp.float32)
+        picked_t = jnp.dot(hidden_t, hot_t, preferred_element_type=jnp.float32).astype(jnp.bfloat16)
+        wgrad_ref[t * channels:(t + 1) * channels, :] = jnp.dot(
+            picked_t, cgrad, preferred_element_type=jnp.float32)
+        back = lax.dot_general(cgrad, weight, (((1,), (1,)), ((), ())), preferred_element_type=jnp.float32)
+        high = back.astype(jnp.bfloat16)
+        low = (back - high.astype(jnp.float32)).astype(jnp.bfloat16)
+        spread_total = spread_total + jnp.dot(
+            hot_t, jnp.concatenate([high, low], axis=1), preferred_element_type=jnp.float32)
+    coarse_ref[...] = coarse.astype(coarse_ref.dtype)
+    hgrad_ref[...] = spread_total[:, :channels] + spread_total[:, channels:]
+
+
 def _vmem_call(kernel, outs, *args):
     return pl.pallas_call(
         kernel,
@@ -272,20 +302,12 @@
     conv_out = _vmem_call(
         conv_fwd_kernel, jax.ShapeDtypeStruct((voxels, channels), jnp.float32), positions, table, w_conv)
     hidden = (features.astype(jnp.float32) + jax.nn.silu(conv_out)).astype(jnp.bfloat16)
-    zero_row = jnp.zeros((1, channels), features.dtype)
-    coarse_count, taps = down_map.shape
-    down_local = jnp.minimum(down_map, voxels)
-    hidden_pad = jnp.concatenate([hidden, zero_row], axis=0)
-    coarse_rows = hidden_pad[down_local].reshape(coarse_count, taps * channels)
-    coarse = jnp.dot(coarse_rows, w_down, preferred_element_type=jnp.float32).astype(jnp.bfloat16)
-    coarse_back = jnp.dot(coarse_grad, w_down.T, preferred_element_type=jnp.float32)
-    hidden_grad = jnp.zeros((voxels + 1, channels), jnp.float32)
-    hidden_grad = hidden_grad.at[down_local.reshape(-1)].add(coarse_back.reshape(-1, channels))[
-        :voxels
-    ]
-    down_wgrad = lax.dot_general(
-        coarse_rows, coarse_grad, (((0,), (0,)), ((), ())), preferred_element_type=jnp.float32
-    )
+    coarse, hidden_grad, down_wgrad = _vmem_call(
+        down_kernel,
+        (jax.ShapeDtypeStruct((down_map.shape[0], w_down.shape[1]), jnp.bfloat16),
+         jax.ShapeDtypeStruct((voxels, channels), jnp.float32),
+         jax.ShapeDtypeStruct(w_down.shape, jnp.float32)),
+        down_map, down_map.T, hidden, hidden.T, w_down, coarse_grad)
     sigmoid_y = jax.nn.sigmoid(conv_out)
     conv_grad = (hidden_grad * sigmoid_y * (1.0 + conv_out * (1.0 - sigmoid_y))).astype(
         jnp.bfloat16

time: 146 us -> 146 us (level)
  Pallas kernels: 113 us -> 119 us
  other arithmetic: 12.1 us -> 8.56 us
  matrix products: 1.91 us -> 0 us
    pallas_call x2 -> x3, Pallas kernels: 18.9 us -> 23 us  [_vmem_call(): pl.pallas_call(kernel, out_shape=outs, in_specs=[pl.BlockSpec(memory_spac...]
    scatter-add x1 -> x0, other arithmetic: 3.67 us -> none  [on_device(): hidden_grad.at[down_local.reshape(-1)]]
    dot_general x3 -> x0, matrix products: 1.91 us -> none  [the longest x1 0.91 us: on_device(): jnp.dot(coarse_grad, w_down.T, preferred_element_type=jnp.float32)]
    pallas_call x1, Pallas kernels: 81.7 us -> 83.4 us  [allreduce(): pl.pallas_call(allreduce_kernel, out_shape=(jax.ShapeDtypeStruct((rows, 1...]
    gather x1 -> x0, local copies, waits for them, and re-layouts: 1.52 us -> none  [on_device(): coarse_rows = hidden_pad[down_local].reshape(coarse_count, taps * channels)]
    unnamed x14 -> x15, local copies, waits for them, and re-layouts: 4.16 us -> 5.52 us
where the time goes in v9:
time: 146 us; the launch traced here: 145 us
  Pallas kernels  119 us (82%)
  local copies, waits for them, and re-layouts  16.8 us (12%)
  other arithmetic  8.56 us (6%)
    pallas_call x1, Pallas kernels, allreduce(): pl.pallas_call(allreduce_kernel, out_shape=(jax.ShapeDtypeStruct((rows, 1...  83.4 us
    pallas_call x3, Pallas kernels, _vmem_call(): pl.pallas_call(kernel, out_shape=outs, in_specs=[pl.BlockSpec(memory_spac...  23 us
    pallas_call x1, Pallas kernels, halo_exchange(): pl.pallas_call(halo_kernel, out_shape=jax.ShapeDtypeStruct(src.shape, src...  12.7 us
    unnamed x15, local copies, waits for them, and re-layouts  5.52 us
    slice x2, local copies, waits for them, and re-layouts, summed_everywhere(): out.append(total[at:at + a.size].reshape(a.shape))  3.04 us

profile of v9, /device:TPU:1, one launch (start us, length us, event | category | flops | bytes accessed | tf_op | source)
XLA Modules:
  0.0 145.1 jit_solution(8057466111786662097)
XLA Ops:
  0.6 0.8 slice.36
  1.4 0.1 copy.22
  1.5 1.4 fusion.9.post_ref
  3.0 0.8 fusion.5
  3.7 1.4 copy.27.down_ref
  5.1 0.9 copy.21
  6.0 0.8 copy.24.pos_ref
  6.8 0.7 broadcast_in_dim.11.src_ref
  7.5 12.7 %shard_map.93 = bf16[8,64,96]{2,1,0:T(8,128)(2,1)} custom-call(bf16[8,64,96]{2,1,0:T(8,128)(2,1)} %broadcast_in_dim.11.src_ref), custom_call_target="tpu_custom_call" | custom-call | tf_op jit(solution)/shard_map/pallas_call | solution.py:187
  20.1 1.0 copy.23
  21.1 1.5 %fusion.8 = (bf16[96,768]{1,0:T(8,128)(2,1)}, bf16[768,96]{0,1:T(8,128)(2,1)S(1)}) fusion(bf16[256,96]{0,1:T(8,128)(2,1)} %param.8, bf16[512,96]{0,1:T(8,128)(2,1)S(1)} %copy.23), kind=kLoop, calls=%fused_computation.22 | loop fusion | flops 294912 | bytes 442368 | tf_op jit(solution)/shard_map/transpose | solution.py:319
  22.6 0.8 copy.25.table_ref
  23.4 0.0 copy-done.2
  23.4 1.1 copy.26.w_ref
  24.5 7.7 %shard_map.94 = f32[256,96]{1,0:T(8,128)} custom-call(s32[256,27]{1,0:T(8,128)} %copy.24.pos_ref, bf16[768,96]{1,0:T(8,128)(2,1)} %copy.25.table_ref, bf16[2592,96]{1,0:T(8,128)(2,1)} %copy.26.w_ref), custom_call_target="tpu_custom_call" | custom-call | tf_op jit(solution)/shard_map/pallas_call | solution.py:279
  32.2 1.0 add_convert_fusion.hidden_ref
  33.2 0.0 copy-start
  33.2 0.7 copy.28.hiddent_ref
  33.9 0.0 copy-done
  33.9 3.8 %shard_map.95 = (bf16[64,128]{1,0:T(8,128)(2,1)}, f32[256,96]{1,0:T(8,128)}, f32[768,128]{1,0:T(8,128)}) custom-call(s32[64,8]{1,0:T(8,128)} %copy.27.down_ref, s32[8,64]{1,0:T(8,128)} %bitcast.15, bf16[256,96]{1,0:T(8,128)(2,1)} %copy-done, bf16[96,256]{1,0:T(8,128)(2,1)} %copy.28.hiddent_ref, bf16[768,128]{1,0:T(8,128)(2,1)} %w_ref.3, ...), custom_call_target="tpu_custom_call" | custom-call | tf_op jit(solution)/shard_map/pallas_call | solution.py:279
  37.7 1.7 %multiply_convert_fusion.grad_ref = bf16[256,96]{1,0:T(8,128)(2,1)} fusion(f32[256,96]{1,0:T(8,128)} %shard_map.94, f32[256,96]{1,0:T(8,128)} %get-tuple-element.24), kind=kLoop, calls=%fused_computation.5 | loop fusion | flops 221184 | bytes 245760 | tf_op jit(solution)/shard_map/convert_element_type | solution.py:312
  39.4 11.5 %shard_map.96 = (f32[768,96]{1,0:T(8,128)}, f32[2592,96]{1,0:T(8,128)}) custom-call(s32[27,256]{1,0:T(8,128)} %fusion.9.post_ref, bf16[96,768]{1,0:T(8,128)(2,1)} %get-tuple-element.38.tablet_ref, bf16[256,96]{1,0:T(8,128)(2,1)} %multiply_convert_fusion.grad_ref, bf16[2592,96]{1,0:T(8,128)(2,1)} %copy.26.w_ref), custom_call_target="tpu_custom_call" | custom-call | tf_op jit(solution)/shard_map/pallas_call | solution.py:279
  50.9 2.3 %reshape.60 = f32[248832]{0:T(1024)S(1)} reshape(f32[2592,96]{1,0:T(8,128)} %get-tuple-element.26) | data formatting | bytes 1990656 | tf_op jit(solution)/shard_map/reshape | solution.py:116
  53.2 0.7 slice.39
  53.9 1.3 fusion.x_ref
  55.2 83.4 %shard_map.97 = (f32[3072,128]{1,0:T(8,128)}, f32[8,64,96]{2,1,0:T(8,128)}) custom-call(f32[3072,128]{1,0:T(8,128)} %fusion.x_ref, f32[8,64,96]{2,1,0:T(8,128)} %bitcast.11), custom_call_target="tpu_custom_call" | custom-call | tf_op jit(solution)/shard_map/pallas_call | solution.py:100
  138.6 1.0 reduce_sum.9
  139.6 0.7 copy.30
  140.3 1.8 %slice.41 = f32[768,128]{1,0:T(8,128)} slice(f32[3072,128]{1,0:T(8,128)} %get-tuple-element.29), slice={[1944:2712], [0:128]} | slice | bytes 786432 | tf_op jit(solution)/shard_map/slice | solution.py:124
  142.1 1.3 slice.40
  143.4 0.3 reshape.64
  143.7 1.4 copy.31
  (9 shorter events, 0.0 us)
Async XLA Ops:
  0.6 22.8 %copy-start.2 = (bf16[2592,96]{0,1:T(8,128)(2,1)S(1)}, bf16[2592,96]{0,1:T(8,128)(2,1)}, u32[]{:S(2)}) copy-start(bf16[2592,96]{0,1:T(8,128)(2,1)} %param.11) | copy-start | bytes 1492996
  33.2 0.7 copy-start
  39.4 13.8 %copy-start.1 = (f32[256,96]{1,0:T(8,128)S(1)}, f32[256,96]{1,0:T(8,128)}, u32[]{:S(2)}) copy-start(f32[256,96]{1,0:T(8,128)} %get-tuple-element.24) | copy-start | bytes 294916
  50.9 2.3 %copy-start.3 = (f32[768,96]{1,0:T(8,128)S(1)}, f32[768,96]{1,0:T(8,128)}, u32[]{:S(2)}) copy-start(f32[768,96]{1,0:T(8,128)} %get-tuple-element.25) | copy-start | bytes 884740
  50.9 3.1 %copy-start.4 = (f32[768,128]{1,0:T(8,128)S(1)}, f32[768,128]{1,0:T(8,128)}, u32[]{:S(2)}) copy-start(f32[768,128]{1,0:T(8,128)} %get-tuple-element.27) | copy-start | bytes 1179652

commit v10 on v8

--- a/solution.py
+++ b/solution.py
@@ -224,6 +224,33 @@
     out_ref[...] = total
 
 
+def conv_fwd_halo_kernel(pos_ref, own_ref, src_ref, w_ref, out_ref, hout_ref, send_sem, recv_sem):
+    channels = own_ref.shape[1]
+    voxels = own_ref.shape[0]
+    halo_rows = hout_ref.shape[0] * hout_ref.shape[1]
+    codes, present, targets, copies, count = _halo_plan(src_ref, hout_ref, send_sem, recv_sem)
+    hout_ref[...] = jnp.zeros(hout_ref.shape, hout_ref.dtype)
+    barrier = pltpu.get_barrier_semaphore()
+    _halo_signal(barrier, codes, present, targets)
+    pl.semaphore_wait(barrier, count)
+    _halo_start(codes, present, copies)
+    own = own_ref[...]
+    own_lanes = lax.broadcasted_iota(jnp.int32, (pos_ref.shape[0], voxels), 1) + halo_rows
+    total = jnp.zeros(out_ref.shape, jnp.float32)
+    for o in range(pos_ref.shape[1]):
+        hot = (pos_ref[:, o:o + 1] == own_lanes).astype(jnp.bfloat16)
+        picked = jnp.dot(hot, own, preferred_element_type=jnp.float32)
+        weight = w_ref[o * channels:(o + 1) * channels, :]
+        total = total + jnp.dot(picked.astype(jnp.bfloat16), weight, preferred_element_type=jnp.float32)
+    _halo_finish(codes, present, copies)
+    halo = hout_ref[...].reshape(halo_rows, channels)
+    for o in range(pos_ref.shape[1]):
+        picked = jnp.dot(_one_hot(pos_ref, o, halo_rows), halo, preferred_element_type=jnp.float32)
+        weight = w_ref[o * channels:(o + 1) * channels, :]
+        total = total + jnp.dot(picked.astype(jnp.bfloat16), weight, preferred_element_type=jnp.float32)
+    out_ref[...] = total
+
+
 def conv_bwd_kernel(post_ref, tablet_ref, grad_ref, w_ref, tgrad_ref, wgrad_ref):
     channels = tablet_ref.shape[0]
     table_t = tablet_ref[...]
@@ -265,12 +292,17 @@
     compact = jnp.where(slot_idx == 4, 8 * rim + local_idx, halo_slot * rim + local_idx)
     positions = jnp.where(absent, -1, compact).astype(jnp.int32)
     sendable = jnp.broadcast_to(features[None, :rim], (8, rim, channels))
-    halo = halo_exchange(sendable, 1).reshape(8 * rim, channels)
-    table = jnp.concatenate([halo, features], axis=0)
+    conv_out, halo = pl.pallas_call(
+        conv_fwd_halo_kernel,
+        out_shape=(jax.ShapeDtypeStruct((voxels, channels), jnp.float32),
+                   jax.ShapeDtypeStruct(sendable.shape, sendable.dtype)),
+        in_specs=[pl.BlockSpec(memory_space=pltpu.VMEM)] * 4,
+        out_specs=(pl.BlockSpec(memory_space=pltpu.VMEM), pl.BlockSpec(memory_space=pltpu.VMEM)),
+        scratch_shapes=[pltpu.SemaphoreType.DMA((8,)), pltpu.SemaphoreType.DMA((8,))],
+        compiler_params=pltpu.CompilerParams(collective_id=1, has_side_effects=True),
+    )(positions, features, sendable, w_conv)
+    table = jnp.concatenate([halo.reshape(8 * rim, channels), features], axis=0)
     table_rows = table.shape[0]
-
-    conv_out = _vmem_call(
-        conv_fwd_kernel, jax.ShapeDtypeStruct((voxels, channels), jnp.float32), positions, table, w_conv)
     hidden = (features.astype(jnp.float32) + jax.nn.silu(conv_out)).astype(jnp.bfloat16)
     zero_row = jnp.zeros((1, channels), features.dtype)
     coarse_count, taps = down_map.shape

time: 146 us -> 142 us (0.973)
  Pallas kernels: 113 us -> 111 us
    pallas_call x2 -> x1, Pallas kernels: 18.9 us -> 11.2 us  [_vmem_call(): pl.pallas_call(kernel, out_shape=outs, in_specs=[pl.BlockSpec(memory_spac...]
    pallas_call x1, Pallas kernels: 12.7 us -> 16.4 us  [on_device(): pl.pallas_call(conv_fwd_halo_kernel, out_shape=(jax.ShapeDtypeStruct((vox...]
    unnamed x14 -> x16, local copies, waits for them, and re-layouts: 4.16 us -> 4.79 us
where the time goes in v10:
time: 142 us
  Pallas kernels  111 us (78%)
  local copies, waits for them, and re-layouts  16.5 us (12%)
  other arithmetic  11.8 us (8%)
  matrix products  1.94 us (1%)
    pallas_call x1, Pallas kernels, allreduce(): pl.pallas_call(allreduce_kernel, out_shape=(jax.ShapeDtypeStruct((rows, 1...  82.9 us
    pallas_call x1, Pallas kernels, on_device(): pl.pallas_call(conv_fwd_halo_kernel, out_shape=(jax.ShapeDtypeStruct((vox...  16.4 us
    pallas_call x1, Pallas kernels, _vmem_call(): pl.pallas_call(kernel, out_shape=outs, in_specs=[pl.BlockSpec(memory_spac...  11.2 us
    unnamed x16, local copies, waits for them, and re-layouts  4.79 us
    scatter-add x1, other arithmetic, on_device(): hidden_grad.at[down_local.reshape(-1)]  3.4 us
    slice x2, local copies, waits for them, and re-layouts, summed_everywhere(): out.append(total[at:at + a.size].reshape(a.shape))  3.04 us

profile of v10, /device:TPU:1, one launch (start us, length us, event | category | flops | bytes accessed | tf_op | source)
XLA Modules:
  0.0 141.6 jit_solution(6703931338241734616)
XLA Ops:
  0.7 0.8 broadcast_minimum_fusion
  1.4 0.7 slice.39
  2.3 0.1 reshape.97
  2.6 1.4 fusion.17.post_ref
  4.0 0.8 fusion.7
  4.8 1.5 %copy.19.own_ref = bf16[256,96]{1,0:T(8,128)(2,1)} copy(bf16[256,96]{0,1:T(8,128)(2,1)} %param.8) | data formatting | bytes 98304 | tf_op args[0]
  6.4 0.8 copy.21.pos_ref
  7.1 0.7 broadcast_in_dim.19.src_ref
  7.8 0.9 fusion.10
  8.7 0.1 reshape.117
  8.9 3.4 %scatter_custom_fusion = f32[257,96]{1,0:T(8,128)S(1)} fusion(s32[512]{0:T(512)S(1)} %bitcast.19, f32[512,96]{1,0:T(8,128)S(1)} %reshape.117, f32[]{:T(128)} %constant.72.clone.1), kind=kCustom, calls=%fused_computation.13 | custom fusion | flops 49152 | bytes 98692 | tf_op jit(solution)/shard_map/scatter-add | solution.py:315
  12.3 1.1 copy.23.w_ref
  13.4 16.4 %shard_map.93 = (f32[256,96]{1,0:T(8,128)}, bf16[8,64,96]{2,1,0:T(8,128)(2,1)}) custom-call(s32[256,27]{1,0:T(8,128)} %copy.21.pos_ref, bf16[256,96]{1,0:T(8,128)(2,1)} %copy.19.own_ref, bf16[8,64,96]{2,1,0:T(8,128)(2,1)} %broadcast_in_dim.19.src_ref, bf16[2592,96]{1,0:T(8,128)(2,1)} %copy.23.w_ref), custom_call_target="tpu_custom_call" | custom-call | tf_op jit(solution)/shard_map/pallas_call | solution.py:295
  29.9 1.6 %multiply_convert_fusion = (bf16[256,96]{1,0:T(8,128)(2,1)}, bf16[256,96]{1,0:T(8,128)(2,1)S(1)}) fusion(f32[256,96]{1,0:T(8,128)} %get-tuple-element.22, f32[257,96]{1,0:T(8,128)S(1)} %scatter_custom_fusion, bf16[256,96]{1,0:T(8,128)(2,1)S(1)} %copy-done.1), kind=kLoop, calls=%fused_computation.9 | loop fusion | flops 319488 | bytes 344064 | tf_op jit(solution)/shard_map/convert_element_type | solution.py:322
  31.5 1.0 copy.26
  32.5 0.7 maximum_bitcast_fusion.tablet_ref
  33.2 1.5 %gather_fusion = bf16[512,96]{1,0:T(8,128)(2,1)S(1)} fusion(bf16[257,96]{1,0:T(8,128)(2,1)S(1)} %concatenate.11, s32[1024]{0:T(1024)S(1)} %pad_clamp_fusion), kind=kCustom, calls=%fused_computation | custom fusion | bytes 198656 | tf_op jit(solution)/shard_map/gather | solution.py:311
  34.7 0.1 reshape.96
  34.8 0.8 convolution_convert_fusion
  35.6 0.2 convolution_bitcast_fusion
  35.9 11.2 %shard_map.94 = (f32[768,96]{1,0:T(8,128)}, f32[2592,96]{1,0:T(8,128)}) custom-call(s32[27,256]{1,0:T(8,128)} %fusion.17.post_ref, bf16[96,768]{1,0:T(8,128)(2,1)} %maximum_bitcast_fusion.tablet_ref, bf16[256,96]{1,0:T(8,128)(2,1)} %get-tuple-element.36.grad_ref, bf16[2592,96]{1,0:T(8,128)(2,1)} %copy.23.w_ref), custom_call_target="tpu_custom_call" | custom-call | tf_op jit(solution)/shard_map/pallas_call | solution.py:276
  47.1 0.9 slice_add_fusion
  48.0 2.2 %reshape.100 = f32[248832]{0:T(1024)S(1)} reshape(f32[2592,96]{1,0:T(8,128)} %get-tuple-element.25) | data formatting | bytes 1990656 | tf_op jit(solution)/shard_map/reshape | solution.py:116
  50.3 1.3 fusion.x_ref
  51.5 0.7 slice.43
  52.2 82.9 %shard_map.95 = (f32[3072,128]{1,0:T(8,128)}, f32[8,64,96]{2,1,0:T(8,128)}) custom-call(f32[3072,128]{1,0:T(8,128)} %fusion.x_ref, f32[8,64,96]{2,1,0:T(8,128)} %bitcast.17), custom_call_target="tpu_custom_call" | custom-call | tf_op jit(solution)/shard_map/pallas_call | solution.py:100
  135.1 1.0 reduce_sum.9
  136.1 0.7 copy.28
  136.8 1.8 %slice.45 = f32[768,128]{1,0:T(8,128)} slice(f32[3072,128]{1,0:T(8,128)} %get-tuple-element.27), slice={[1944:2712], [0:128]} | slice | bytes 786432 | tf_op jit(solution)/shard_map/slice | solution.py:124
  138.6 1.3 slice.44
  139.9 0.3 reshape.104
  140.2 1.4 copy.29
  (20 shorter events, 0.4 us)
Async XLA Ops:
  0.6 7.2 %copy-start = (bf16[768,128]{1,0:T(8,128)(2,1)S(1)}, bf16[768,128]{1,0:T(8,128)(2,1)}, u32[]{:S(2)}) copy-start(bf16[768,128]{1,0:T(8,128)(2,1)} %param.12) | copy-start | bytes 589828
  0.6 11.7 %copy-start.2 = (bf16[2592,96]{0,1:T(8,128)(2,1)S(1)}, bf16[2592,96]{0,1:T(8,128)(2,1)}, u32[]{:S(2)}) copy-start(bf16[2592,96]{0,1:T(8,128)(2,1)} %param.11) | copy-start | bytes 1492996
  7.8 22.1 %copy-start.1 = (bf16[256,96]{1,0:T(8,128)(2,1)S(1)}, bf16[256,96]{1,0:T(8,128)(2,1)}, u32[]{:S(2)}) copy-start(bf16[256,96]{1,0:T(8,128)(2,1)} %copy.19.own_ref) | copy-start | bytes 147460
  8.9 23.6 %copy-start.4 = (bf16[256,96]{0,1:T(8,128)(2,1)S(1)}, bf16[256,96]{0,1:T(8,128)(2,1)}, u32[]{:S(2)}) copy-start(bf16[256,96]{0,1:T(8,128)(2,1)} %param.8) | copy-start | bytes 147460
  29.8 5.8 %copy-start.5 = (bf16[64,128]{1,0:T(8,128)(2,1)S(1)}, bf16[64,128]{1,0:T(8,128)(2,1)}, u32[]{:S(2)}) copy-start(bf16[64,128]{1,0:T(8,128)(2,1)} %param.13) | copy-start | bytes 49156
  50.2 1.3 copy-start.3

commit v11 on v10

--- a/solution.py
+++ b/solution.py
@@ -99,12 +99,12 @@
     n_copies = 9 + 7
     return pl.pallas_call(
         allreduce_kernel,
-        out_shape=(jax.ShapeDtypeStruct((rows, 128), jnp.float32),
+        out_shape=(jax.ShapeDtypeStruct((rows, x.shape[1]), jnp.float32),
                    jax.ShapeDtypeStruct(hsrc.shape, hsrc.dtype)),
         in_specs=[pl.BlockSpec(memory_space=pltpu.VMEM)] * 2,
         out_specs=(pl.BlockSpec(memory_space=pltpu.VMEM), pl.BlockSpec(memory_space=pltpu.VMEM)),
-        scratch_shapes=[pltpu.VMEM((h, 128), jnp.float32) for h in HALVES]
-        + [pltpu.VMEM((HALVES[-1], 128), jnp.float32)] * 2
+        scratch_shapes=[pltpu.VMEM((h, x.shape[1]), jnp.float32) for h in HALVES]
+        + [pltpu.VMEM((HALVES[-1], x.shape[1]), jnp.float32)] * 2
         + [pltpu.SemaphoreType.DMA((n_copies,)), pltpu.SemaphoreType.DMA((n_copies,))]
         + [pltpu.SemaphoreType.REGULAR((HALVINGS,))]
         + [pltpu.SemaphoreType.DMA((8,)), pltpu.SemaphoreType.DMA((8,))],
@@ -113,18 +113,18 @@
 
 
 def summed_everywhere(arrays, hsrc):
-    flat = jnp.concatenate([a.reshape(-1) for a in arrays])
-    unit = 128 * 8 << HALVINGS
-    rows = -(-flat.size // unit) * unit // 128
-    padded = jnp.pad(flat, (0, rows * 128 - flat.size)).reshape(rows, 128)
+    width = arrays[0].shape[1]
+    parts = [a.reshape(-1, width) for a in arrays]
+    unit = 8 << HALVINGS
+    used = sum(p.shape[0] for p in parts)
+    rows = -(-used // unit) * unit
+    padded = jnp.concatenate(parts + [jnp.zeros((rows - used, width), jnp.float32)], axis=0)
     total, hout = allreduce(padded, hsrc)
-    total = total.reshape(-1)
     out, at = [], 0
-    for a in arrays:
-        out.append(total[at:at + a.size].reshape(a.shape))
-        at += a.size
+    for a, p in zip(arrays, parts):
+        out.append(total[at:at + p.shape[0]].reshape(a.shape))
+        at += p.shape[0]
     return out, hout
-
 
 def _exists(index, size):
     low = (index + size - 1) // size

time: 142 us -> 155 us (1.092)
  Pallas kernels: 111 us -> 123 us
  local copies, waits for them, and re-layouts: 16.5 us -> 14.7 us
    pallas_call x1, Pallas kernels: 82.9 us -> 93.9 us  [allreduce(): pl.pallas_call(allreduce_kernel, out_shape=(jax.ShapeDtypeStruct((rows, x...]
    concatenate x0 -> x1, other arithmetic: none -> 3.27 us  [summed_everywhere(): jnp.concatenate(parts + [jnp.zeros((rows - used, width), jnp.float32)], a...]
    pallas_call x1, Pallas kernels: 16.4 us -> 18.2 us  [on_device(): pl.pallas_call(conv_fwd_halo_kernel, out_shape=(jax.ShapeDtypeStruct((vox...]
where the time goes in v11:
time: 155 us; the launch traced here: 154 us
  Pallas kernels  123 us (79%)
  local copies, waits for them, and re-layouts  14.7 us (9%)
  other arithmetic  13.3 us (9%)
  matrix products  1.91 us (1%)
    pallas_call x1, Pallas kernels, allreduce(): pl.pallas_call(allreduce_kernel, out_shape=(jax.ShapeDtypeStruct((rows, x...  93.9 us
    pallas_call x1, Pallas kernels, on_device(): pl.pallas_call(conv_fwd_halo_kernel, out_shape=(jax.ShapeDtypeStruct((vox...  18.2 us
    pallas_call x1, Pallas kernels, _vmem_call(): pl.pallas_call(kernel, out_shape=outs, in_specs=[pl.BlockSpec(memory_spac...  11.2 us
    unnamed x16, local copies, waits for them, and re-layouts  4.78 us
    concatenate x1, other arithmetic, summed_everywhere(): jnp.concatenate(parts + [jnp.zeros((rows - used, width), jnp.float32)], a...  3.27 us

profile of v11, /device:TPU:1, one launch (start us, length us, event | category | flops | bytes accessed | tf_op | source)
XLA Modules:
  0.0 154.1 jit_solution(18432436169891839040)
XLA Ops:
  0.7 0.8 broadcast_minimum_fusion
  1.5 0.7 slice.37
  2.4 0.1 reshape.85
  2.7 1.4 fusion.17.post_ref
  4.1 0.8 fusion.6
  4.9 1.5 copy.19.own_ref
  6.4 0.8 copy.21.pos_ref
  7.2 0.7 broadcast_in_dim.22.src_ref
  7.9 0.9 fusion.9
  8.8 0.1 reshape.103
  8.9 2.8 %scatter_custom_fusion = f32[257,96]{1,0:T(8,128)S(1)} fusion(s32[512]{0:T(512)S(1)} %bitcast.15, f32[512,96]{1,0:T(8,128)S(1)} %reshape.103, f32[]{:T(128)} %constant.71.clone.1), kind=kCustom, calls=%fused_computation.10 | custom fusion | flops 49152 | bytes 98692 | tf_op jit(solution)/shard_map/scatter-add | solution.py:315
  11.8 1.1 copy.23.w_ref
  12.9 18.2 %shard_map.93 = (f32[256,96]{1,0:T(8,128)}, bf16[8,64,96]{2,1,0:T(8,128)(2,1)}) custom-call(s32[256,27]{1,0:T(8,128)} %copy.21.pos_ref, bf16[256,96]{1,0:T(8,128)(2,1)} %copy.19.own_ref, bf16[8,64,96]{2,1,0:T(8,128)(2,1)} %broadcast_in_dim.22.src_ref, bf16[2592,96]{1,0:T(8,128)(2,1)} %copy.23.w_ref), custom_call_target="tpu_custom_call" | custom-call | tf_op jit(solution)/shard_map/pallas_call | solution.py:295
  31.1 1.6 %multiply_convert_fusion = (bf16[256,96]{1,0:T(8,128)(2,1)}, bf16[256,96]{1,0:T(8,128)(2,1)S(1)}) fusion(f32[256,96]{1,0:T(8,128)} %get-tuple-element.22, f32[257,96]{1,0:T(8,128)S(1)} %scatter_custom_fusion, bf16[256,96]{1,0:T(8,128)(2,1)S(1)} %copy-done.1), kind=kLoop, calls=%fused_computation.6 | loop fusion | flops 319488 | bytes 344064 | tf_op jit(solution)/shard_map/convert_element_type | solution.py:322
  32.7 1.0 copy.26
  33.8 0.7 maximum_bitcast_fusion.tablet_ref
  34.4 1.5 gather_fusion
  36.0 0.1 reshape.84
  36.1 0.8 convolution_convert_fusion
  36.9 0.2 fusion.10
  37.1 0.2 reshape.88
  37.3 11.2 %shard_map.94 = (f32[768,96]{1,0:T(8,128)}, f32[2592,96]{1,0:T(8,128)}) custom-call(s32[27,256]{1,0:T(8,128)} %fusion.17.post_ref, bf16[96,768]{1,0:T(8,128)(2,1)} %maximum_bitcast_fusion.tablet_ref, bf16[256,96]{1,0:T(8,128)(2,1)} %get-tuple-element.36.grad_ref, bf16[2592,96]{1,0:T(8,128)(2,1)} %copy.23.w_ref), custom_call_target="tpu_custom_call" | custom-call | tf_op jit(solution)/shard_map/pallas_call | solution.py:276
  48.5 1.0 slice_add_fusion
  49.5 3.3 %maximum_maximum_fusion.x_ref = f32[4096,96]{1,0:T(8,128)} fusion(f32[1024,96]{1,0:T(8,128)S(1)} %reshape.88, f32[2592,96]{1,0:T(8,128)} %get-tuple-element.25, f32[4096]{0:T(1024)S(1)} %pad.5.clone), kind=kLoop, calls=%fused_computation.2 | loop fusion | flops 786432 | bytes 2977792 | tf_op jit(solution)/shard_map/concatenate | solution.py:121
  52.8 0.7 slice.41
  53.5 93.9 %shard_map.95 = (f32[4096,96]{1,0:T(8,128)}, f32[8,64,96]{2,1,0:T(8,128)}) custom-call(f32[4096,96]{1,0:T(8,128)} %maximum_maximum_fusion.x_ref, f32[8,64,96]{2,1,0:T(8,128)} %bitcast.13), custom_call_target="tpu_custom_call" | custom-call | tf_op jit(solution)/shard_map/pallas_call | solution.py:100
  147.4 1.0 reduce_sum.9
  148.4 0.7 copy.28
  149.2 1.1 slice.43
  150.3 1.4 slice.42
  151.7 1.4 copy.29
  153.1 1.1 reshape.90
  (22 shorter events, 0.5 us)
Async XLA Ops:
  0.6 7.2 %copy-start = (bf16[768,128]{1,0:T(8,128)(2,1)S(1)}, bf16[768,128]{1,0:T(8,128)(2,1)}, u32[]{:S(2)}) copy-start(bf16[768,128]{1,0:T(8,128)(2,1)} %param.12) | copy-start | bytes 589828
  0.6 11.1 %copy-start.2 = (bf16[2592,96]{0,1:T(8,128)(2,1)S(1)}, bf16[2592,96]{0,1:T(8,128)(2,1)}, u32[]{:S(2)}) copy-start(bf16[2592,96]{0,1:T(8,128)(2,1)} %param.11) | copy-start | bytes 1492996
  6.4 24.7 %copy-start.1 = (bf16[256,96]{1,0:T(8,128)(2,1)S(1)}, bf16[256,96]{1,0:T(8,128)(2,1)}, u32[]{:S(2)}) copy-start(bf16[256,96]{1,0:T(8,128)(2,1)} %copy.19.own_ref) | copy-start | bytes 147460
  6.4 27.3 %copy-start.4 = (bf16[256,96]{0,1:T(8,128)(2,1)S(1)}, bf16[256,96]{0,1:T(8,128)(2,1)}, u32[]{:S(2)}) copy-start(bf16[256,96]{0,1:T(8,128)(2,1)} %param.8) | copy-start | bytes 147460
  12.9 24.0 %copy-start.5 = (bf16[64,128]{1,0:T(8,128)(2,1)S(1)}, bf16[64,128]{1,0:T(8,128)(2,1)}, u32[]{:S(2)}) copy-start(bf16[64,128]{1,0:T(8,128)(2,1)} %param.13) | copy-start | bytes 49156
  48.5 4.3 %copy-start.3 = (f32[768,96]{1,0:T(8,128)S(1)}, f32[768,96]{1,0:T(8,128)}, u32[]{:S(2)}) copy-start(f32[768,96]{1,0:T(8,128)} %get-tuple-element.24) | copy-start | bytes 884740

commit v12 on v10

--- a/solution.py
+++ b/solution.py
@@ -30,7 +30,7 @@
     return va + core * (vb - va), ra + core * (rb - ra), sa + core * (sb - sa)
 
 
-def allreduce_kernel(x_ref, hsrc_ref, o_ref, hout_ref, *scratch):
+def allreduce_kernel(x_ref, post_ref, grad_ref, w_ref, o_ref, hsrc_ref, own_ref, hout_ref, *scratch):
     HALVES = [x_ref.shape[0] >> (k + 1) for k in range(HALVINGS)]
     recvs = scratch[:9]
     send_sem, recv_sem, free_sem = scratch[9], scratch[10], scratch[11]
@@ -48,6 +48,7 @@
     for _, r, s in steps + fulls:
         pl.semaphore_signal(barrier, inc=1, device_id=(r, s), device_id_type=MESH)
     _halo_signal(barrier, codes, present, targets)
+    conv_scatter_body(post_ref, grad_ref, w_ref, hsrc_ref, own_ref)
     pl.semaphore_wait(barrier, len(steps) + len(fulls) + hcount)
     _halo_start(codes, present, hcopies)
 
@@ -93,37 +94,39 @@
     _halo_finish(codes, present, hcopies)
 
 
-def allreduce(x, hsrc):
+def allreduce(x, post, grad, w, hshape, own_rows):
     rows = x.shape[0]
     HALVES = [rows >> (k + 1) for k in range(HALVINGS)]
     n_copies = 9 + 7
     return pl.pallas_call(
         allreduce_kernel,
         out_shape=(jax.ShapeDtypeStruct((rows, 128), jnp.float32),
-                   jax.ShapeDtypeStruct(hsrc.shape, hsrc.dtype)),
-        in_specs=[pl.BlockSpec(memory_space=pltpu.VMEM)] * 2,
-        out_specs=(pl.BlockSpec(memory_space=pltpu.VMEM), pl.BlockSpec(memory_space=pltpu.VMEM)),
+                   jax.ShapeDtypeStruct(hshape, jnp.float32),
+                   jax.ShapeDtypeStruct((own_rows, hshape[2]), jnp.float32),
+                   jax.ShapeDtypeStruct(hshape, jnp.float32)),
+        in_specs=[pl.BlockSpec(memory_space=pltpu.VMEM)] * 4,
+        out_specs=tuple(pl.BlockSpec(memory_space=pltpu.VMEM) for _ in range(4)),
         scratch_shapes=[pltpu.VMEM((h, 128), jnp.float32) for h in HALVES]
         + [pltpu.VMEM((HALVES[-1], 128), jnp.float32)] * 2
         + [pltpu.SemaphoreType.DMA((n_copies,)), pltpu.SemaphoreType.DMA((n_copies,))]
         + [pltpu.SemaphoreType.REGULAR((HALVINGS,))]
         + [pltpu.SemaphoreType.DMA((8,)), pltpu.SemaphoreType.DMA((8,))],
         compiler_params=pltpu.CompilerParams(collective_id=0, has_side_effects=True),
-    )(x, hsrc)
-
-
-def summed_everywhere(arrays, hsrc):
+    )(x, post, grad, w)
+
+
+def summed_everywhere(arrays, post, grad, w, hshape, own_rows):
     flat = jnp.concatenate([a.reshape(-1) for a in arrays])
     unit = 128 * 8 << HALVINGS
     rows = -(-flat.size // unit) * unit // 128
     padded = jnp.pad(flat, (0, rows * 128 - flat.size)).reshape(rows, 128)
-    total, hout = allreduce(padded, hsrc)
+    total, _, own, hout = allreduce(padded, post, grad, w, hshape, own_rows)
     total = total.reshape(-1)
     out, at = [], 0
     for a in arrays:
         out.append(total[at:at + a.size].reshape(a.shape))
         at += a.size
-    return out, hout
+    return out, own, hout
 
 
 def _exists(index, size):
@@ -251,25 +254,37 @@
     out_ref[...] = total
 
 
-def conv_bwd_kernel(post_ref, tablet_ref, grad_ref, w_ref, tgrad_ref, wgrad_ref):
+def conv_wgrad_kernel(post_ref, tablet_ref, grad_ref, wgrad_ref):
     channels = tablet_ref.shape[0]
     table_t = tablet_ref[...]
     grad = grad_ref[...]
     rows = table_t.shape[1]
     sublanes = lax.broadcasted_iota(jnp.int32, (rows, post_ref.shape[1]), 0)
-    total = jnp.zeros((rows, 2 * channels), jnp.float32)
     for o in range(post_ref.shape[0]):
         hot_t = (sublanes == post_ref[o:o + 1, :]).astype(jnp.bfloat16)
         picked_t = jnp.dot(table_t, hot_t, preferred_element_type=jnp.float32).astype(jnp.bfloat16)
         wgrad_ref[o * channels:(o + 1) * channels, :] = jnp.dot(
             picked_t, grad, preferred_element_type=jnp.float32)
+
+
+def conv_scatter_body(post_ref, grad_ref, w_ref, halo_ref, own_ref):
+    channels = grad_ref.shape[1]
+    grad = grad_ref[...]
+    halo_rows = halo_ref.shape[0] * halo_ref.shape[1]
+    rows = halo_rows + own_ref.shape[0]
+    sublanes = lax.broadcasted_iota(jnp.int32, (rows, post_ref.shape[1]), 0)
+    total = jnp.zeros((rows, 2 * channels), jnp.float32)
+    for o in range(post_ref.shape[0]):
+        hot_t = (sublanes == post_ref[o:o + 1, :]).astype(jnp.bfloat16)
         weight = w_ref[o * channels:(o + 1) * channels, :]
         spread = lax.dot_general(grad, weight, (((1,), (1,)), ((), ())), preferred_element_type=jnp.float32)
         high = spread.astype(jnp.bfloat16)
         low = (spread - high.astype(jnp.float32)).astype(jnp.bfloat16)
         total = total + jnp.dot(hot_t, jnp.concatenate([high, low], axis=1),
                                 preferred_element_type=jnp.float32)
-    tgrad_ref[...] = total[:, :channels] + total[:, channels:]
+    summed = total[:, :channels] + total[:, channels:]
+    halo_ref[...] = summed[:halo_rows].reshape(halo_ref.shape)
+    own_ref[...] = summed[halo_rows:]
 
 
 def _vmem_call(kernel, outs, *args):
@@ -322,14 +337,11 @@
     conv_grad = (hidden_grad * sigmoid_y * (1.0 + conv_out * (1.0 - sigmoid_y))).astype(
         jnp.bfloat16
     )
-    table_grad, conv_wgrad = _vmem_call(
-        conv_bwd_kernel,
-        (jax.ShapeDtypeStruct((table_rows, channels), jnp.float32),
-         jax.ShapeDtypeStruct(w_conv.shape, jnp.float32)),
-        positions.T, table.T, conv_grad, w_conv)
-    halo_grad = table_grad[: 8 * rim].reshape(8, rim, channels)
-    (conv_wgrad, down_wgrad), returned = summed_everywhere([conv_wgrad, down_wgrad], halo_grad)
-    own_part = table_grad[8 * rim:]
+    conv_wgrad = _vmem_call(
+        conv_wgrad_kernel, jax.ShapeDtypeStruct(w_conv.shape, jnp.float32),
+        positions.T, table.T, conv_grad)
+    (conv_wgrad, down_wgrad), own_part, returned = summed_everywhere(
+        [conv_wgrad, down_wgrad], positions.T, conv_grad, w_conv, (8, rim, channels), voxels)
     incoming = jnp.sum(returned, axis=0)
     grad_input = hidden_grad + own_part
     grad_input = grad_input.at[:rim].add(incoming)

time: 142 us -> 143 us (level)
    pallas_call x1, Pallas kernels: 82.9 us -> 86.9 us  [allreduce(): pl.pallas_call(allreduce_kernel, out_shape=(jax.ShapeDtypeStruct((rows, 1...]
    pallas_call x1, Pallas kernels: 11.2 us -> 7.98 us  [_vmem_call(): pl.pallas_call(kernel, out_shape=outs, in_specs=[pl.BlockSpec(memory_spac...]
    unnamed x16 -> x14, local copies, waits for them, and re-layouts: 4.79 us -> 4.79 us
where the time goes in v12:
time: 143 us; the launch traced here: 142 us
  Pallas kernels  112 us (78%)
  local copies, waits for them, and re-layouts  15.6 us (11%)
  other arithmetic  11.1 us (8%)
  matrix products  1.94 us (1%)
    pallas_call x1, Pallas kernels, allreduce(): pl.pallas_call(allreduce_kernel, out_shape=(jax.ShapeDtypeStruct((rows, 1...  86.9 us
    pallas_call x1, Pallas kernels, on_device(): pl.pallas_call(conv_fwd_halo_kernel, out_shape=(jax.ShapeDtypeStruct((vox...  17.5 us
    pallas_call x1, Pallas kernels, _vmem_call(): pl.pallas_call(kernel, out_shape=outs, in_specs=[pl.BlockSpec(memory_spac...  7.98 us
    unnamed x14, local copies, waits for them, and re-layouts  4.79 us
    slice x2, local copies, waits for them, and re-layouts, summed_everywhere(): out.append(total[at:at + a.size].reshape(a.shape))  3.04 us

profile of v12, /device:TPU:1, one launch (start us, length us, event | category | flops | bytes accessed | tf_op | source)
XLA Modules:
  0.0 141.8 jit_solution(15367630994321110839)
XLA Ops:
  0.7 0.8 broadcast_minimum_fusion
  1.4 0.7 slice.33
  2.3 0.1 reshape.94
  2.4 1.4 fusion.17.post_ref
  3.9 0.1 reshape.103
  4.0 0.8 fusion.7
  4.8 1.5 %copy.19.own_ref = bf16[256,96]{1,0:T(8,128)(2,1)} copy(bf16[256,96]{0,1:T(8,128)(2,1)} %param.8) | data formatting | bytes 98304 | tf_op args[0]
  6.4 0.8 copy.21.pos_ref
  7.1 0.7 broadcast_in_dim.19.src_ref
  7.8 0.9 fusion.10
  8.7 0.1 reshape.113
  8.9 2.7 %scatter_custom_fusion = f32[257,96]{1,0:T(8,128)S(1)} fusion(s32[512]{0:T(512)S(1)} %bitcast.17, f32[512,96]{1,0:T(8,128)S(1)} %reshape.113, f32[]{:T(128)} %constant.72.clone.1), kind=kCustom, calls=%fused_computation.13 | custom fusion | flops 49152 | bytes 98692 | tf_op jit(solution)/shard_map/scatter-add | solution.py:330
  11.6 1.1 copy.23.w_ref
  12.7 17.5 %shard_map.93 = (f32[256,96]{1,0:T(8,128)}, bf16[8,64,96]{2,1,0:T(8,128)(2,1)}) custom-call(s32[256,27]{1,0:T(8,128)} %copy.21.pos_ref, bf16[256,96]{1,0:T(8,128)(2,1)} %copy.19.own_ref, bf16[8,64,96]{2,1,0:T(8,128)(2,1)} %broadcast_in_dim.19.src_ref, bf16[2592,96]{1,0:T(8,128)(2,1)} %copy.23.w_ref), custom_call_target="tpu_custom_call" | custom-call | tf_op jit(solution)/shard_map/pallas_call | solution.py:310
  30.2 1.6 %multiply_convert_fusion = (bf16[256,96]{1,0:T(8,128)(2,1)}, bf16[256,96]{1,0:T(8,128)(2,1)S(1)}) fusion(f32[256,96]{1,0:T(8,128)} %get-tuple-element.21, f32[257,96]{1,0:T(8,128)S(1)} %scatter_custom_fusion, bf16[256,96]{1,0:T(8,128)(2,1)S(1)} %copy-done.1), kind=kLoop, calls=%fused_computation.8 | loop fusion | flops 319488 | bytes 344064 | tf_op jit(solution)/shard_map/convert_element_type | solution.py:337
  31.8 1.0 copy.26
  32.8 0.7 maximum_bitcast_fusion.tablet_ref
  33.5 1.3 gather_fusion
  34.8 0.1 reshape.93
  35.0 0.8 convolution_convert_fusion
  35.8 0.2 convolution_bitcast_fusion
  36.0 8.0 %shard_map.94 = f32[2592,96]{1,0:T(8,128)} custom-call(s32[27,256]{1,0:T(8,128)} %fusion.17.post_ref, bf16[96,768]{1,0:T(8,128)(2,1)} %maximum_bitcast_fusion.tablet_ref, bf16[256,96]{1,0:T(8,128)(2,1)} %get-tuple-element.34.grad_ref), custom_call_target="tpu_custom_call" | custom-call | tf_op jit(solution)/shard_map/pallas_call | solution.py:291
  44.0 2.2 %reshape.97 = f32[248832]{0:T(1024)S(1)} reshape(f32[2592,96]{1,0:T(8,128)} %shard_map.94) | data formatting | bytes 1990656 | tf_op jit(solution)/shard_map/reshape | solution.py:119
  46.2 1.3 fusion.x_ref
  47.5 86.9 %shard_map.95 = (f32[3072,128]{1,0:T(8,128)}, f32[8,64,96]{2,1,0:T(8,128)}, f32[256,96]{1,0:T(8,128)}, f32[8,64,96]{2,1,0:T(8,128)}) custom-call(f32[3072,128]{1,0:T(8,128)} %fusion.x_ref, s32[27,256]{1,0:T(8,128)} %fusion.17.post_ref, bf16[256,96]{1,0:T(8,128)(2,1)} %get-tuple-element.34.grad_ref, bf16[2592,96]{1,0:T(8,128)(2,1)} %copy.23.w_ref), custom_call_target="tpu_custom_call" | custom-call | tf_op jit(solution)/shard_map/pallas_call | solution.py:101
  134.4 0.9 slice_add_fusion
  135.3 1.0 reduce_sum.9
  136.3 0.7 copy.28
  137.0 1.8 %slice.37 = f32[768,128]{1,0:T(8,128)} slice(f32[3072,128]{1,0:T(8,128)} %get-tuple-element.25), slice={[1944:2712], [0:128]} | slice | bytes 786432 | tf_op jit(solution)/shard_map/slice | solution.py:127
  138.8 1.3 slice.36
  140.1 0.3 reshape.100
  140.4 1.4 copy.29
  (17 shorter events, 0.3 us)
Async XLA Ops:
  0.6 7.2 %copy-start = (bf16[768,128]{1,0:T(8,128)(2,1)S(1)}, bf16[768,128]{1,0:T(8,128)(2,1)}, u32[]{:S(2)}) copy-start(bf16[768,128]{1,0:T(8,128)(2,1)} %param.12) | copy-start | bytes 589828
  0.6 10.9 %copy-start.2 = (bf16[2592,96]{0,1:T(8,128)(2,1)S(1)}, bf16[2592,96]{0,1:T(8,128)(2,1)}, u32[]{:S(2)}) copy-start(bf16[2592,96]{0,1:T(8,128)(2,1)} %param.11) | copy-start | bytes 1492996
  7.8 22.4 %copy-start.1 = (bf16[256,96]{1,0:T(8,128)(2,1)S(1)}, bf16[256,96]{1,0:T(8,128)(2,1)}, u32[]{:S(2)}) copy-start(bf16[256,96]{1,0:T(8,128)(2,1)} %copy.19.own_ref) | copy-start | bytes 147460
  8.9 23.9 %copy-start.3 = (bf16[256,96]{0,1:T(8,128)(2,1)S(1)}, bf16[256,96]{0,1:T(8,128)(2,1)}, u32[]{:S(2)}) copy-start(bf16[256,96]{0,1:T(8,128)(2,1)} %param.8) | copy-start | bytes 147460
  30.2 5.6 %copy-start.4 = (bf16[64,128]{1,0:T(8,128)(2,1)S(1)}, bf16[64,128]{1,0:T(8,128)(2,1)}, u32[]{:S(2)}) copy-start(bf16[64,128]{1,0:T(8,128)(2,1)} %param.13) | copy-start | bytes 49156

commit v13 on v12

--- a/solution.py
+++ b/solution.py
@@ -30,7 +30,7 @@
     return va + core * (vb - va), ra + core * (rb - ra), sa + core * (sb - sa)
 
 
-def allreduce_kernel(x_ref, post_ref, grad_ref, w_ref, o_ref, hsrc_ref, own_ref, hout_ref, *scratch):
+def allreduce_kernel(x_ref, post_ref, grad_ref, w_ref, hgrad_ref, o_ref, hsrc_ref, own_ref, hout_ref, *scratch):
     HALVES = [x_ref.shape[0] >> (k + 1) for k in range(HALVINGS)]
     recvs = scratch[:9]
     send_sem, recv_sem, free_sem = scratch[9], scratch[10], scratch[11]
@@ -92,9 +92,12 @@
         copy.start()
         copy.wait()
     _halo_finish(codes, present, hcopies)
-
-
-def allreduce(x, post, grad, w, hshape, own_rows):
+    rim = hout_ref.shape[1]
+    own_ref[...] = hgrad_ref[...] + own_ref[...]
+    own_ref[:rim] = own_ref[:rim] + jnp.sum(hout_ref[...], axis=0)
+
+
+def allreduce(x, post, grad, w, hgrad, hshape, own_rows):
     rows = x.shape[0]
     HALVES = [rows >> (k + 1) for k in range(HALVINGS)]
     n_copies = 9 + 7
@@ -104,7 +107,7 @@
                    jax.ShapeDtypeStruct(hshape, jnp.float32),
                    jax.ShapeDtypeStruct((own_rows, hshape[2]), jnp.float32),
                    jax.ShapeDtypeStruct(hshape, jnp.float32)),
-        in_specs=[pl.BlockSpec(memory_space=pltpu.VMEM)] * 4,
+        in_specs=[pl.BlockSpec(memory_space=pltpu.VMEM)] * 5,
         out_specs=tuple(pl.BlockSpec(memory_space=pltpu.VMEM) for _ in range(4)),
         scratch_shapes=[pltpu.VMEM((h, 128), jnp.float32) for h in HALVES]
         + [pltpu.VMEM((HALVES[-1], 128), jnp.float32)] * 2
@@ -112,15 +115,15 @@
         + [pltpu.SemaphoreType.REGULAR((HALVINGS,))]
         + [pltpu.SemaphoreType.DMA((8,)), pltpu.SemaphoreType.DMA((8,))],
         compiler_params=pltpu.CompilerParams(collective_id=0, has_side_effects=True),
-    )(x, post, grad, w)
-
-
-def summed_everywhere(arrays, post, grad, w, hshape, own_rows):
+    )(x, post, grad, w, hgrad)
+
+
+def summed_everywhere(arrays, post, grad, w, hgrad, hshape, own_rows):
     flat = jnp.concatenate([a.reshape(-1) for a in arrays])
     unit = 128 * 8 << HALVINGS
     rows = -(-flat.size // unit) * unit // 128
     padded = jnp.pad(flat, (0, rows * 128 - flat.size)).reshape(rows, 128)
-    total, _, own, hout = allreduce(padded, post, grad, w, hshape, own_rows)
+    total, _, own, hout = allreduce(padded, post, grad, w, hgrad, hshape, own_rows)
     total = total.reshape(-1)
     out, at = [], 0
     for a in arrays:
@@ -340,11 +343,8 @@
     conv_wgrad = _vmem_call(
         conv_wgrad_kernel, jax.ShapeDtypeStruct(w_conv.shape, jnp.float32),
         positions.T, table.T, conv_grad)
-    (conv_wgrad, down_wgrad), own_part, returned = summed_everywhere(
-        [conv_wgrad, down_wgrad], positions.T, conv_grad, w_conv, (8, rim, channels), voxels)
-    incoming = jnp.sum(returned, axis=0)
-    grad_input = hidden_grad + own_part
-    grad_input = grad_input.at[:rim].add(incoming)
+    (conv_wgrad, down_wgrad), grad_input, _ = summed_everywhere(
+        [conv_wgrad, down_wgrad], positions.T, conv_grad, w_conv, hidden_grad, (8, rim, channels), voxels)
     return (coarse, grad_input, conv_wgrad, down_wgrad)
 
 

time: 143 us -> 141 us (0.986)
  Pallas kernels: 112 us -> 110 us
    pallas_call x1, Pallas kernels: 86.9 us -> 84.9 us  [allreduce(): pl.pallas_call(allreduce_kernel, out_shape=(jax.ShapeDtypeStruct((rows, 1...]
    slice x0 -> x1, other arithmetic: none -> 1.62 us  [on_device(): hidden_grad.at[down_local.reshape(-1)]]
    convert_element_type x1 -> x0, other arithmetic: 1.61 us -> none  [on_device(): (hidden_grad * sigmoid_y * (1.0 + conv_out * (1.0 - sigmoid_y))).astype(j...]
where the time goes in v13:
time: 141 us; the launch traced here: 140 us
  Pallas kernels  110 us (78%)
  local copies, waits for them, and re-layouts  16.5 us (12%)
  other arithmetic  10.2 us (7%)
  matrix products  1.94 us (1%)
    pallas_call x1, Pallas kernels, allreduce(): pl.pallas_call(allreduce_kernel, out_shape=(jax.ShapeDtypeStruct((rows, 1...  84.9 us
    pallas_call x1, Pallas kernels, on_device(): pl.pallas_call(conv_fwd_halo_kernel, out_shape=(jax.ShapeDtypeStruct((vox...  17.3 us
    pallas_call x1, Pallas kernels, _vmem_call(): pl.pallas_call(kernel, out_shape=outs, in_specs=[pl.BlockSpec(memory_spac...  7.99 us
    unnamed x14, local copies, waits for them, and re-layouts  5.69 us
    scatter-add x1, other arithmetic, on_device(): hidden_grad.at[down_local.reshape(-1)]  3.65 us
    slice x2, local copies, waits for them, and re-layouts, summed_everywhere(): out.append(total[at:at + a.size].reshape(a.shape))  3.04 us

profile of v13, /device:TPU:1, one launch (start us, length us, event | category | flops | bytes accessed | tf_op | source)
XLA Modules:
  0.0 139.6 jit_solution(17747009790875840889)
XLA Ops:
  0.7 0.8 broadcast_minimum_fusion
  1.4 0.7 slice.14
  2.2 0.1 copy.20
  2.2 0.1 copy.26
  2.3 0.1 reshape.69
  2.4 1.4 %fusion.17.post_ref = s32[27,256]{1,0:T(8,128)} fusion(s32[256,27]{0,1:T(8,128)} %param.7), kind=kLoop, calls=%fused_computation.31 | loop fusion | flops 186624 | bytes 55296 | tf_op jit(solution)/shard_map/transpose | solution.py:345
  3.9 0.1 reshape.77
  4.0 0.8 fusion.7
  4.8 1.5 %copy.19.own_ref = bf16[256,96]{1,0:T(8,128)(2,1)} copy(bf16[256,96]{0,1:T(8,128)(2,1)} %param.6) | data formatting | bytes 98304 | tf_op args[0]
  6.4 0.8 copy.21.pos_ref
  7.1 0.7 broadcast_in_dim.19.src_ref
  7.8 0.9 fusion.10
  8.8 0.1 reshape.87
  8.9 3.7 %scatter_custom_fusion = f32[257,96]{1,0:T(8,128)S(1)} fusion(s32[512]{0:T(512)S(1)} %bitcast.17, f32[512,96]{1,0:T(8,128)S(1)} %reshape.87, f32[]{:T(128)} %constant.44.clone.1), kind=kCustom, calls=%fused_computation.12 | custom fusion | flops 49152 | bytes 98692 | tf_op jit(solution)/shard_map/scatter-add | solution.py:333
  12.6 1.1 copy.23.w_ref
  13.7 17.3 %shard_map.93 = (f32[256,96]{1,0:T(8,128)}, bf16[8,64,96]{2,1,0:T(8,128)(2,1)}) custom-call(s32[256,27]{1,0:T(8,128)} %copy.21.pos_ref, bf16[256,96]{1,0:T(8,128)(2,1)} %copy.19.own_ref, bf16[8,64,96]{2,1,0:T(8,128)(2,1)} %broadcast_in_dim.19.src_ref, bf16[2592,96]{1,0:T(8,128)(2,1)} %copy.23.w_ref), custom_call_target="tpu_custom_call" | custom-call | tf_op jit(solution)/shard_map/pallas_call | solution.py:313
  31.0 1.6 %fusion.9 = (f32[256,96]{1,0:T(8,128)}, bf16[256,96]{1,0:T(8,128)(2,1)}, bf16[256,96]{1,0:T(8,128)(2,1)S(1)}) fusion(f32[257,96]{1,0:T(8,128)S(1)} %scatter_custom_fusion, f32[256,96]{1,0:T(8,128)} %get-tuple-element.8, bf16[256,96]{1,0:T(8,128)(2,1)S(1)} %copy-done.1), kind=kLoop, calls=%fused_computation.29 | loop fusion | flops 319488 | bytes 442368 | tf_op jit(solution)/shard_map/slice | solution.py:333
  32.6 1.0 copy.25
  33.6 0.7 maximum_bitcast_fusion.tablet_ref
  34.3 1.3 gather_fusion
  35.7 0.1 reshape.67
  35.8 0.8 convolution_convert_fusion
  36.6 0.2 convolution_bitcast_fusion
  36.8 8.0 %shard_map.94 = f32[2592,96]{1,0:T(8,128)} custom-call(s32[27,256]{1,0:T(8,128)} %fusion.17.post_ref, bf16[96,768]{1,0:T(8,128)(2,1)} %maximum_bitcast_fusion.tablet_ref, bf16[256,96]{1,0:T(8,128)(2,1)} %get-tuple-element.21.grad_ref), custom_call_target="tpu_custom_call" | custom-call | tf_op jit(solution)/shard_map/pallas_call | solution.py:294
  44.8 2.2 %reshape.71 = f32[248832]{0:T(1024)S(1)} reshape(f32[2592,96]{1,0:T(8,128)} %shard_map.94) | data formatting | bytes 1990656 | tf_op jit(solution)/shard_map/reshape | solution.py:122
  47.0 1.3 fusion.x_ref
  48.3 84.9 %shard_map.95 = (f32[3072,128]{1,0:T(8,128)}, f32[8,64,96]{2,1,0:T(8,128)}, f32[256,96]{1,0:T(8,128)}, f32[8,64,96]{2,1,0:T(8,128)}) custom-call(f32[3072,128]{1,0:T(8,128)} %fusion.x_ref, s32[27,256]{1,0:T(8,128)} %fusion.17.post_ref, bf16[256,96]{1,0:T(8,128)(2,1)} %get-tuple-element.21.grad_ref, bf16[2592,96]{1,0:T(8,128)(2,1)} %copy.23.w_ref, ...), custom_call_target="tpu_custom_call" | custom-call | tf_op jit(solution)/shard_map/pallas_call | solution.py:104
  133.2 1.6 %copy.28 = f32[256,96]{0,1:T(8,128)} copy(f32[256,96]{1,0:T(8,128)} %get-tuple-element.17) | data formatting | bytes 196608
  134.9 1.8 %slice.17 = f32[768,128]{1,0:T(8,128)} slice(f32[3072,128]{1,0:T(8,128)} %get-tuple-element.11), slice={[1944:2712], [0:128]} | slice | bytes 786432 | tf_op jit(solution)/shard_map/slice | solution.py:130
  136.6 1.3 slice.16
  137.9 0.3 reshape.74
  138.2 1.4 copy.29
  (14 shorter events, 0.1 us)
Async XLA Ops:
  0.6 7.2 %copy-start = (bf16[768,128]{1,0:T(8,128)(2,1)S(1)}, bf16[768,128]{1,0:T(8,128)(2,1)}, u32[]{:S(2)}) copy-start(bf16[768,128]{1,0:T(8,128)(2,1)} %param.10) | copy-start | bytes 589828
  0.6 11.9 %copy-start.2 = (bf16[2592,96]{0,1:T(8,128)(2,1)S(1)}, bf16[2592,96]{0,1:T(8,128)(2,1)}, u32[]{:S(2)}) copy-start(bf16[2592,96]{0,1:T(8,128)(2,1)} %param.9) | copy-start | bytes 1492996
  7.8 23.2 %copy-start.1 = (bf16[256,96]{1,0:T(8,128)(2,1)S(1)}, bf16[256,96]{1,0:T(8,128)(2,1)}, u32[]{:S(2)}) copy-start(bf16[256,96]{1,0:T(8,128)(2,1)} %copy.19.own_ref) | copy-start | bytes 147460
  8.9 24.7 %copy-start.3 = (bf16[256,96]{0,1:T(8,128)(2,1)S(1)}, bf16[256,96]{0,1:T(8,128)(2,1)}, u32[]{:S(2)}) copy-start(bf16[256,96]{0,1:T(8,128)(2,1)} %param.6) | copy-start | bytes 147460
  31.0 5.6 %copy-start.4 = (bf16[64,128]{1,0:T(8,128)(2,1)S(1)}, bf16[64,128]{1,0:T(8,128)(2,1)}, u32[]{:S(2)}) copy-start(bf16[64,128]{1,0:T(8,128)(2,1)} %param.11) | copy-start | bytes 49156

commit v14 on v13

--- a/solution.py
+++ b/solution.py
@@ -119,18 +119,17 @@
 
 
 def summed_everywhere(arrays, post, grad, w, hgrad, hshape, own_rows):
-    flat = jnp.concatenate([a.reshape(-1) for a in arrays])
-    unit = 128 * 8 << HALVINGS
-    rows = -(-flat.size // unit) * unit // 128
-    padded = jnp.pad(flat, (0, rows * 128 - flat.size)).reshape(rows, 128)
+    parts = [a.reshape(-1, 128) for a in arrays]
+    unit = 8 << HALVINGS
+    used = sum(p.shape[0] for p in parts)
+    rows = -(-used // unit) * unit
+    padded = jnp.concatenate(parts + [jnp.zeros((rows - used, 128), jnp.float32)], axis=0)
     total, _, own, hout = allreduce(padded, post, grad, w, hgrad, hshape, own_rows)
-    total = total.reshape(-1)
     out, at = [], 0
-    for a in arrays:
-        out.append(total[at:at + a.size].reshape(a.shape))
-        at += a.size
+    for a, p in zip(arrays, parts):
+        out.append(total[at:at + p.shape[0]].reshape(a.shape))
+        at += p.shape[0]
     return out, own, hout
-
 
 def _exists(index, size):
     low = (index + size - 1) // size

time: 141 us -> 141 us (level)
    concatenate x0 -> x1, other arithmetic: none -> 1.63 us  [summed_everywhere(): jnp.concatenate(parts + [jnp.zeros((rows - used, 128), jnp.float32)], axi...]
    pallas_call x1, Pallas kernels: 84.9 us -> 86.4 us  [allreduce(): pl.pallas_call(allreduce_kernel, out_shape=(jax.ShapeDtypeStruct((rows, 1...]
where the time goes in v14:
time: 141 us
  Pallas kernels  111 us (79%)
  local copies, waits for them, and re-layouts  16.6 us (12%)
  other arithmetic  10.6 us (8%)
  matrix products  1.94 us (1%)
    pallas_call x1, Pallas kernels, allreduce(): pl.pallas_call(allreduce_kernel, out_shape=(jax.ShapeDtypeStruct((rows, 1...  86.4 us
    pallas_call x1, Pallas kernels, on_device(): pl.pallas_call(conv_fwd_halo_kernel, out_shape=(jax.ShapeDtypeStruct((vox...  16.5 us
    pallas_call x1, Pallas kernels, _vmem_call(): pl.pallas_call(kernel, out_shape=outs, in_specs=[pl.BlockSpec(memory_spac...  7.99 us
    unnamed x14, local copies, waits for them, and re-layouts  5.7 us
    scatter-add x1, other arithmetic, on_device(): hidden_grad.at[down_local.reshape(-1)]  3.68 us
    slice x2, local copies, waits for them, and re-layouts, summed_everywhere(): out.append(total[at:at + p.shape[0]].reshape(a.shape))  3.04 us

profile of v14, /device:TPU:1, one launch (start us, length us, event | category | flops | bytes accessed | tf_op | source)
XLA Modules:
  0.0 140.8 jit_solution(5591450399362782810)
XLA Ops:
  0.7 0.8 broadcast_minimum_fusion
  1.5 0.7 slice.12
  2.2 0.1 copy.20
  2.3 0.1 copy.26
  2.4 0.1 reshape.57
  2.5 1.4 fusion.17.post_ref
  4.0 0.1 reshape.63
  4.1 0.8 fusion.6
  4.9 1.5 %copy.19.own_ref = bf16[256,96]{1,0:T(8,128)(2,1)} copy(bf16[256,96]{0,1:T(8,128)(2,1)} %param.6) | data formatting | bytes 98304 | tf_op args[0]
  6.5 0.8 copy.21.pos_ref
  7.2 0.7 broadcast_in_dim.22.src_ref
  7.9 0.9 fusion.9
  8.8 0.1 reshape.73
  9.0 3.7 %scatter_custom_fusion = f32[257,96]{1,0:T(8,128)S(1)} fusion(s32[512]{0:T(512)S(1)} %bitcast.13, f32[512,96]{1,0:T(8,128)S(1)} %reshape.73, f32[]{:T(128)} %constant.43.clone.1), kind=kCustom, calls=%fused_computation.9 | custom fusion | flops 49152 | bytes 98692 | tf_op jit(solution)/shard_map/scatter-add | solution.py:332
  12.7 1.1 copy.23.w_ref
  13.8 16.5 %shard_map.93 = (f32[256,96]{1,0:T(8,128)}, bf16[8,64,96]{2,1,0:T(8,128)(2,1)}) custom-call(s32[256,27]{1,0:T(8,128)} %copy.21.pos_ref, bf16[256,96]{1,0:T(8,128)(2,1)} %copy.19.own_ref, bf16[8,64,96]{2,1,0:T(8,128)(2,1)} %broadcast_in_dim.22.src_ref, bf16[2592,96]{1,0:T(8,128)(2,1)} %copy.23.w_ref), custom_call_target="tpu_custom_call" | custom-call | tf_op jit(solution)/shard_map/pallas_call | solution.py:312
  30.3 1.6 %fusion.8 = (f32[256,96]{1,0:T(8,128)}, bf16[256,96]{1,0:T(8,128)(2,1)}, bf16[256,96]{1,0:T(8,128)(2,1)S(1)}) fusion(f32[257,96]{1,0:T(8,128)S(1)} %scatter_custom_fusion, f32[256,96]{1,0:T(8,128)} %get-tuple-element.8, bf16[256,96]{1,0:T(8,128)(2,1)S(1)} %copy-done.1), kind=kLoop, calls=%fused_computation.26 | loop fusion | flops 319488 | bytes 442368 | tf_op jit(solution)/shard_map/slice | solution.py:332
  32.0 1.0 copy.25
  33.0 0.7 maximum_bitcast_fusion.tablet_ref
  33.7 1.3 gather_fusion
  35.0 0.1 reshape.55
  35.1 0.8 convolution_convert_fusion
  35.9 0.2 fusion.10
  36.2 8.0 %shard_map.94 = f32[2592,96]{1,0:T(8,128)} custom-call(s32[27,256]{1,0:T(8,128)} %fusion.17.post_ref, bf16[96,768]{1,0:T(8,128)(2,1)} %maximum_bitcast_fusion.tablet_ref, bf16[256,96]{1,0:T(8,128)(2,1)} %get-tuple-element.21.grad_ref), custom_call_target="tpu_custom_call" | custom-call | tf_op jit(solution)/shard_map/pallas_call | solution.py:293
  44.2 2.2 %reshape.59 = f32[1944,128]{1,0:T(8,128)S(1)} reshape(f32[2592,96]{1,0:T(8,128)} %shard_map.94) | data formatting | bytes 1990656 | tf_op jit(solution)/shard_map/reshape | solution.py:122
  46.4 1.6 %maximum_maximum_fusion.x_ref = f32[3072,128]{1,0:T(8,128)} fusion(f32[768,128]{1,0:T(8,128)S(1)} %fusion.10, f32[1944,128]{1,0:T(8,128)S(1)} %reshape.59, f32[3072]{0:T(1024)S(1)} %pad.3.clone), kind=kLoop, calls=%fused_computation.2 | loop fusion | flops 786432 | bytes 2973696 | tf_op jit(solution)/shard_map/concatenate | solution.py:126
  48.0 86.4 %shard_map.95 = (f32[3072,128]{1,0:T(8,128)}, f32[8,64,96]{2,1,0:T(8,128)}, f32[256,96]{1,0:T(8,128)}, f32[8,64,96]{2,1,0:T(8,128)}) custom-call(f32[3072,128]{1,0:T(8,128)} %maximum_maximum_fusion.x_ref, s32[27,256]{1,0:T(8,128)} %fusion.17.post_ref, bf16[256,96]{1,0:T(8,128)(2,1)} %get-tuple-element.21.grad_ref, bf16[2592,96]{1,0:T(8,128)(2,1)} %copy.23.w_ref, ...), custom_call_target="tpu_custom_call" | custom-call | tf_op jit(solution)/shard_map/pallas_call | solution.py:104
  134.4 1.6 %copy.28 = f32[256,96]{0,1:T(8,128)} copy(f32[256,96]{1,0:T(8,128)} %get-tuple-element.17) | data formatting | bytes 196608
  136.0 1.8 %slice.15 = f32[768,128]{1,0:T(8,128)} slice(f32[3072,128]{1,0:T(8,128)} %get-tuple-element.11), slice={[1944:2712], [0:128]} | slice | bytes 786432 | tf_op jit(solution)/shard_map/slice | solution.py:130
  137.8 1.3 slice.14
  139.1 0.3 reshape.60
  139.4 1.4 copy.29
  (16 shorter events, 0.2 us)
Async XLA Ops:
  0.6 7.3 %copy-start = (bf16[768,128]{1,0:T(8,128)(2,1)S(1)}, bf16[768,128]{1,0:T(8,128)(2,1)}, u32[]{:S(2)}) copy-start(bf16[768,128]{1,0:T(8,128)(2,1)} %param.10) | copy-start | bytes 589828
  0.6 12.0 %copy-start.2 = (bf16[2592,96]{0,1:T(8,128)(2,1)S(1)}, bf16[2592,96]{0,1:T(8,128)(2,1)}, u32[]{:S(2)}) copy-start(bf16[2592,96]{0,1:T(8,128)(2,1)} %param.9) | copy-start | bytes 1492996
  7.9 22.4 %copy-start.1 = (bf16[256,96]{1,0:T(8,128)(2,1)S(1)}, bf16[256,96]{1,0:T(8,128)(2,1)}, u32[]{:S(2)}) copy-start(bf16[256,96]{1,0:T(8,128)(2,1)} %copy.19.own_ref) | copy-start | bytes 147460
  9.0 24.0 %copy-start.3 = (bf16[256,96]{0,1:T(8,128)(2,1)S(1)}, bf16[256,96]{0,1:T(8,128)(2,1)}, u32[]{:S(2)}) copy-start(bf16[256,96]{0,1:T(8,128)(2,1)} %param.6) | copy-start | bytes 147460
  30.3 5.6 %copy-start.4 = (bf16[64,128]{1,0:T(8,128)(2,1)S(1)}, bf16[64,128]{1,0:T(8,128)(2,1)}, u32[]{:S(2)}) copy-start(bf16[64,128]{1,0:T(8,128)(2,1)} %param.11) | copy-start | bytes 49156

commit v15 on v13

--- a/solution.py
+++ b/solution.py
@@ -50,7 +50,6 @@
     _halo_signal(barrier, codes, present, targets)
     conv_scatter_body(post_ref, grad_ref, w_ref, hsrc_ref, own_ref)
     pl.semaphore_wait(barrier, len(steps) + len(fulls) + hcount)
-    _halo_start(codes, present, hcopies)
 
     off = 0
     offs = []
@@ -69,6 +68,7 @@
         o_ref[pl.ds(keep, size)] = src[pl.ds(keep, size)] + recvs[k][...]
         off = keep
         offs.append(keep)
+    _halo_start(codes, present, hcopies)
     last = HALVES[-1]
     for i, (v, r, s) in enumerate(fulls):
         k = len(steps) + i

time: 141 us -> 142 us (level)
  Pallas kernels: 110 us -> 113 us
    pallas_call x1, Pallas kernels: 84.9 us -> 87.2 us  [allreduce(): pl.pallas_call(allreduce_kernel, out_shape=(jax.ShapeDtypeStruct((rows, 1...]
where the time goes in v15:
time: 142 us
  Pallas kernels  113 us (80%)
  local copies, waits for them, and re-layouts  16.5 us (12%)
  other arithmetic  9.05 us (6%)
  matrix products  1.94 us (1%)
    pallas_call x1, Pallas kernels, allreduce(): pl.pallas_call(allreduce_kernel, out_shape=(jax.ShapeDtypeStruct((rows, 1...  87.2 us
    pallas_call x1, Pallas kernels, on_device(): pl.pallas_call(conv_fwd_halo_kernel, out_shape=(jax.ShapeDtypeStruct((vox...  18.3 us
    pallas_call x1, Pallas kernels, _vmem_call(): pl.pallas_call(kernel, out_shape=outs, in_specs=[pl.BlockSpec(memory_spac...  7.99 us
    unnamed x14, local copies, waits for them, and re-layouts  5.69 us
    slice x2, local copies, waits for them, and re-layouts, summed_everywhere(): out.append(total[at:at + a.size].reshape(a.shape))  3.04 us

profile of v15, /device:TPU:1, one launch (start us, length us, event | category | flops | bytes accessed | tf_op | source)
XLA Modules:
  0.0 141.7 jit_solution(18338482442670626921)
XLA Ops:
  0.7 0.8 broadcast_minimum_fusion
  1.4 0.7 slice.14
  2.2 0.1 copy.20
  2.2 0.1 copy.26
  2.3 0.1 reshape.69
  2.4 1.4 fusion.17.post_ref
  3.9 0.1 reshape.77
  4.0 0.8 fusion.7
  4.8 1.5 %copy.19.own_ref = bf16[256,96]{1,0:T(8,128)(2,1)} copy(bf16[256,96]{0,1:T(8,128)(2,1)} %param.6) | data formatting | bytes 98304 | tf_op args[0]
  6.4 0.8 copy.21.pos_ref
  7.1 0.7 broadcast_in_dim.19.src_ref
  7.8 0.9 fusion.10
  8.8 0.1 reshape.87
  8.9 2.5 %scatter_custom_fusion = f32[257,96]{1,0:T(8,128)S(1)} fusion(s32[512]{0:T(512)S(1)} %bitcast.17, f32[512,96]{1,0:T(8,128)S(1)} %reshape.87, f32[]{:T(128)} %constant.44.clone.1), kind=kCustom, calls=%fused_computation.12 | custom fusion | flops 49152 | bytes 98692 | tf_op jit(solution)/shard_map/scatter-add | solution.py:333
  11.5 1.1 copy.23.w_ref
  12.6 18.3 %shard_map.93 = (f32[256,96]{1,0:T(8,128)}, bf16[8,64,96]{2,1,0:T(8,128)(2,1)}) custom-call(s32[256,27]{1,0:T(8,128)} %copy.21.pos_ref, bf16[256,96]{1,0:T(8,128)(2,1)} %copy.19.own_ref, bf16[8,64,96]{2,1,0:T(8,128)(2,1)} %broadcast_in_dim.19.src_ref, bf16[2592,96]{1,0:T(8,128)(2,1)} %copy.23.w_ref), custom_call_target="tpu_custom_call" | custom-call | tf_op jit(solution)/shard_map/pallas_call | solution.py:313
  30.8 1.6 %fusion.9 = (f32[256,96]{1,0:T(8,128)}, bf16[256,96]{1,0:T(8,128)(2,1)}, bf16[256,96]{1,0:T(8,128)(2,1)S(1)}) fusion(f32[257,96]{1,0:T(8,128)S(1)} %scatter_custom_fusion, f32[256,96]{1,0:T(8,128)} %get-tuple-element.8, bf16[256,96]{1,0:T(8,128)(2,1)S(1)} %copy-done.1), kind=kLoop, calls=%fused_computation.29 | loop fusion | flops 319488 | bytes 442368 | tf_op jit(solution)/shard_map/slice | solution.py:333
  32.5 1.0 copy.25
  33.5 0.7 maximum_bitcast_fusion.tablet_ref
  34.2 1.3 gather_fusion
  35.5 0.1 reshape.67
  35.7 0.8 convolution_convert_fusion
  36.4 0.2 convolution_bitcast_fusion
  36.7 8.0 %shard_map.94 = f32[2592,96]{1,0:T(8,128)} custom-call(s32[27,256]{1,0:T(8,128)} %fusion.17.post_ref, bf16[96,768]{1,0:T(8,128)(2,1)} %maximum_bitcast_fusion.tablet_ref, bf16[256,96]{1,0:T(8,128)(2,1)} %get-tuple-element.21.grad_ref), custom_call_target="tpu_custom_call" | custom-call | tf_op jit(solution)/shard_map/pallas_call | solution.py:294
  44.7 2.2 %reshape.71 = f32[248832]{0:T(1024)S(1)} reshape(f32[2592,96]{1,0:T(8,128)} %shard_map.94) | data formatting | bytes 1990656 | tf_op jit(solution)/shard_map/reshape | solution.py:122
  46.9 1.3 fusion.x_ref
  48.1 87.2 %shard_map.95 = (f32[3072,128]{1,0:T(8,128)}, f32[8,64,96]{2,1,0:T(8,128)}, f32[256,96]{1,0:T(8,128)}, f32[8,64,96]{2,1,0:T(8,128)}) custom-call(f32[3072,128]{1,0:T(8,128)} %fusion.x_ref, s32[27,256]{1,0:T(8,128)} %fusion.17.post_ref, bf16[256,96]{1,0:T(8,128)(2,1)} %get-tuple-element.21.grad_ref, bf16[2592,96]{1,0:T(8,128)(2,1)} %copy.23.w_ref, ...), custom_call_target="tpu_custom_call" | custom-call | tf_op jit(solution)/shard_map/pallas_call | solution.py:104
  135.3 1.6 %copy.28 = f32[256,96]{0,1:T(8,128)} copy(f32[256,96]{1,0:T(8,128)} %get-tuple-element.17) | data formatting | bytes 196608
  137.0 1.8 %slice.17 = f32[768,128]{1,0:T(8,128)} slice(f32[3072,128]{1,0:T(8,128)} %get-tuple-element.11), slice={[1944:2712], [0:128]} | slice | bytes 786432 | tf_op jit(solution)/shard_map/slice | solution.py:130
  138.7 1.3 slice.16
  140.0 0.3 reshape.74
  140.3 1.4 copy.29
  (14 shorter events, 0.1 us)
Async XLA Ops:
  0.6 7.2 %copy-start = (bf16[768,128]{1,0:T(8,128)(2,1)S(1)}, bf16[768,128]{1,0:T(8,128)(2,1)}, u32[]{:S(2)}) copy-start(bf16[768,128]{1,0:T(8,128)(2,1)} %param.10) | copy-start | bytes 589828
  0.6 10.8 %copy-start.2 = (bf16[2592,96]{0,1:T(8,128)(2,1)S(1)}, bf16[2592,96]{0,1:T(8,128)(2,1)}, u32[]{:S(2)}) copy-start(bf16[2592,96]{0,1:T(8,128)(2,1)} %param.9) | copy-start | bytes 1492996
  7.8 23.0 %copy-start.1 = (bf16[256,96]{1,0:T(8,128)(2,1)S(1)}, bf16[256,96]{1,0:T(8,128)(2,1)}, u32[]{:S(2)}) copy-start(bf16[256,96]{1,0:T(8,128)(2,1)} %copy.19.own_ref) | copy-start | bytes 147460
  8.9 24.6 %copy-start.3 = (bf16[256,96]{0,1:T(8,128)(2,1)S(1)}, bf16[256,96]{0,1:T(8,128)(2,1)}, u32[]{:S(2)}) copy-start(bf16[256,96]{0,1:T(8,128)(2,1)} %param.6) | copy-start | bytes 147460
  30.8 5.6 %copy-start.4 = (bf16[64,128]{1,0:T(8,128)(2,1)S(1)}, bf16[64,128]{1,0:T(8,128)(2,1)}, u32[]{:S(2)}) copy-start(bf16[64,128]{1,0:T(8,128)(2,1)} %param.11) | copy-start | bytes 49156
